TPU v7x, 32 devices: a whole 2x2x4 slice. The times are simulated.
32 devices in a mesh: lvl: 4 (over x, core), gx: 2 (over y), gy: 4 (over z).
Axes of the slice: x: 2, y: 2, z: 4, core: 2. Of those that a mesh axis runs over, the one named last changes fastest.
Arguments:
- initial: float32 [16, 16, 32, 128], P(None, 'gx', 'gy'), may hold values from 0.07 to 1, as said below
- rate_factor: float32 [16, 32, 128], P('gx', 'gy'), may hold values from 0.5 to 2
- diffusivity: float32 [16], replicated, may hold values from 0.3 to 2
- loss_rate: float32 [16], replicated, may hold values from 0.05 to 1.5
- quench: float32 [16, 16], replicated, may hold values from 0 to 0.1
- formation: float32 [16, 16], replicated, may hold values from 0 to 0.1
Outputs:
- final: float32 [4, 16, 16, 32, 128], P('lvl', None, 'gx', 'gy')
Inputs may be any that keep to these rules, and one draw needn't show every extreme that they name: `initial`: positive concentrations.
All inputs are finite; a program needn't handle non-finite values.
Results may differ from a plain program's by a relative error of at most 0.0001.
Values sent between devices are 32-bit elements; how exact they have to be, the bound alone decides.
No kernel may reach another device: no remote copies, remote signals or barrier semaphores. Data moves between devices by JAX's collectives and lax.ppermute only.
A program may use at most 64 MiB of HBM per device.

v0:
```python
import jax
import jax.numpy as jnp
from jax import lax
from jax.sharding import PartitionSpec as P

REACT = 11
STEPS = 4
SWEEPS = 4


def padded_2(x, sides, width):
    for axis, dim in sides:
        size, length = (lax.axis_size(axis), x.shape[dim])
        up = [(i, (i + 1) % size) for i in range(size - 1)]
        down = [(j, i) for i, j in up]
        last = lax.slice_in_dim(x, length - width, length, axis=dim)
        leading = lax.slice_in_dim(x, 0, width, axis=dim)
        before = lax.ppermute(last, axis, up)
        after = lax.ppermute(leading, axis, down)
        x = jnp.concatenate([before, x, after], axis=dim)
    return x


def from_behind(value, axis, steps):
    count = lax.axis_size(axis)
    leading, last = (max(0, -steps), min(count, count - steps))
    return lax.ppermute(value, axis, [(source, source + steps) for source in range(leading, last)])


def trim_rim(values, amount):
    if amount == 0:
        return values
    return values[..., amount : values.shape[-3] - amount, amount : values.shape[-2] - amount, :]


def trim_all(coeffs, amount):
    return tuple((trim_rim(values, amount) for values in coeffs))


def conduct(fields, diffusivity):
    return diffusivity[:, None, None, None] * (1.0 + fields * fields)


def face_weights(padded, diffusivity):
    conductance = conduct(padded, diffusivity)
    centre = conductance[:, 1:-1, 1:-1]
    inner_cells = padded[:, 1:-1, 1:-1]
    vertical = conduct(jnp.pad(inner_cells, ((0, 0), (0, 0), (0, 0), (1, 1))), diffusivity)
    west_face = 0.5 * (centre + conductance[:, :-2, 1:-1])
    east_face = 0.5 * (centre + conductance[:, 2:, 1:-1])
    south_face = 0.5 * (centre + conductance[:, 1:-1, :-2])
    north_face = 0.5 * (centre + conductance[:, 1:-1, 2:])
    lower_face = 0.5 * (centre + vertical[..., :-2])
    upper_face = 0.5 * (centre + vertical[..., 2:])
    weight_sum = west_face + east_face + south_face + north_face + lower_face + upper_face
    return ((west_face, east_face, south_face, north_face, lower_face, upper_face), weight_sum)


def neighbours(padded, coeffs):
    west_face, east_face, south_face, north_face, lower_face, upper_face = coeffs
    inner_cells = padded[:, 1:-1, 1:-1]
    stacked = jnp.pad(inner_cells, ((0, 0), (0, 0), (0, 0), (1, 1)))
    return (
        west_face * padded[:, :-2, 1:-1]
        + east_face * padded[:, 2:, 1:-1]
        + south_face * padded[:, 1:-1, :-2]
        + north_face * padded[:, 1:-1, 2:]
        + lower_face * stacked[..., :-2]
        + upper_face * stacked[..., 2:]
    )


def chemistry(fields, rate_factor, loss_rate, quench, formation):
    reacting = (jnp.arange(fields.shape[0]) < REACT).astype(jnp.float32)[:, None, None, None]
    squares = jnp.einsum("ij,jxyz->ixyz", quench, fields * fields, precision=lax.Precision.HIGHEST)
    produced = jnp.einsum("ij,jxyz->ixyz", formation, fields, precision=lax.Precision.HIGHEST)
    loss_term = reacting * loss_rate[:, None, None, None] * rate_factor[None] * (1.0 + squares)
    production = reacting * rate_factor[None] * produced
    return (loss_term, production)


def inside_mask(rim_depth, tile_rows, tile_cols):
    along_first = lax.axis_index("gx") * tile_rows + jnp.arange(-rim_depth, tile_rows + rim_depth)
    along_second = lax.axis_index("gy") * tile_cols + jnp.arange(-rim_depth, tile_cols + rim_depth)
    first_inside = (along_first >= 0) & (along_first < tile_rows * lax.axis_size("gx"))
    second_inside = (along_second >= 0) & (along_second < tile_cols * lax.axis_size("gy"))
    return (first_inside[:, None] & second_inside[None, :]).astype(jnp.float32)[None, :, :, None]


def on_device(initial, rate_factor, diffusivity, loss_rate, quench, formation):
    level_index = lax.axis_index("lvl")
    tile_rows = initial.shape[1]
    tile_cols = initial.shape[2]
    rim_depth = SWEEPS - 1
    current_state = initial
    rate_wide = padded_2(rate_factor, (("gx", 0), ("gy", 1)), SWEEPS)
    rate_core = trim_rim(rate_wide, 1)
    inside = inside_mask(rim_depth, tile_rows, tile_cols)
    carried = jnp.zeros_like(initial)
    received_prev = jnp.zeros_like(initial)
    for tick_index in range(STEPS + lax.axis_size("lvl") - 1):
        node_index = tick_index - level_index
        advance = (node_index >= 0) & (node_index < STEPS)
        widened = padded_2(current_state, (("gx", 1), ("gy", 2)), SWEEPS)
        coeffs, weight_sum = face_weights(widened, diffusivity)
        core_cells = trim_rim(widened, 1)
        loss_term, production = chemistry(core_cells, rate_core, loss_rate, quench, formation)
        diffused = (
            neighbours(trim_rim(widened, rim_depth), trim_all(coeffs, rim_depth))
            - trim_rim(weight_sum, rim_depth) * current_state
        )
        tendency = (
            diffused
            + trim_rim(production, rim_depth)
            - trim_rim(loss_term, rim_depth) * current_state
        )
        received_tendency, received_carried = from_behind((tendency, carried), "lvl", 1)
        inflow = 0.5 * (received_prev + received_tendency) - received_carried
        received_prev = received_tendency
        inflow_wide = padded_2(inflow, (("gx", 1), ("gy", 2)), rim_depth)
        right_side = core_cells + production + inflow_wide
        denominator = 1.0 + loss_term + weight_sum
        iterate = widened
        for sweep_index in range(SWEEPS):
            summed = trim_rim(right_side, sweep_index) + neighbours(
                iterate, trim_all(coeffs, sweep_index)
            )
            iterate = trim_rim(inside, sweep_index) * summed / trim_rim(denominator, sweep_index)
        right_inner = trim_rim(right_side, rim_depth)
        production_inner = trim_rim(production, rim_depth)
        carried = production_inner + (iterate - right_inner)
        current_state = jnp.where(advance, iterate, current_state)
    return current_state[None]


def solution(mesh):
    in_specs = (P(None, "gx", "gy", None), P("gx", "gy", None), P(), P(), P(), P())
    out_specs = P("lvl", None, "gx", "gy", None)
    return jax.shard_map(
        on_device, mesh=mesh, in_specs=in_specs, out_specs=out_specs, check_vma=False
    )
```

profile of v0, /device:TPU:2, one launch (start us, length us, event | category | flops | bytes accessed | tf_op | source)
XLA Modules:
  0.0 579.2 jit_solution(12078204597514492033)
XLA Ops:
  2.1 4.7 collective-permute-start.4
  9.5 4.6 collective-permute-start
  24.9 4.5 collective-permute-start.6
  33.8 3.9 collective-permute-done.7
  41.5 4.6 add_add_fusion.12
  50.5 8.4 %collective-permute-done.8 = f32[16,8,8,128]{3,0,2,1:T(8,128)S(1)} collective-permute-done((f32[16,8,8,128]{3,0,2,1:T(8,128)S(1)}, f32[16,8,8,128]{3,0,2,1:T(8,128)S(1)}, u32[]{:S(2)}, u32[]{:S(2)}) %collective-permute-start.8) | collective-permute-done | bytes 524320 | tf_op jit(solution)/shard_map/ppermute | solution.py:27
  60.3 4.5 collective-permute-start.10
  68.0 4.4 collective-permute-done.11
  81.4 3.8 collective-permute-done.13
  85.2 4.4 fusion.19
  100.5 4.4 collective-permute-done.15
  115.3 4.4 collective-permute-done.17
  132.3 8.6 %collective-permute-done.18 = f32[16,8,8,128]{3,0,2,1:T(8,128)S(1)} collective-permute-done((f32[16,8,8,128]{3,0,2,1:T(8,128)S(1)}, f32[16,8,8,128]{3,0,2,1:T(8,128)S(1)}, u32[]{:S(2)}, u32[]{:S(2)}) %collective-permute-start.18) | collective-permute-done | bytes 524320 | tf_op jit(solution)/shard_map/ppermute | solution.py:27
  145.6 4.4 collective-permute-done.21
  157.9 5.1 collective-permute-done.23
  163.1 8.0 %fusion.26 = (f32[16,14,14,128]{3,0,2,1:T(8,128)S(1)}, f32[16,14,14,128]{3,0,2,1:T(8,128)S(1)}) fusion(f32[16,14,14,128]{3,0,2,1:T(8,128)} %copy-done.21, f32[16,14,14,128]{3,0,2,1:T(8,128)} %copy-done.74, f32[16,14,14,128]{3,0,2,1:T(8,128)} %copy-done.23, f32[16,14,14,128]{3,0,2,1:T(8,128)} %copy-done.19, f32[16,16,16,128]{3,0,2,1:T(8,128)S(1)} %get-tuple-element.98, ...), kind=kLoop, calls=%fused_computation.103 | loop fusion | flops 8830976 | bytes 28902160 | tf_op jit(solution)/shard_map/div | solution.py:128
  182.8 4.4 collective-permute-done.25
  195.5 4.4 collective-permute-done.27
  212.3 8.6 %collective-permute-done.28 = f32[16,8,8,128]{3,0,2,1:T(8,128)S(1)} collective-permute-done((f32[16,8,8,128]{3,0,2,1:T(8,128)S(1)}, f32[16,8,8,128]{3,0,2,1:T(8,128)S(1)}, u32[]{:S(2)}, u32[]{:S(2)}) %collective-permute-start.28) | collective-permute-done | bytes 524320 | tf_op jit(solution)/shard_map/ppermute | solution.py:27
  225.6 4.4 collective-permute-done.31
  237.9 5.1 collective-permute-done.33
  243.1 8.0 %fusion.33 = (f32[16,14,14,128]{3,0,2,1:T(8,128)S(1)}, f32[16,14,14,128]{3,0,2,1:T(8,128)S(1)}) fusion(f32[16,14,14,128]{3,0,2,1:T(8,128)} %copy-done.33, f32[16,14,14,128]{3,0,2,1:T(8,128)} %copy-done.75, f32[16,14,14,128]{3,0,2,1:T(8,128)} %copy-done.35, f32[16,14,14,128]{3,0,2,1:T(8,128)} %copy-done.31, f32[16,16,16,128]{3,0,2,1:T(8,128)S(1)} %get-tuple-element.96, ...), kind=kLoop, calls=%fused_computation.110 | loop fusion | flops 8830976 | bytes 28902160 | tf_op jit(solution)/shard_map/div | solution.py:128
  262.8 4.4 collective-permute-done.35
  275.5 4.4 collective-permute-done.37
  281.8 3.8 add_add_fusion.6
  292.3 8.6 %collective-permute-done.38 = f32[16,8,8,128]{3,0,2,1:T(8,128)S(1)} collective-permute-done((f32[16,8,8,128]{3,0,2,1:T(8,128)S(1)}, f32[16,8,8,128]{3,0,2,1:T(8,128)S(1)}, u32[]{:S(2)}, u32[]{:S(2)}) %collective-permute-start.38) | collective-permute-done | bytes 524320 | tf_op jit(solution)/shard_map/ppermute | solution.py:27
  305.6 4.4 collective-permute-done.41
  317.9 5.1 collective-permute-done.43
  323.1 8.0 %fusion.40 = (f32[16,14,14,128]{3,0,2,1:T(8,128)S(1)}, f32[16,14,14,128]{3,0,2,1:T(8,128)S(1)}) fusion(f32[16,14,14,128]{3,0,2,1:T(8,128)} %copy-done.45, f32[16,14,14,128]{3,0,2,1:T(8,128)} %copy-done.76, f32[16,14,14,128]{3,0,2,1:T(8,128)} %copy-done.47, f32[16,14,14,128]{3,0,2,1:T(8,128)} %copy-done.43, f32[16,16,16,128]{3,0,2,1:T(8,128)S(1)} %get-tuple-element.94, ...), kind=kLoop, calls=%fused_computation.117 | loop fusion | flops 8830976 | bytes 28902160 | tf_op jit(solution)/shard_map/div | solution.py:128
  342.8 4.4 collective-permute-done.45
  355.5 4.4 collective-permute-done.47
  372.3 8.6 %collective-permute-done.48 = f32[16,8,8,128]{3,0,2,1:T(8,128)S(1)} collective-permute-done((f32[16,8,8,128]{3,0,2,1:T(8,128)S(1)}, f32[16,8,8,128]{3,0,2,1:T(8,128)S(1)}, u32[]{:S(2)}, u32[]{:S(2)}) %collective-permute-start.48) | collective-permute-done | bytes 524320 | tf_op jit(solution)/shard_map/ppermute | solution.py:27
  385.6 4.4 collective-permute-done.51
  397.9 5.1 collective-permute-done.53
  403.1 8.0 %fusion.47 = (f32[16,14,14,128]{3,0,2,1:T(8,128)S(1)}, f32[16,14,14,128]{3,0,2,1:T(8,128)S(1)}) fusion(f32[16,14,14,128]{3,0,2,1:T(8,128)} %copy-done.57, f32[16,14,14,128]{3,0,2,1:T(8,128)} %copy-done.78, f32[16,14,14,128]{3,0,2,1:T(8,128)} %copy-done.59, f32[16,14,14,128]{3,0,2,1:T(8,128)} %copy-done.55, f32[16,16,16,128]{3,0,2,1:T(8,128)S(1)} %get-tuple-element.92, ...), kind=kLoop, calls=%fused_computation.124 | loop fusion | flops 8830976 | bytes 28902160 | tf_op jit(solution)/shard_map/div | solution.py:128
  422.8 4.4 collective-permute-done.55
  435.5 4.4 collective-permute-done.57
  452.3 8.6 %collective-permute-done.58 = f32[16,8,8,128]{3,0,2,1:T(8,128)S(1)} collective-permute-done((f32[16,8,8,128]{3,0,2,1:T(8,128)S(1)}, f32[16,8,8,128]{3,0,2,1:T(8,128)S(1)}, u32[]{:S(2)}, u32[]{:S(2)}) %collective-permute-start.58) | collective-permute-done | bytes 524320 | tf_op jit(solution)/shard_map/ppermute | solution.py:27
  465.7 4.4 collective-permute-done.61
  478.0 5.1 collective-permute-done.63
  483.1 8.0 %fusion.54 = (f32[16,14,14,128]{3,0,2,1:T(8,128)S(1)}, f32[16,14,14,128]{3,0,2,1:T(8,128)S(1)}) fusion(f32[16,14,14,128]{3,0,2,1:T(8,128)} %copy-done.69, f32[16,14,14,128]{3,0,2,1:T(8,128)} %copy-done.77, f32[16,14,14,128]{3,0,2,1:T(8,128)} %copy-done.71, f32[16,14,14,128]{3,0,2,1:T(8,128)} %copy-done.67, f32[16,16,16,128]{3,0,2,1:T(8,128)S(1)} %get-tuple-element.90, ...), kind=kLoop, calls=%fused_computation.131 | loop fusion | flops 8830976 | bytes 28902160 | tf_op jit(solution)/shard_map/div | solution.py:128
  503.3 4.4 collective-permute-done.65
  516.1 4.4 collective-permute-done.67
  522.3 3.8 add_add_fusion
  532.7 8.6 %collective-permute-done.68 = f32[16,8,8,128]{3,0,2,1:T(8,128)S(1)} collective-permute-done((f32[16,8,8,128]{3,0,2,1:T(8,128)S(1)}, f32[16,8,8,128]{3,0,2,1:T(8,128)S(1)}, u32[]{:S(2)}, u32[]{:S(2)}) %collective-permute-start.68) | collective-permute-done | bytes 524320 | tf_op jit(solution)/shard_map/ppermute | solution.py:27
  546.1 4.4 collective-permute-done.71
  558.3 5.1 collective-permute-done.73
  563.5 8.0 %fusion.61 = (f32[16,14,14,128]{3,0,2,1:T(8,128)S(1)}, f32[16,14,14,128]{3,0,2,1:T(8,128)S(1)}) fusion(f32[16,14,14,128]{3,0,2,1:T(8,128)} %copy-done.9, f32[16,14,14,128]{3,0,2,1:T(8,128)} %copy-done.73, f32[16,14,14,128]{3,0,2,1:T(8,128)} %copy-done.11, f32[16,14,14,128]{3,0,2,1:T(8,128)} %copy-done.7, f32[16,16,16,128]{3,0,2,1:T(8,128)S(1)} %get-tuple-element.88, ...), kind=kLoop, calls=%fused_computation.138 | loop fusion | flops 8830976 | bytes 28902160 | tf_op jit(solution)/shard_map/div | solution.py:128
  (554 shorter events, 311.0 us)
Async XLA Ops:
  0.8 24.1 %collective-permute-start.5 = (f32[4,8,128]{2,1,0:T(8,128)S(1)}, f32[4,8,128]{2,1,0:T(8,128)S(1)}, u32[]{:S(2)}, u32[]{:S(2)}) collective-permute-start(f32[4,8,128]{2,1,0:T(8,128)S(1)} %get-tuple-element.159), channel_id=1, source_target_pairs={{4,0},{5,1},{6,2},{7,3},{12,8},{13,9},{14,10},{15,11},{20,16},{21,... | collective-permute-start | bytes 49160 | tf_op jit(solution)/shard_map/ppermute | solution.py:19
  2.1 14.7 %collective-permute-start.4 = (f32[4,8,128]{2,1,0:T(8,128)S(1)}, f32[4,8,128]{2,1,0:T(8,128)S(1)}, u32[]{:S(2)}, u32[]{:S(2)}) collective-permute-start(f32[4,8,128]{2,1,0:T(8,128)S(1)} %get-tuple-element.160), channel_id=1, source_target_pairs={{0,4},{1,5},{2,6},{3,7},{8,12},{9,13},{10,14},{11,15},{16,20},{17,... | collective-permute-start | bytes 49160 | tf_op jit(solution)/shard_map/ppermute | solution.py:18
  8.2 10.9 %collective-permute-start.1 = (f32[16,4,8,128]{3,0,2,1:T(8,128)S(1)}, f32[16,4,8,128]{3,0,2,1:T(8,128)S(1)}, u32[]{:S(2)}, u32[]{:S(2)}) collective-permute-start(f32[16,4,8,128]{3,0,2,1:T(8,128)S(1)} %get-tuple-element.155), channel_id=1, source_target_pairs={{4,0},{5,1},{6,2},{7,3},{12,8},{13,9},{14,10},{15,11},{20,16},{21,... | collective-permute-start | bytes 786440 | tf_op jit(solution)/shard_map/ppermute | solution.py:19
  9.5 9.3 %collective-permute-start = (f32[16,4,8,128]{3,0,2,1:T(8,128)S(1)}, f32[16,4,8,128]{3,0,2,1:T(8,128)S(1)}, u32[]{:S(2)}, u32[]{:S(2)}) collective-permute-start(f32[16,4,8,128]{3,0,2,1:T(8,128)S(1)} %get-tuple-element.156), channel_id=1, source_target_pairs={{0,4},{1,5},{2,6},{3,7},{8,12},{9,13},{10,14},{11,15},{16,20},{17,... | collective-permute-start | bytes 786440 | tf_op jit(solution)/shard_map/ppermute | solution.py:18
  14.9 35.6 %collective-permute-start.9 = (f32[16,8,8,128]{3,0,2,1:T(8,128)}, f32[16,8,8,128]{3,0,2,1:T(8,128)}, u32[]{:S(2)}, u32[]{:S(2)}) collective-permute-start(f32[16,8,8,128]{3,0,2,1:T(8,128)} %broadcast_in_dim.4), channel_id=1, source_target_pairs={{0,8},{8,16},{16,24},{1,9},{9,17},{17,25},{2,10},{10,18},{18,26},{... | collective-permute-start | bytes 1572872 | tf_op jit(solution)/shard_map/ppermute | solution.py:27
  20.1 17.8 %collective-permute-start.2 = (f32[16,16,4,128]{3,0,2,1:T(8,128)}, f32[16,16,4,128]{3,0,2,1:T(8,128)S(1)}, u32[]{:S(2)}, u32[]{:S(2)}) collective-permute-start(f32[16,16,4,128]{3,0,2,1:T(8,128)} %get-tuple-element.113), channel_id=1, source_target_pairs={{0,1},{1,2},{2,3},{4,5},{5,6},{6,7},{8,9},{9,10},{10,11},{12,13},{... | collective-permute-start | bytes 1572872 | tf_op jit(solution)/shard_map/ppermute | solution.py:18
  23.6 14.3 %collective-permute-start.3 = (f32[16,16,4,128]{3,0,2,1:T(8,128)S(1)}, f32[16,16,4,128]{3,0,2,1:T(8,128)S(1)}, u32[]{:S(2)}, u32[]{:S(2)}) collective-permute-start(f32[16,16,4,128]{3,0,2,1:T(8,128)S(1)} %get-tuple-element.114), channel_id=1, source_target_pairs={{1,0},{2,1},{3,2},{5,4},{6,5},{7,6},{9,8},{10,9},{11,10},{13,12},{... | collective-permute-start | bytes 1572872 | tf_op jit(solution)/shard_map/ppermute | solution.py:19
  24.9 8.9 %collective-permute-start.6 = (f32[16,4,128]{2,1,0:T(4,128)S(1)}, f32[16,4,128]{2,1,0:T(4,128)S(1)}, u32[]{:S(2)}, u32[]{:S(2)}) collective-permute-start(f32[16,4,128]{2,1,0:T(4,128)S(1)} %get-tuple-element.157), channel_id=1, source_target_pairs={{0,1},{1,2},{2,3},{4,5},{5,6},{6,7},{8,9},{9,10},{10,11},{12,13},{... | collective-permute-start | bytes 98312 | tf_op jit(solution)/shard_map/ppermute | solution.py:18
  29.5 8.3 %collective-permute-start.7 = (f32[16,4,128]{2,1,0:T(4,128)S(1)}, f32[16,4,128]{2,1,0:T(4,128)S(1)}, u32[]{:S(2)}, u32[]{:S(2)}) collective-permute-start(f32[16,4,128]{2,1,0:T(4,128)S(1)} %get-tuple-element.158), channel_id=1, source_target_pairs={{1,0},{2,1},{3,2},{5,4},{6,5},{7,6},{9,8},{10,9},{11,10},{13,12},{... | collective-permute-start | bytes 98312 | tf_op jit(solution)/shard_map/ppermute | solution.py:19
  48.4 10.5 %collective-permute-start.8 = (f32[16,8,8,128]{3,0,2,1:T(8,128)S(1)}, f32[16,8,8,128]{3,0,2,1:T(8,128)S(1)}, u32[]{:S(2)}, u32[]{:S(2)}) collective-permute-start(f32[16,8,8,128]{3,0,2,1:T(8,128)S(1)} %fusion.299), channel_id=1, source_target_pairs={{0,8},{8,16},{16,24},{1,9},{9,17},{17,25},{2,10},{10,18},{18,26},{... | collective-permute-start | bytes 1572872 | tf_op jit(solution)/shard_map/ppermute | solution.py:27
  72.5 8.2 %collective-permute-start.12 = (f32[16,14,3,128]{3,0,2,1:T(8,128)S(1)}, f32[16,14,3,128]{3,0,2,1:T(8,128)S(1)}, u32[]{:S(2)}, u32[]{:S(2)}) collective-permute-start(f32[16,14,3,128]{3,0,2,1:T(8,128)S(1)} %get-tuple-element.127), channel_id=1, source_target_pairs={{0,1},{1,2},{2,3},{4,5},{5,6},{6,7},{8,9},{9,10},{10,11},{12,13},{... | collective-permute-start | bytes 1032200 | tf_op jit(solution)/shard_map/ppermute | solution.py:18
  75.9 9.2 %collective-permute-start.13 = (f32[16,14,3,128]{3,0,2,1:T(8,128)S(1)}, f32[16,14,3,128]{3,0,2,1:T(8,128)}, u32[]{:S(2)}, u32[]{:S(2)}) collective-permute-start(f32[16,14,3,128]{3,0,2,1:T(8,128)S(1)} %get-tuple-element.128), channel_id=1, source_target_pairs={{1,0},{2,1},{3,2},{5,4},{6,5},{7,6},{9,8},{10,9},{11,10},{13,12},{... | collective-permute-start | bytes 1032200 | tf_op jit(solution)/shard_map/ppermute | solution.py:19
  96.7 8.3 %collective-permute-start.15 = (f32[16,4,8,128]{3,0,2,1:T(8,128)S(1)}, f32[16,4,8,128]{3,0,2,1:T(8,128)S(1)}, u32[]{:S(2)}, u32[]{:S(2)}) collective-permute-start(f32[16,4,8,128]{3,0,2,1:T(8,128)S(1)} %get-tuple-element.152), channel_id=1, source_target_pairs={{4,0},{5,1},{6,2},{7,3},{12,8},{13,9},{14,10},{15,11},{20,16},{21,... | collective-permute-start | bytes 786440 | tf_op jit(solution)/shard_map/ppermute | solution.py:19
  105.1 10.2 %collective-permute-start.16 = (f32[16,16,4,128]{3,0,2,1:T(8,128)S(1)}, f32[16,16,4,128]{3,0,2,1:T(8,128)S(1)}, u32[]{:S(2)}, u32[]{:S(2)}) collective-permute-start(f32[16,16,4,128]{3,0,2,1:T(8,128)S(1)} %get-tuple-element.111), channel_id=1, source_target_pairs={{0,1},{1,2},{2,3},{4,5},{5,6},{6,7},{8,9},{9,10},{10,11},{12,13},{... | collective-permute-start | bytes 1572872 | tf_op jit(solution)/shard_map/ppermute | solution.py:18
  108.6 11.1 %collective-permute-start.17 = (f32[16,16,4,128]{3,0,2,1:T(8,128)S(1)}, f32[16,16,4,128]{3,0,2,1:T(8,128)S(1)}, u32[]{:S(2)}, u32[]{:S(2)}) collective-permute-start(f32[16,16,4,128]{3,0,2,1:T(8,128)S(1)} %get-tuple-element.112), channel_id=1, source_target_pairs={{1,0},{2,1},{3,2},{5,4},{6,5},{7,6},{9,8},{10,9},{11,10},{13,12},{... | collective-permute-start | bytes 1572872 | tf_op jit(solution)/shard_map/ppermute | solution.py:19
  110.8 21.5 %collective-permute-start.19 = (f32[16,8,8,128]{3,0,2,1:T(8,128)}, f32[16,8,8,128]{3,0,2,1:T(8,128)S(1)}, u32[]{:S(2)}, u32[]{:S(2)}) collective-permute-start(f32[16,8,8,128]{3,0,2,1:T(8,128)} %subtract_add_fusion.5), channel_id=1, source_target_pairs={{0,8},{8,16},{16,24},{1,9},{9,17},{17,25},{2,10},{10,18},{18,26},{... | collective-permute-start | bytes 1572872 | tf_op jit(solution)/shard_map/ppermute | solution.py:27
  130.3 10.5 %collective-permute-start.18 = (f32[16,8,8,128]{3,0,2,1:T(8,128)S(1)}, f32[16,8,8,128]{3,0,2,1:T(8,128)S(1)}, u32[]{:S(2)}, u32[]{:S(2)}) collective-permute-start(f32[16,8,8,128]{3,0,2,1:T(8,128)S(1)} %fusion.313), channel_id=1, source_target_pairs={{0,8},{8,16},{16,24},{1,9},{9,17},{17,25},{2,10},{10,18},{18,26},{... | collective-permute-start | bytes 1572872 | tf_op jit(solution)/shard_map/ppermute | solution.py:27
  153.6 9.4 %collective-permute-start.23 = (f32[16,14,3,128]{3,0,2,1:T(8,128)}, f32[16,14,3,128]{3,0,2,1:T(8,128)}, u32[]{:S(2)}, u32[]{:S(2)}) collective-permute-start(f32[16,14,3,128]{3,0,2,1:T(8,128)} %get-tuple-element.126), channel_id=1, source_target_pairs={{1,0},{2,1},{3,2},{5,4},{6,5},{7,6},{9,8},{10,9},{11,10},{13,12},{... | collective-permute-start | bytes 1032200 | tf_op jit(solution)/shard_map/ppermute | solution.py:19
  179.0 8.3 %collective-permute-start.25 = (f32[16,4,8,128]{3,0,2,1:T(8,128)S(1)}, f32[16,4,8,128]{3,0,2,1:T(8,128)S(1)}, u32[]{:S(2)}, u32[]{:S(2)}) collective-permute-start(f32[16,4,8,128]{3,0,2,1:T(8,128)S(1)} %get-tuple-element.148), channel_id=1, source_target_pairs={{4,0},{5,1},{6,2},{7,3},{12,8},{13,9},{14,10},{15,11},{20,16},{21,... | collective-permute-start | bytes 786440 | tf_op jit(solution)/shard_map/ppermute | solution.py:19
  187.4 8.1 %collective-permute-start.26 = (f32[16,16,4,128]{3,0,2,1:T(8,128)S(1)}, f32[16,16,4,128]{3,0,2,1:T(8,128)S(1)}, u32[]{:S(2)}, u32[]{:S(2)}) collective-permute-start(f32[16,16,4,128]{3,0,2,1:T(8,128)S(1)} %get-tuple-element.109), channel_id=1, source_target_pairs={{0,1},{1,2},{2,3},{4,5},{5,6},{6,7},{8,9},{9,10},{10,11},{12,13},{... | collective-permute-start | bytes 1572872 | tf_op jit(solution)/shard_map/ppermute | solution.py:18
  188.9 11.1 %collective-permute-start.27 = (f32[16,16,4,128]{3,0,2,1:T(8,128)S(1)}, f32[16,16,4,128]{3,0,2,1:T(8,128)S(1)}, u32[]{:S(2)}, u32[]{:S(2)}) collective-permute-start(f32[16,16,4,128]{3,0,2,1:T(8,128)S(1)} %get-tuple-element.110), channel_id=1, source_target_pairs={{1,0},{2,1},{3,2},{5,4},{6,5},{7,6},{9,8},{10,9},{11,10},{13,12},{... | collective-permute-start | bytes 1572872 | tf_op jit(solution)/shard_map/ppermute | solution.py:19
  191.3 20.9 %collective-permute-start.29 = (f32[16,8,8,128]{3,0,2,1:T(8,128)S(1)}, f32[16,8,8,128]{3,0,2,1:T(8,128)S(1)}, u32[]{:S(2)}, u32[]{:S(2)}) collective-permute-start(f32[16,8,8,128]{3,0,2,1:T(8,128)S(1)} %subtract_add_fusion.4), channel_id=1, source_target_pairs={{0,8},{8,16},{16,24},{1,9},{9,17},{17,25},{2,10},{10,18},{18,26},{... | collective-permute-start | bytes 1572872 | tf_op jit(solution)/shard_map/ppermute | solution.py:27
  210.3 10.5 %collective-permute-start.28 = (f32[16,8,8,128]{3,0,2,1:T(8,128)S(1)}, f32[16,8,8,128]{3,0,2,1:T(8,128)S(1)}, u32[]{:S(2)}, u32[]{:S(2)}) collective-permute-start(f32[16,8,8,128]{3,0,2,1:T(8,128)S(1)} %fusion.327), channel_id=1, source_target_pairs={{0,8},{8,16},{16,24},{1,9},{9,17},{17,25},{2,10},{10,18},{18,26},{... | collective-permute-start | bytes 1572872 | tf_op jit(solution)/shard_map/ppermute | solution.py:27
  233.6 9.4 %collective-permute-start.33 = (f32[16,14,3,128]{3,0,2,1:T(8,128)}, f32[16,14,3,128]{3,0,2,1:T(8,128)}, u32[]{:S(2)}, u32[]{:S(2)}) collective-permute-start(f32[16,14,3,128]{3,0,2,1:T(8,128)} %get-tuple-element.124), channel_id=1, source_target_pairs={{1,0},{2,1},{3,2},{5,4},{6,5},{7,6},{9,8},{10,9},{11,10},{13,12},{... | collective-permute-start | bytes 1032200 | tf_op jit(solution)/shard_map/ppermute | solution.py:19
  259.0 8.3 %collective-permute-start.35 = (f32[16,4,8,128]{3,0,2,1:T(8,128)S(1)}, f32[16,4,8,128]{3,0,2,1:T(8,128)S(1)}, u32[]{:S(2)}, u32[]{:S(2)}) collective-permute-start(f32[16,4,8,128]{3,0,2,1:T(8,128)S(1)} %get-tuple-element.144), channel_id=1, source_target_pairs={{4,0},{5,1},{6,2},{7,3},{12,8},{13,9},{14,10},{15,11},{20,16},{21,... | collective-permute-start | bytes 786440 | tf_op jit(solution)/shard_map/ppermute | solution.py:19
  267.4 8.1 %collective-permute-start.36 = (f32[16,16,4,128]{3,0,2,1:T(8,128)S(1)}, f32[16,16,4,128]{3,0,2,1:T(8,128)S(1)}, u32[]{:S(2)}, u32[]{:S(2)}) collective-permute-start(f32[16,16,4,128]{3,0,2,1:T(8,128)S(1)} %get-tuple-element.107), channel_id=1, source_target_pairs={{0,1},{1,2},{2,3},{4,5},{5,6},{6,7},{8,9},{9,10},{10,11},{12,13},{... | collective-permute-start | bytes 1572872 | tf_op jit(solution)/shard_map/ppermute | solution.py:18
  268.9 11.1 %collective-permute-start.37 = (f32[16,16,4,128]{3,0,2,1:T(8,128)S(1)}, f32[16,16,4,128]{3,0,2,1:T(8,128)S(1)}, u32[]{:S(2)}, u32[]{:S(2)}) collective-permute-start(f32[16,16,4,128]{3,0,2,1:T(8,128)S(1)} %get-tuple-element.108), channel_id=1, source_target_pairs={{1,0},{2,1},{3,2},{5,4},{6,5},{7,6},{9,8},{10,9},{11,10},{13,12},{... | collective-permute-start | bytes 1572872 | tf_op jit(solution)/shard_map/ppermute | solution.py:19
  271.3 20.9 %collective-permute-start.39 = (f32[16,8,8,128]{3,0,2,1:T(8,128)S(1)}, f32[16,8,8,128]{3,0,2,1:T(8,128)S(1)}, u32[]{:S(2)}, u32[]{:S(2)}) collective-permute-start(f32[16,8,8,128]{3,0,2,1:T(8,128)S(1)} %subtract_add_fusion.3), channel_id=1, source_target_pairs={{0,8},{8,16},{16,24},{1,9},{9,17},{17,25},{2,10},{10,18},{18,26},{... | collective-permute-start | bytes 1572872 | tf_op jit(solution)/shard_map/ppermute | solution.py:27
  290.4 10.5 %collective-permute-start.38 = (f32[16,8,8,128]{3,0,2,1:T(8,128)S(1)}, f32[16,8,8,128]{3,0,2,1:T(8,128)S(1)}, u32[]{:S(2)}, u32[]{:S(2)}) collective-permute-start(f32[16,8,8,128]{3,0,2,1:T(8,128)S(1)} %fusion.341), channel_id=1, source_target_pairs={{0,8},{8,16},{16,24},{1,9},{9,17},{17,25},{2,10},{10,18},{18,26},{... | collective-permute-start | bytes 1572872 | tf_op jit(solution)/shard_map/ppermute | solution.py:27
  313.6 9.4 %collective-permute-start.43 = (f32[16,14,3,128]{3,0,2,1:T(8,128)}, f32[16,14,3,128]{3,0,2,1:T(8,128)}, u32[]{:S(2)}, u32[]{:S(2)}) collective-permute-start(f32[16,14,3,128]{3,0,2,1:T(8,128)} %get-tuple-element.122), channel_id=1, source_target_pairs={{1,0},{2,1},{3,2},{5,4},{6,5},{7,6},{9,8},{10,9},{11,10},{13,12},{... | collective-permute-start | bytes 1032200 | tf_op jit(solution)/shard_map/ppermute | solution.py:19
  339.0 8.3 %collective-permute-start.45 = (f32[16,4,8,128]{3,0,2,1:T(8,128)S(1)}, f32[16,4,8,128]{3,0,2,1:T(8,128)S(1)}, u32[]{:S(2)}, u32[]{:S(2)}) collective-permute-start(f32[16,4,8,128]{3,0,2,1:T(8,128)S(1)} %get-tuple-element.140), channel_id=1, source_target_pairs={{4,0},{5,1},{6,2},{7,3},{12,8},{13,9},{14,10},{15,11},{20,16},{21,... | collective-permute-start | bytes 786440 | tf_op jit(solution)/shard_map/ppermute | solution.py:19
  347.4 8.1 %collective-permute-start.46 = (f32[16,16,4,128]{3,0,2,1:T(8,128)S(1)}, f32[16,16,4,128]{3,0,2,1:T(8,128)S(1)}, u32[]{:S(2)}, u32[]{:S(2)}) collective-permute-start(f32[16,16,4,128]{3,0,2,1:T(8,128)S(1)} %get-tuple-element.105), channel_id=1, source_target_pairs={{0,1},{1,2},{2,3},{4,5},{5,6},{6,7},{8,9},{9,10},{10,11},{12,13},{... | collective-permute-start | bytes 1572872 | tf_op jit(solution)/shard_map/ppermute | solution.py:18
  348.9 11.1 %collective-permute-start.47 = (f32[16,16,4,128]{3,0,2,1:T(8,128)S(1)}, f32[16,16,4,128]{3,0,2,1:T(8,128)S(1)}, u32[]{:S(2)}, u32[]{:S(2)}) collective-permute-start(f32[16,16,4,128]{3,0,2,1:T(8,128)S(1)} %get-tuple-element.106), channel_id=1, source_target_pairs={{1,0},{2,1},{3,2},{5,4},{6,5},{7,6},{9,8},{10,9},{11,10},{13,12},{... | collective-permute-start | bytes 1572872 | tf_op jit(solution)/shard_map/ppermute | solution.py:19
  351.3 20.9 %collective-permute-start.49 = (f32[16,8,8,128]{3,0,2,1:T(8,128)S(1)}, f32[16,8,8,128]{3,0,2,1:T(8,128)S(1)}, u32[]{:S(2)}, u32[]{:S(2)}) collective-permute-start(f32[16,8,8,128]{3,0,2,1:T(8,128)S(1)} %subtract_add_fusion.2), channel_id=1, source_target_pairs={{0,8},{8,16},{16,24},{1,9},{9,17},{17,25},{2,10},{10,18},{18,26},{... | collective-permute-start | bytes 1572872 | tf_op jit(solution)/shard_map/ppermute | solution.py:27
  370.4 10.5 %collective-permute-start.48 = (f32[16,8,8,128]{3,0,2,1:T(8,128)S(1)}, f32[16,8,8,128]{3,0,2,1:T(8,128)S(1)}, u32[]{:S(2)}, u32[]{:S(2)}) collective-permute-start(f32[16,8,8,128]{3,0,2,1:T(8,128)S(1)} %fusion.355), channel_id=1, source_target_pairs={{0,8},{8,16},{16,24},{1,9},{9,17},{17,25},{2,10},{10,18},{18,26},{... | collective-permute-start | bytes 1572872 | tf_op jit(solution)/shard_map/ppermute | solution.py:27
  393.6 9.4 %collective-permute-start.53 = (f32[16,14,3,128]{3,0,2,1:T(8,128)}, f32[16,14,3,128]{3,0,2,1:T(8,128)}, u32[]{:S(2)}, u32[]{:S(2)}) collective-permute-start(f32[16,14,3,128]{3,0,2,1:T(8,128)} %get-tuple-element.120), channel_id=1, source_target_pairs={{1,0},{2,1},{3,2},{5,4},{6,5},{7,6},{9,8},{10,9},{11,10},{13,12},{... | collective-permute-start | bytes 1032200 | tf_op jit(solution)/shard_map/ppermute | solution.py:19
  419.0 8.3 %collective-permute-start.55 = (f32[16,4,8,128]{3,0,2,1:T(8,128)S(1)}, f32[16,4,8,128]{3,0,2,1:T(8,128)S(1)}, u32[]{:S(2)}, u32[]{:S(2)}) collective-permute-start(f32[16,4,8,128]{3,0,2,1:T(8,128)S(1)} %get-tuple-element.136), channel_id=1, source_target_pairs={{4,0},{5,1},{6,2},{7,3},{12,8},{13,9},{14,10},{15,11},{20,16},{21,... | collective-permute-start | bytes 786440 | tf_op jit(solution)/shard_map/ppermute | solution.py:19
  427.4 8.1 %collective-permute-start.56 = (f32[16,16,4,128]{3,0,2,1:T(8,128)S(1)}, f32[16,16,4,128]{3,0,2,1:T(8,128)S(1)}, u32[]{:S(2)}, u32[]{:S(2)}) collective-permute-start(f32[16,16,4,128]{3,0,2,1:T(8,128)S(1)} %get-tuple-element.103), channel_id=1, source_target_pairs={{0,1},{1,2},{2,3},{4,5},{5,6},{6,7},{8,9},{9,10},{10,11},{12,13},{... | collective-permute-start | bytes 1572872 | tf_op jit(solution)/shard_map/ppermute | solution.py:18
  428.9 11.1 %collective-permute-start.57 = (f32[16,16,4,128]{3,0,2,1:T(8,128)S(1)}, f32[16,16,4,128]{3,0,2,1:T(8,128)S(1)}, u32[]{:S(2)}, u32[]{:S(2)}) collective-permute-start(f32[16,16,4,128]{3,0,2,1:T(8,128)S(1)} %get-tuple-element.104), channel_id=1, source_target_pairs={{1,0},{2,1},{3,2},{5,4},{6,5},{7,6},{9,8},{10,9},{11,10},{13,12},{... | collective-permute-start | bytes 1572872 | tf_op jit(solution)/shard_map/ppermute | solution.py:19
  431.3 21.0 %collective-permute-start.59 = (f32[16,8,8,128]{3,0,2,1:T(8,128)S(1)}, f32[16,8,8,128]{3,0,2,1:T(8,128)S(1)}, u32[]{:S(2)}, u32[]{:S(2)}) collective-permute-start(f32[16,8,8,128]{3,0,2,1:T(8,128)S(1)} %subtract_add_fusion.1), channel_id=1, source_target_pairs={{0,8},{8,16},{16,24},{1,9},{9,17},{17,25},{2,10},{10,18},{18,26},{... | collective-permute-start | bytes 1572872 | tf_op jit(solution)/shard_map/ppermute | solution.py:27
  450.4 10.5 %collective-permute-start.58 = (f32[16,8,8,128]{3,0,2,1:T(8,128)S(1)}, f32[16,8,8,128]{3,0,2,1:T(8,128)S(1)}, u32[]{:S(2)}, u32[]{:S(2)}) collective-permute-start(f32[16,8,8,128]{3,0,2,1:T(8,128)S(1)} %fusion.369), channel_id=1, source_target_pairs={{0,8},{8,16},{16,24},{1,9},{9,17},{17,25},{2,10},{10,18},{18,26},{... | collective-permute-start | bytes 1572872 | tf_op jit(solution)/shard_map/ppermute | solution.py:27
  473.6 9.4 %collective-permute-start.63 = (f32[16,14,3,128]{3,0,2,1:T(8,128)}, f32[16,14,3,128]{3,0,2,1:T(8,128)}, u32[]{:S(2)}, u32[]{:S(2)}) collective-permute-start(f32[16,14,3,128]{3,0,2,1:T(8,128)} %get-tuple-element.118), channel_id=1, source_target_pairs={{1,0},{2,1},{3,2},{5,4},{6,5},{7,6},{9,8},{10,9},{11,10},{13,12},{... | collective-permute-start | bytes 1032200 | tf_op jit(solution)/shard_map/ppermute | solution.py:19
  499.5 8.3 %collective-permute-start.65 = (f32[16,4,8,128]{3,0,2,1:T(8,128)S(1)}, f32[16,4,8,128]{3,0,2,1:T(8,128)S(1)}, u32[]{:S(2)}, u32[]{:S(2)}) collective-permute-start(f32[16,4,8,128]{3,0,2,1:T(8,128)S(1)} %get-tuple-element.132), channel_id=1, source_target_pairs={{4,0},{5,1},{6,2},{7,3},{12,8},{13,9},{14,10},{15,11},{20,16},{21,... | collective-permute-start | bytes 786440 | tf_op jit(solution)/shard_map/ppermute | solution.py:19
  507.9 8.1 %collective-permute-start.66 = (f32[16,16,4,128]{3,0,2,1:T(8,128)S(1)}, f32[16,16,4,128]{3,0,2,1:T(8,128)S(1)}, u32[]{:S(2)}, u32[]{:S(2)}) collective-permute-start(f32[16,16,4,128]{3,0,2,1:T(8,128)S(1)} %get-tuple-element.101), channel_id=1, source_target_pairs={{0,1},{1,2},{2,3},{4,5},{5,6},{6,7},{8,9},{9,10},{10,11},{12,13},{... | collective-permute-start | bytes 1572872 | tf_op jit(solution)/shard_map/ppermute | solution.py:18
  509.4 11.1 %collective-permute-start.67 = (f32[16,16,4,128]{3,0,2,1:T(8,128)S(1)}, f32[16,16,4,128]{3,0,2,1:T(8,128)S(1)}, u32[]{:S(2)}, u32[]{:S(2)}) collective-permute-start(f32[16,16,4,128]{3,0,2,1:T(8,128)S(1)} %get-tuple-element.102), channel_id=1, source_target_pairs={{1,0},{2,1},{3,2},{5,4},{6,5},{7,6},{9,8},{10,9},{11,10},{13,12},{... | collective-permute-start | bytes 1572872 | tf_op jit(solution)/shard_map/ppermute | solution.py:19
  510.7 22.0 %collective-permute-start.69 = (f32[16,8,8,128]{3,0,2,1:T(8,128)S(1)}, f32[16,8,8,128]{3,0,2,1:T(8,128)S(1)}, u32[]{:S(2)}, u32[]{:S(2)}) collective-permute-start(f32[16,8,8,128]{3,0,2,1:T(8,128)S(1)} %get-tuple-element.7), channel_id=1, source_target_pairs={{0,8},{8,16},{16,24},{1,9},{9,17},{17,25},{2,10},{10,18},{18,26},{... | collective-permute-start | bytes 1572872 | tf_op jit(solution)/shard_map/ppermute | solution.py:27
  530.8 10.5 %collective-permute-start.68 = (f32[16,8,8,128]{3,0,2,1:T(8,128)S(1)}, f32[16,8,8,128]{3,0,2,1:T(8,128)S(1)}, u32[]{:S(2)}, u32[]{:S(2)}) collective-permute-start(f32[16,8,8,128]{3,0,2,1:T(8,128)S(1)} %fusion.383), channel_id=1, source_target_pairs={{0,8},{8,16},{16,24},{1,9},{9,17},{17,25},{2,10},{10,18},{18,26},{... | collective-permute-start | bytes 1572872 | tf_op jit(solution)/shard_map/ppermute | solution.py:27
  554.0 9.4 %collective-permute-start.73 = (f32[16,14,3,128]{3,0,2,1:T(8,128)}, f32[16,14,3,128]{3,0,2,1:T(8,128)}, u32[]{:S(2)}, u32[]{:S(2)}) collective-permute-start(f32[16,14,3,128]{3,0,2,1:T(8,128)} %get-tuple-element.116), channel_id=1, source_target_pairs={{1,0},{2,1},{3,2},{5,4},{6,5},{7,6},{9,8},{10,9},{11,10},{13,12},{... | collective-permute-start | bytes 1032200 | tf_op jit(solution)/shard_map/ppermute | solution.py:19
  (174 other events, 1140.4 us)
where the time goes:
time: 588 us; the launch traced here: 579 us
  waiting for transfers between devices  248 us (42%)
  starting transfers between devices  137 us (23%)
  other arithmetic  115 us (20%)
  matrix products  38.1 us (6%)
  local copies, waits for them, and re-layouts  37.5 us (6%)
    ppermute x30, waiting for transfers between devices, padded_2(): after = lax.ppermute(leading, axis, down)  122 us
    div x21, other arithmetic, on_device(): trim_rim(inside, sweep_index) * summed / trim_rim(denominator, sweep_index)  75 us
    ppermute x30, starting transfers between devices, padded_2(): before = lax.ppermute(last, axis, up)  69.5 us
    ppermute x30, waiting for transfers between devices, padded_2(): before = lax.ppermute(last, axis, up)  66.2 us
    ppermute x14, waiting for transfers between devices, from_behind(): lax.ppermute(value, axis, [(source, source + steps) for source in range(l...  59.8 us
    ppermute x30, starting transfers between devices, padded_2(): after = lax.ppermute(leading, axis, down)  40.4 us
    unnamed x301, local copies, waits for them, and re-layouts  29.4 us
    dot_general x7, matrix products, chemistry(): jnp.einsum('ij,jxyz->ixyz', quench, fields * fields, precision=lax.Precis...  27.3 us
  transfers between devices with their start and end apart: 74, of which 62 were waited for; matrix products, arithmetic and copies ran while one was open for 11% of the time, Pallas kernels for 0%

commit v1 on v0

v1 whole, which is shorter than its diff:
```python
import functools

import jax
import jax.numpy as jnp
from jax import lax
from jax.experimental import pallas as pl
from jax.experimental.pallas import tpu as pltpu
from jax.sharding import PartitionSpec as P

REACT = 11
STEPS = 4
SWEEPS = 4
RIM = SWEEPS - 1
AXES = ("lvl", "gx", "gy")


def split_of(count, rows, cols):
    parts_x = 1
    while parts_x * parts_x < count:
        parts_x *= 2
    parts_y = count // parts_x
    assert parts_x * parts_y == count and rows % parts_x == 0 and cols % parts_y == 0
    assert rows // parts_x >= SWEEPS and cols // parts_y >= SWEEPS
    return parts_x, parts_y


class Layout:
    def __init__(self, rows, cols):
        self.levels, self.gx, self.gy = (lax.axis_size(a) for a in AXES)
        self.parts_x, self.parts_y = split_of(self.levels, rows, cols)
        self.sub_x, self.sub_y = rows // self.parts_x, cols // self.parts_y

    def spot(self, part, gx, gy):
        half = part // self.parts_y
        half = half if gx % 2 == 0 else self.parts_x - 1 - half
        return gx * self.parts_x + half, gy * self.parts_y + part % self.parts_y

    def shifts(self, dx, dy):
        device = {}
        for part in range(self.levels):
            for gx in range(self.gx):
                for gy in range(self.gy):
                    device[self.spot(part, gx, gy)] = (part * self.gx + gx) * self.gy + gy
        return [(d, device[x + dx, y + dy]) for (x, y), d in sorted(device.items()) if (x + dx, y + dy) in device]

    def traced_spot(self):
        part, gx, gy = (lax.axis_index(a) for a in AXES)
        half = part // self.parts_y
        half = jnp.where(gx % 2 == 0, half, self.parts_x - 1 - half)
        return half, part % self.parts_y, gx, gy


def send(value, layout, dx, dy):
    return lax.ppermute(value, AXES, layout.shifts(dx, dy))


def exchange(state, layout, dim, width):
    rows, cols = state.shape[dim], state.shape[dim + 1]
    before = send(lax.slice_in_dim(state, rows - width, rows, axis=dim), layout, 1, 0)
    after = send(lax.slice_in_dim(state, 0, width, axis=dim), layout, -1, 0)
    middle = jnp.concatenate([before, state, after], axis=dim)
    left = send(lax.slice_in_dim(middle, cols - width, cols, axis=dim + 1), layout, 0, 1)
    right = send(lax.slice_in_dim(middle, 0, width, axis=dim + 1), layout, 0, -1)
    return left, middle, right


def halves(x):
    high = x.astype(jnp.bfloat16)
    return high, (x - high.astype(jnp.float32)).astype(jnp.bfloat16)


def matrix_halves(x):
    high = lax.reduce_precision(x, 8, 7)
    return high.astype(jnp.bfloat16), (x - high).astype(jnp.bfloat16)


def product(high, low, x):
    x_high, x_low = halves(x)
    dot = functools.partial(jnp.dot, preferred_element_type=jnp.float32)
    return dot(high, x_high) + (dot(high, x_low) + dot(low, x_high))


def level_pass(u_src, env, node, first, inflow_in, inflow_out, kept_old, kept_new, out):
    u, c, sq, pr, va, vb, wx, wy, wu, wl, rhs, rden, infl = env["scratch"]
    rate, mask, half_d, loss, mats = env["rate"], env["mask"], env["half_d"], env["loss"], env["mats"]
    wide_x, wide_y, fields, nz = u.shape
    rx, ry = wide_x - 2, wide_y - 2
    widths = [s.shape[1] for s in u_src]

    hd = half_d[...]

    def widen(x, carry):
        at = 0
        for strip, width in zip(u_src, widths):
            for y in range(width):
                value = strip[x, y]
                u[x, at + y] = value
                c[x, at + y] = hd + hd * (value * value)
            at += width
        return carry

    lax.fori_loop(0, wide_x, widen, 0)

    def chemistry(i, carry):
        rows = [u[2 * i + 1 + k, 1 : 1 + ry].reshape(ry * fields, nz) for k in range(2)]
        value = jnp.concatenate(rows, axis=1)
        squares = product(mats[0], mats[1], value * value)
        made = product(mats[2], mats[3], value)
        for k in range(2):
            sq[2 * i + k] = squares[:, k * nz : (k + 1) * nz].reshape(ry, fields, nz)
            pr[2 * i + k] = made[:, k * nz : (k + 1) * nz].reshape(ry, fields, nz)
        return carry

    lax.fori_loop(0, rx // 2, chemistry, 0)

    lane = lax.broadcasted_iota(jnp.int32, (fields, nz), 1)
    bottom, top = lane == 0, lane == nz - 1
    lr = loss[...]
    advance = node < STEPS

    def setup(x, carry):
        X = x + 1
        u_here, u_next = u[X, 0], u[X, 1]
        c_here, c_next = c[X, 0], c[X, 1]
        wy_next = c_here + c_next
        for y in range(ry):
            Y = y + 1
            u_prev, u_here, u_next = u_here, u_next, u[X, Y + 1]
            c_here, c_next = c_next, c[X, Y + 1]
            wy_prev, wy_next = wy_next, c_here + c_next
            wx_prev = c_here + c[X - 1, Y]
            wx_next = c_here + c[X + 1, Y]
            w_up = c_here + jnp.where(top, hd, pltpu.roll(c_here, nz - 1, 1))
            w_low = c_here + jnp.where(bottom, hd, pltpu.roll(c_here, 1, 1))
            weights = ((wx_prev + wx_next) + (wy_prev + wy_next)) + (w_up + w_low)
            w_up = jnp.where(top, 0.0, w_up)
            w_low = jnp.where(bottom, 0.0, w_low)
            near = (
                (wx_prev * u[X - 1, Y] + wx_next * u[X + 1, Y])
                + (wy_prev * u_prev + wy_next * u_next)
                + (w_low * pltpu.roll(u_here, 1, 1) + w_up * pltpu.roll(u_here, nz - 1, 1))
            )
            factor = jnp.broadcast_to(rate[x, pl.ds(y, 1), :], (fields, nz))
            made = factor * pr[x, y]
            drop = factor * (lr + sq[x, y]) + weights
            if inflow_out:
                half_t = 0.5 * (near + made - drop * u_here)
            if advance:
                source = u_here + infl[x, y] if inflow_in else u_here
            if inflow_out:
                if not first:
                    infl[x, y] = kept_old[x, y] + (half_t - u_here)
                if advance:
                    kept_new[x, y] = half_t + source
            if advance:
                right = source + made
                inverse = (mask[0, x] * mask[1, y]) / (1.0 + drop)
                rhs[x, y] = right
                rden[x, y] = inverse
                wx[x, y] = wx_next
                wy[x, y] = wy_next
                wu[x, y] = w_up
                wl[x, y] = w_low
                va[x, y] = (right + near) * inverse
        return carry

    lax.fori_loop(0, rx, setup, 0)
    if not advance:
        return

    old, new = va, vb
    for k in range(1, SWEEPS):
        last = k == SWEEPS - 1

        def sweep(x, carry, k=k, old=old, new=new, last=last):
            v_here, v_next = old[x, k - 1], old[x, k]
            w_next = wy[x, k - 1]
            for y in range(k, ry - k):
                v_prev, v_here, v_next = v_here, v_next, old[x, y + 1]
                w_prev, w_next = w_next, wy[x, y]
                near = (
                    (wx[x - 1, y] * old[x - 1, y] + wx[x, y] * old[x + 1, y])
                    + (w_prev * v_prev + w_next * v_next)
                    + (wl[x, y] * pltpu.roll(v_here, 1, 1) + wu[x, y] * pltpu.roll(v_here, nz - 1, 1))
                )
                value = (rhs[x, y] + near) * rden[x, y]
                if last:
                    out[x - k, y - k] = value
                else:
                    new[x, y] = value
            return carry

        lax.fori_loop(k, rx - k, sweep, 0)
        old, new = new, old


def wave(diagonal, levels, shapes, started, moved, rate, mask, half_d, loss, mats, kept):
    active = [p for p in range(levels) if 0 <= diagonal - p <= STEPS and not (p == levels - 1 and diagonal - p == STEPS)]
    going = [p for p in active if diagonal - p < STEPS]
    keepers = [p for p in going if p < levels - 1]
    old = [p for p in active if 0 < diagonal - p and p < levels - 1]
    sub_x, sub_y, fields, nz = shapes
    wide = (sub_x + 2 * SWEEPS, sub_y + 2 * SWEEPS, fields, nz)
    core = (sub_x + 2 * RIM, sub_y + 2 * RIM, fields, nz)
    sources = (list(started) if any(p == diagonal for p in active) else []) + (list(moved) if moved is not None else [])
    n_src = len(sources)

    def kernel(*refs):
        refs = list(refs)
        take = lambda n: [refs.pop(0) for _ in range(n)]
        src = take(n_src)
        rate_ref, mask_ref, half_ref, loss_ref, mats_ref = take(5)
        old_refs = dict(zip(old, take(len(old))))
        (state_ref,) = take(1)
        new_refs = dict(zip(keepers, take(len(keepers))))
        scratch = refs
        env = {"scratch": scratch, "rate": rate_ref, "mask": mask_ref, "half_d": half_ref, "loss": loss_ref, "mats": mats_ref}
        slot = 0
        for p in active:
            node = diagonal - p
            if node == 0:
                strips = src[:3]
            else:
                strips = [r.at[slot] for r in src[n_src - 3 :]]
                slot += 1
            level_pass(
                strips, env, node, node == 0, p > 0, p < levels - 1,
                old_refs.get(p), new_refs.get(p),
                state_ref.at[going.index(p)] if p in going else None,
            )

    vmem = pl.BlockSpec(memory_space=pltpu.VMEM)
    smem = pl.BlockSpec(memory_space=pltpu.SMEM)
    f32 = jnp.float32
    operands = sources + [rate, mask, half_d, loss, mats] + [kept[p] for p in old]
    in_specs = [vmem] * n_src + [vmem, smem, vmem, vmem, vmem] + [vmem] * len(old)
    out_shape = [jax.ShapeDtypeStruct((len(going), sub_x, sub_y, fields, nz), f32)]
    out_shape += [jax.ShapeDtypeStruct(core, f32) for _ in keepers]
    cells = core[0] * core[1] * fields * nz
    results = pl.pallas_call(
        kernel,
        out_shape=out_shape,
        in_specs=in_specs,
        out_specs=[vmem] * len(out_shape),
        scratch_shapes=[pltpu.VMEM(wide, f32)] * 2 + [pltpu.VMEM(core, f32)] * 11,
        compiler_params=pltpu.CompilerParams(vmem_limit_bytes=50 * 2**20),
        cost_estimate=pl.CostEstimate(flops=150 * cells * len(active), bytes_accessed=8 * cells, transcendentals=0),
        name="wave%d" % diagonal,
    )(*operands)
    return going, results[0], dict(zip(keepers, results[1:]))


def inside_mask(layout, half_x, half_y, gx, gy):
    length = max(layout.sub_x, layout.sub_y) + 2 * RIM
    offsets = jnp.arange(length) - RIM
    rows = (gx * layout.parts_x + half_x) * layout.sub_x + offsets
    cols = (gy * layout.parts_y + half_y) * layout.sub_y + offsets
    row_ok = (rows >= 0) & (rows < layout.sub_x * layout.parts_x * layout.gx)
    col_ok = (cols >= 0) & (cols < layout.sub_y * layout.parts_y * layout.gy)
    return jnp.stack([row_ok, col_ok]).astype(jnp.float32)


def on_device(initial, rate_factor, diffusivity, loss_rate, quench, formation):
    fields, rows, cols, nz = initial.shape
    layout = Layout(rows, cols)
    levels = layout.levels
    half_x, half_y, gx, gy = layout.traced_spot()
    sub_x, sub_y = layout.sub_x, layout.sub_y
    row_at, col_at = half_x * sub_x, half_y * sub_y

    own = lax.dynamic_slice(initial, (0, row_at, col_at, 0), (fields, sub_x, sub_y, nz))
    own = jnp.transpose(own, (1, 2, 0, 3))
    started = exchange(own, layout, 0, SWEEPS)
    own_rate = lax.dynamic_slice(rate_factor, (row_at, col_at, 0), (sub_x, sub_y, nz))
    rate = jnp.concatenate(exchange(own_rate, layout, 0, RIM), axis=1)
    mask = inside_mask(layout, half_x, half_y, gx, gy)

    reacting = (jnp.arange(fields) < REACT).astype(jnp.float32)
    half_d = jnp.broadcast_to(0.5 * diffusivity[:, None], (fields, nz))
    loss = jnp.broadcast_to((reacting * loss_rate)[:, None], (fields, nz))
    eye = jnp.eye(sub_y + 2 * RIM, dtype=jnp.float32)
    mats = []
    for matrix in ((reacting * loss_rate)[:, None] * quench, reacting[:, None] * formation):
        mats += matrix_halves(jnp.kron(eye, matrix))
    mats = jnp.stack(mats)

    kept, moved, finals = {}, None, {}
    for diagonal in range(levels + STEPS - 1):
        going, states, kept = wave(
            diagonal, levels, (sub_x, sub_y, fields, nz), started, moved, rate, mask, half_d, loss, mats, kept
        )
        needed = []
        for i, p in enumerate(going):
            done = diagonal - p + 1 == STEPS
            if done:
                finals[p] = states[i]
            if not (done and p == levels - 1):
                needed.append(i)
        if needed:
            moved = exchange(states[needed[0] : needed[-1] + 1], layout, 1, SWEEPS)

    parts = lax.all_to_all(jnp.stack([finals[p] for p in range(levels)]), "lvl", 0, 0, tiled=True)
    parts = parts.reshape(layout.parts_x, layout.parts_y, sub_x, sub_y, fields, nz)
    parts = jnp.where(gx % 2 == 0, parts, parts[::-1])
    return jnp.transpose(parts, (4, 0, 2, 1, 3, 5)).reshape(1, fields, rows, cols, nz)


def solution(mesh):
    in_specs = (P(None, "gx", "gy", None), P("gx", "gy", None), P(), P(), P(), P())
    out_specs = P("lvl", None, "gx", "gy", None)
    return jax.shard_map(
        on_device, mesh=mesh, in_specs=in_specs, out_specs=out_specs, check_vma=False
    )
```

time: 588 us -> 336 us (0.57)
  waiting for transfers between devices: 248 us -> 46.4 us
  other arithmetic: 115 us -> 3.69 us
  Pallas kernels: 0 us -> 105 us
  matrix products: 38.1 us -> 0 us
  local copies, waits for them, and re-layouts: 37.5 us -> 9.2 us
  blocking collectives: 0 us -> 20.8 us
  starting transfers between devices: 137 us -> 145 us
    ppermute x74 -> x32, waiting for transfers between devices: 248 us -> 46.4 us  [send(): return lax.ppermute(value, AXES, layout.shifts(dx, dy))]
    pallas_call x0 -> x7, Pallas kernels: none -> 105 us  [wave(): pl.pallas_call(kernel, out_shape=out_shape, in_specs=in_specs, out_specs=...]
    div x21 -> x0, other arithmetic: 75 us -> none  [on_device(): trim_rim(inside, sweep_index) * summed / trim_rim(denominator, sweep_index)]
    dot_general x14 -> x0, matrix products: 38.1 us -> none  [the longest x7 27.3 us: chemistry(): jnp.einsum('ij,jxyz->ixyz', quench, fields * fields, precision=lax.Precis...]
    unnamed x301 -> x39, local copies, waits for them, and re-layouts: 29.4 us -> 5.57 us
    all_to_all x0 -> x1, blocking collectives: none -> 20.8 us  [on_device(): lax.all_to_all(jnp.stack([finals[p] for p in range(levels)]), 'lvl', 0, 0...]
    mul x15 -> x4, other arithmetic: 11.6 us -> 2.43 us  [the longest x1 0.78 us: on_device(): reacting[:, None] * formation]
    ppermute x74 -> x32, starting transfers between devices: 137 us -> 145 us  [send(): return lax.ppermute(value, AXES, layout.shifts(dx, dy))]
  transfers between devices with their start and end apart: 74 -> 32, of which waited for: 62 -> 22; matrix products, arithmetic and copies ran while one was open for 11% -> 2% of each run, Pallas kernels for 0% -> 0%
where the time goes in v1:
time: 336 us; the launch traced here: 331 us
  starting transfers between devices  145 us (43%)
  Pallas kernels  105 us (31%)
  waiting for transfers between devices  46.4 us (14%)
  blocking collectives  20.8 us (6%)
  local copies, waits for them, and re-layouts  9.2 us (3%)
  other arithmetic  3.69 us (1%)
    ppermute x32, starting transfers between devices, send(): return lax.ppermute(value, AXES, layout.shifts(dx, dy))  145 us
    pallas_call x7, Pallas kernels, wave(): pl.pallas_call(kernel, out_shape=out_shape, in_specs=in_specs, out_specs=...  105 us
    ppermute x32, waiting for transfers between devices, send(): return lax.ppermute(value, AXES, layout.shifts(dx, dy))  46.4 us
    all_to_all x1, blocking collectives, on_device(): lax.all_to_all(jnp.stack([finals[p] for p in range(levels)]), 'lvl', 0, 0...  20.8 us
  transfers between devices with their start and end apart: 32, of which 22 were waited for; matrix products, arithmetic and copies ran while one was open for 2% of the time, Pallas kernels for 0%

profile of v1, /device:TPU:2, one launch (start us, length us, event | category | flops | bytes accessed | tf_op | source)
XLA Modules:
  0.0 331.1 jit_solution(4055876704036826354)
XLA Ops:
  1.1 1.9 collective-permute-start.1
  3.1 3.9 %collective-permute-start = (f32[4,4,16,128]{3,2,1,0:T(8,128)S(1)}, f32[4,4,16,128]{3,2,1,0:T(8,128)}, u32[]{:S(2)}, u32[]{:S(2)}) collective-permute-start(f32[4,4,16,128]{3,2,1,0:T(8,128)S(1)} %bitcast.9), channel_id=1, source_target_pairs={{0,16},{8,24},{1,17},{9,25},{2,18},{10,26},{3,19},{11,27},{16,20},... | collective-permute-start | bytes 393224 | tf_op jit(solution)/shard_map/ppermute | solution.py:54
  7.8 4.1 %collective-permute-start.4 = (f32[3,4,128]{2,1,0:T(4,128)S(1)}, f32[3,4,128]{2,1,0:T(4,128)S(1)}, u32[]{:S(2)}, u32[]{:S(2)}) collective-permute-start(f32[3,4,128]{2,1,0:T(4,128)S(1)} %get-tuple-element.45), channel_id=1, source_target_pairs={{0,16},{8,24},{1,17},{9,25},{2,18},{10,26},{3,19},{11,27},{16,20},... | collective-permute-start | bytes 18440 | tf_op jit(solution)/shard_map/ppermute | solution.py:54
  11.8 1.9 collective-permute-start.5
  20.2 3.1 collective-permute-start.2
  23.3 3.1 collective-permute-start.6
  29.7 5.6 %wave0.1 = (f32[1,4,4,16,128]{4,3,2,1,0:T(8,128)S(1)}, f32[10,10,16,128]{3,2,1,0:T(8,128)S(1)}) custom-call(f32[12,4,16,128]{3,2,1,0:T(8,128)S(1)} %collective-permute-done.2.refs_0_, f32[12,4,16,128]{3,2,1,0:T(8,128)S(1)} %pad_maximum_fusion.1.refs_1_, f32[12,4,16,128]{3,2,1,0:T(8,128)S(1)} %collective-permute-done.3.refs_2_, ...), custom_call_target="tpu_custom_call" | custom-call | flops 30720000 | bytes 1638400 | tf_op jit(solution)/shard_map/wave0/pallas_call | solution.py:240
  36.2 3.9 %collective-permute-start.8 = (f32[1,4,4,16,128]{4,3,2,1,0:T(8,128)S(1)}, f32[1,4,4,16,128]{4,3,2,1,0:T(8,128)S(1)}, u32[]{:S(2)}, u32[]{:S(2)}) collective-permute-start(f32[1,4,4,16,128]{4,3,2,1,0:T(8,128)S(1)} %get-tuple-element.23), channel_id=1, source_target_pairs={{0,16},{8,24},{1,17},{9,25},{2,18},{10,26},{3,19},{11,27},{16,20},... | collective-permute-start | bytes 393224 | tf_op jit(solution)/shard_map/ppermute | solution.py:54
  40.1 1.9 collective-permute-start.9
  43.1 4.0 %collective-permute-done.9 = f32[1,4,4,16,128]{4,3,2,1,0:T(8,128)S(1)} collective-permute-done((f32[1,4,4,16,128]{4,3,2,1,0:T(8,128)S(1)}, f32[1,4,4,16,128]{4,3,2,1,0:T(8,128)S(1)}, u32[]{:S(2)}, u32[]{:S(2)}) %collective-permute-start.9) | collective-permute-done | bytes 131104 | tf_op jit(solution)/shard_map/ppermute | solution.py:54
  48.4 3.7 %collective-permute-start.10 = (f32[1,12,4,16,128]{4,3,2,1,0:T(8,128)S(1)}, f32[1,12,4,16,128]{4,3,2,1,0:T(8,128)S(1)}, u32[]{:S(2)}, u32[]{:S(2)}) collective-permute-start(f32[1,12,4,16,128]{4,3,2,1,0:T(8,128)S(1)} %constant_dynamic-update-slice_fusion.refs_4_), channel_id=1, source_target_pairs={{0,8},{8,1},{1,9},{9,2},{2,10},{10,3},{3,11},{16,24},{24,17},{17,2... | collective-permute-start | bytes 1179656 | tf_op jit(solution)/shard_map/ppermute | solution.py:54
  53.4 12.1 %wave1.1 = (f32[2,4,4,16,128]{4,3,2,1,0:T(8,128)S(1)}, f32[10,10,16,128]{3,2,1,0:T(8,128)S(1)}, f32[10,10,16,128]{3,2,1,0:T(8,128)}) custom-call(f32[12,4,16,128]{3,2,1,0:T(8,128)S(1)} %collective-permute-done.2.refs_0_, f32[12,4,16,128]{3,2,1,0:T(8,128)S(1)} %pad_maximum_fusion.1.refs_1_, f32[12,4,16,128]{3,2,1,0:T(8,128)S(1)} %collective-permute-done.3.refs_2_, ...), custom_call_target="tpu_custom_call" | custom-call | flops 61440000 | bytes 1638400 | tf_op jit(solution)/shard_map/wave1/pallas_call | solution.py:240
  65.5 2.1 collective-permute-start.12
  67.6 3.8 %collective-permute-start.13 = (f32[2,4,4,16,128]{4,3,2,1,0:T(8,128)S(1)}, f32[2,4,4,16,128]{4,3,2,1,0:T(8,128)S(1)}, u32[]{:S(2)}, u32[]{:S(2)}) collective-permute-start(f32[2,4,4,16,128]{4,3,2,1,0:T(8,128)S(1)} %get-tuple-element.25), channel_id=1, source_target_pairs={{16,0},{24,8},{17,1},{25,9},{18,2},{26,10},{19,3},{27,11},{20,16},... | collective-permute-start | bytes 786440 | tf_op jit(solution)/shard_map/ppermute | solution.py:54
  71.4 2.4 collective-permute-done.12
  73.8 2.0 collective-permute-done.13
  77.2 7.0 %collective-permute-start.14 = (f32[2,12,4,16,128]{4,3,2,1,0:T(8,128)S(1)}, f32[2,12,4,16,128]{4,3,2,1,0:T(8,128)S(1)}, u32[]{:S(2)}, u32[]{:S(2)}) collective-permute-start(f32[2,12,4,16,128]{4,3,2,1,0:T(8,128)S(1)} %constant_dynamic-update-slice_fusion.3.refs_4_), channel_id=1, source_target_pairs={{0,8},{8,1},{1,9},{9,2},{2,10},{10,3},{3,11},{16,24},{24,17},{17,2... | collective-permute-start | bytes 2359304 | tf_op jit(solution)/shard_map/ppermute | solution.py:54
  84.2 1.8 collective-permute-done.14.refs_3_
  86.0 18.2 %wave2.1 = (f32[3,4,4,16,128]{4,3,2,1,0:T(8,128)S(1)}, f32[10,10,16,128]{3,2,1,0:T(8,128)}, f32[10,10,16,128]{3,2,1,0:T(8,128)}, f32[10,10,16,128]{3,2,1,0:T(8,128)}) custom-call(f32[12,4,16,128]{3,2,1,0:T(8,128)S(1)} %collective-permute-done.2.refs_0_, f32[12,4,16,128]{3,2,1,0:T(8,128)S(1)} %pad_maximum_fusion.1.refs_1_, ...), custom_call_target="tpu_custom_call" | custom-call | flops 92160000 | bytes 1638400 | tf_op jit(solution)/shard_map/wave2/pallas_call | solution.py:240
  104.3 1.9 collective-permute-start.16
  106.2 3.9 %collective-permute-start.17 = (f32[3,4,4,16,128]{4,3,2,1,0:T(8,128)S(1)}, f32[3,4,4,16,128]{4,3,2,1,0:T(8,128)S(1)}, u32[]{:S(2)}, u32[]{:S(2)}) collective-permute-start(f32[3,4,4,16,128]{4,3,2,1,0:T(8,128)S(1)} %get-tuple-element.28), channel_id=1, source_target_pairs={{16,0},{24,8},{17,1},{25,9},{18,2},{26,10},{19,3},{27,11},{20,16},... | collective-permute-start | bytes 1179656 | tf_op jit(solution)/shard_map/ppermute | solution.py:54
  110.1 3.8 %collective-permute-done.16 = f32[3,4,4,16,128]{4,3,2,1,0:T(8,128)S(1)} collective-permute-done((f32[3,4,4,16,128]{4,3,2,1,0:T(8,128)S(1)}, f32[3,4,4,16,128]{4,3,2,1,0:T(8,128)S(1)}, u32[]{:S(2)}, u32[]{:S(2)}) %collective-permute-start.16) | collective-permute-done | bytes 393248 | tf_op jit(solution)/shard_map/ppermute | solution.py:54
  114.0 1.9 collective-permute-done.17
  117.2 13.4 %collective-permute-start.18 = (f32[3,12,4,16,128]{4,3,2,1,0:T(8,128)S(1)}, f32[3,12,4,16,128]{4,3,2,1,0:T(8,128)S(1)}, u32[]{:S(2)}, u32[]{:S(2)}) collective-permute-start(f32[3,12,4,16,128]{4,3,2,1,0:T(8,128)S(1)} %constant_dynamic-update-slice_fusion.6.refs_4_), channel_id=1, source_target_pairs={{0,8},{8,1},{1,9},{9,2},{2,10},{10,3},{3,11},{16,24},{24,17},{17,2... | collective-permute-start | bytes 3538952 | tf_op jit(solution)/shard_map/ppermute | solution.py:54
  130.9 2.1 collective-permute-done.18.refs_3_
  134.0 23.9 %wave3.1 = (f32[4,4,4,16,128]{4,3,2,1,0:T(8,128)S(1)}, f32[10,10,16,128]{3,2,1,0:T(8,128)S(1)}, f32[10,10,16,128]{3,2,1,0:T(8,128)S(1)}, f32[10,10,16,128]{3,2,1,0:T(8,128)}) custom-call(f32[12,4,16,128]{3,2,1,0:T(8,128)S(1)} %collective-permute-done.2.refs_0_, f32[12,4,16,128]{3,2,1,0:T(8,128)S(1)} %pad_maximum_fusion.1.refs_1_, ...), custom_call_target="tpu_custom_call" | custom-call | flops 122880000 | bytes 1638400 | tf_op jit(solution)/shard_map/wave3/pallas_call | solution.py:240
  157.8 1.9 collective-permute-start.20
  159.8 4.0 %collective-permute-start.21 = (f32[4,4,4,16,128]{4,3,2,1,0:T(8,128)S(1)}, f32[4,4,4,16,128]{4,3,2,1,0:T(8,128)S(1)}, u32[]{:S(2)}, u32[]{:S(2)}) collective-permute-start(f32[4,4,4,16,128]{4,3,2,1,0:T(8,128)S(1)} %get-tuple-element.32), channel_id=1, source_target_pairs={{16,0},{24,8},{17,1},{25,9},{18,2},{26,10},{19,3},{27,11},{20,16},... | collective-permute-start | bytes 1572872 | tf_op jit(solution)/shard_map/ppermute | solution.py:54
  163.7 5.2 %collective-permute-done.20 = f32[4,4,4,16,128]{4,3,2,1,0:T(8,128)S(1)} collective-permute-done((f32[4,4,4,16,128]{4,3,2,1,0:T(8,128)S(1)}, f32[4,4,4,16,128]{4,3,2,1,0:T(8,128)S(1)}, u32[]{:S(2)}, u32[]{:S(2)}) %collective-permute-start.20) | collective-permute-done | bytes 524320 | tf_op jit(solution)/shard_map/ppermute | solution.py:54
  169.0 1.8 collective-permute-done.21
  172.2 18.2 %collective-permute-start.22 = (f32[4,12,4,16,128]{4,3,2,1,0:T(8,128)S(1)}, f32[4,12,4,16,128]{4,3,2,1,0:T(8,128)S(1)}, u32[]{:S(2)}, u32[]{:S(2)}) collective-permute-start(f32[4,12,4,16,128]{4,3,2,1,0:T(8,128)S(1)} %constant_dynamic-update-slice_fusion.9.refs_1_), channel_id=1, source_target_pairs={{0,8},{8,1},{1,9},{9,2},{2,10},{10,3},{3,11},{16,24},{24,17},{17,2... | collective-permute-start | bytes 4718600 | tf_op jit(solution)/shard_map/ppermute | solution.py:54
  191.3 2.1 collective-permute-done.22.refs_0_
  194.5 21.1 %wave4.1 = (f32[3,4,4,16,128]{4,3,2,1,0:T(8,128)S(1)}, f32[10,10,16,128]{3,2,1,0:T(8,128)S(1)}, f32[10,10,16,128]{3,2,1,0:T(8,128)S(1)}) custom-call(f32[4,12,4,16,128]{4,3,2,1,0:T(8,128)} %copy-done.7, f32[4,12,4,16,128]{4,3,2,1,0:T(8,128)} %copy-done.3, f32[4,12,4,16,128]{4,3,2,1,0:T(8,128)} %copy-done.6, ...), custom_call_target="tpu_custom_call" | custom-call | flops 122880000 | bytes 1638400 | tf_op jit(solution)/shard_map/wave4/pallas_call | solution.py:240
  215.7 2.1 collective-permute-start.24
  217.8 3.9 %collective-permute-start.25 = (f32[3,4,4,16,128]{4,3,2,1,0:T(8,128)S(1)}, f32[3,4,4,16,128]{4,3,2,1,0:T(8,128)S(1)}, u32[]{:S(2)}, u32[]{:S(2)}) collective-permute-start(f32[3,4,4,16,128]{4,3,2,1,0:T(8,128)S(1)} %get-tuple-element.36), channel_id=1, source_target_pairs={{16,0},{24,8},{17,1},{25,9},{18,2},{26,10},{19,3},{27,11},{20,16},... | collective-permute-start | bytes 1179656 | tf_op jit(solution)/shard_map/ppermute | solution.py:54
  221.7 3.6 %collective-permute-done.24 = f32[3,4,4,16,128]{4,3,2,1,0:T(8,128)S(1)} collective-permute-done((f32[3,4,4,16,128]{4,3,2,1,0:T(8,128)S(1)}, f32[3,4,4,16,128]{4,3,2,1,0:T(8,128)S(1)}, u32[]{:S(2)}, u32[]{:S(2)}) %collective-permute-start.24) | collective-permute-done | bytes 393248 | tf_op jit(solution)/shard_map/ppermute | solution.py:54
  225.4 2.0 collective-permute-done.25
  228.8 22.2 %collective-permute-start.26 = (f32[3,12,4,16,128]{4,3,2,1,0:T(8,128)S(1)}, f32[3,12,4,16,128]{4,3,2,1,0:T(8,128)S(1)}, u32[]{:S(2)}, u32[]{:S(2)}) collective-permute-start(f32[3,12,4,16,128]{4,3,2,1,0:T(8,128)S(1)} %constant_dynamic-update-slice_fusion.12.refs_1_), channel_id=1, source_target_pairs={{0,8},{8,1},{1,9},{9,2},{2,10},{10,3},{3,11},{16,24},{24,17},{17,2... | collective-permute-start | bytes 3538952 | tf_op jit(solution)/shard_map/ppermute | solution.py:54
  251.4 2.1 collective-permute-done.26.refs_0_
  254.5 15.5 %wave5.1 = (f32[2,4,4,16,128]{4,3,2,1,0:T(8,128)S(1)}, f32[10,10,16,128]{3,2,1,0:T(8,128)S(1)}) custom-call(f32[3,12,4,16,128]{4,3,2,1,0:T(8,128)} %copy-done.11, f32[3,12,4,16,128]{4,3,2,1,0:T(8,128)} %copy-done.5, f32[3,12,4,16,128]{4,3,2,1,0:T(8,128)} %copy-done.10, f32[10,10,128]{2,1,0:T(8,128)S(1)} %pad_maximum_fusion.3.refs_3_.refs_6_, ...), custom_call_target="tpu_custom_call" | custom-call | flops 92160000 | bytes 1638400 | tf_op jit(solution)/shard_map/wave5/pallas_call | solution.py:240
  269.9 1.9 collective-permute-start.28
  271.9 3.9 %collective-permute-start.29 = (f32[2,4,4,16,128]{4,3,2,1,0:T(8,128)S(1)}, f32[2,4,4,16,128]{4,3,2,1,0:T(8,128)S(1)}, u32[]{:S(2)}, u32[]{:S(2)}) collective-permute-start(f32[2,4,4,16,128]{4,3,2,1,0:T(8,128)S(1)} %get-tuple-element.39), channel_id=1, source_target_pairs={{16,0},{24,8},{17,1},{25,9},{18,2},{26,10},{19,3},{27,11},{20,16},... | collective-permute-start | bytes 786440 | tf_op jit(solution)/shard_map/ppermute | solution.py:54
  275.8 2.4 collective-permute-done.28
  278.3 1.9 collective-permute-done.29
  281.5 17.0 %collective-permute-start.30 = (f32[2,12,4,16,128]{4,3,2,1,0:T(8,128)S(1)}, f32[2,12,4,16,128]{4,3,2,1,0:T(8,128)S(1)}, u32[]{:S(2)}, u32[]{:S(2)}) collective-permute-start(f32[2,12,4,16,128]{4,3,2,1,0:T(8,128)S(1)} %constant_dynamic-update-slice_fusion.15.refs_1_), channel_id=1, source_target_pairs={{0,8},{8,1},{1,9},{9,2},{2,10},{10,3},{3,11},{16,24},{24,17},{17,2... | collective-permute-start | bytes 2359304 | tf_op jit(solution)/shard_map/ppermute | solution.py:54
  298.5 1.8 collective-permute-done.30.refs_0_
  300.3 8.9 %wave6.1 = f32[1,4,4,16,128]{4,3,2,1,0:T(8,128)S(1)} custom-call(f32[2,12,4,16,128]{4,3,2,1,0:T(8,128)S(1)} %collective-permute-done.30.refs_0_, f32[2,12,4,16,128]{4,3,2,1,0:T(8,128)S(1)} %constant_dynamic-update-slice_fusion.15.refs_1_, f32[2,12,4,16,128]{4,3,2,1,0:T(8,128)S(1)} %collective-permute-done.31.refs_2_, ...), custom_call_target="tpu_custom_call" | custom-call | flops 61440000 | bytes 1638400 | tf_op jit(solution)/shard_map/wave6/pallas_call | solution.py:240
  309.3 20.8 %all_to_all.5 = f32[4,4,4,16,128]{4,3,2,1,0:T(8,128)S(1)} all-to-all(f32[4,4,4,16,128]{4,3,2,1,0:T(8,128)S(1)} %pad_maximum_fusion), channel_id=1, replica_groups=mesh['lvl'=4,'gx'=2,'gy'=4] {'lvl'}, dimensions={0} | all-to-all | bytes 1048576 | tf_op jit(solution)/shard_map/all_to_all | solution.py:302
  (97 shorter events, 28.8 us)
Async XLA Ops:
  0.0 1.0 copy-start
  1.1 16.8 %collective-permute-start.1 = (f32[4,4,16,128]{3,2,1,0:T(8,128)S(1)}, f32[4,4,16,128]{3,2,1,0:T(8,128)}, u32[]{:S(2)}, u32[]{:S(2)}) collective-permute-start(f32[4,4,16,128]{3,2,1,0:T(8,128)S(1)} %bitcast.8), channel_id=1, source_target_pairs={{16,0},{24,8},{17,1},{25,9},{18,2},{26,10},{19,3},{27,11},{20,16},... | collective-permute-start | bytes 393224 | tf_op jit(solution)/shard_map/ppermute | solution.py:54
  3.1 14.9 %collective-permute-start = (f32[4,4,16,128]{3,2,1,0:T(8,128)S(1)}, f32[4,4,16,128]{3,2,1,0:T(8,128)}, u32[]{:S(2)}, u32[]{:S(2)}) collective-permute-start(f32[4,4,16,128]{3,2,1,0:T(8,128)S(1)} %bitcast.9), channel_id=1, source_target_pairs={{0,16},{8,24},{1,17},{9,25},{2,18},{10,26},{3,19},{11,27},{16,20},... | collective-permute-start | bytes 393224 | tf_op jit(solution)/shard_map/ppermute | solution.py:54
  7.8 10.1 %collective-permute-start.4 = (f32[3,4,128]{2,1,0:T(4,128)S(1)}, f32[3,4,128]{2,1,0:T(4,128)S(1)}, u32[]{:S(2)}, u32[]{:S(2)}) collective-permute-start(f32[3,4,128]{2,1,0:T(4,128)S(1)} %get-tuple-element.45), channel_id=1, source_target_pairs={{0,16},{8,24},{1,17},{9,25},{2,18},{10,26},{3,19},{11,27},{16,20},... | collective-permute-start | bytes 18440 | tf_op jit(solution)/shard_map/ppermute | solution.py:54
  11.8 6.1 %collective-permute-start.5 = (f32[3,4,128]{2,1,0:T(4,128)S(1)}, f32[3,4,128]{2,1,0:T(4,128)S(1)}, u32[]{:S(2)}, u32[]{:S(2)}) collective-permute-start(f32[3,4,128]{2,1,0:T(4,128)S(1)} %get-tuple-element.46), channel_id=1, source_target_pairs={{16,0},{24,8},{17,1},{25,9},{18,2},{26,10},{19,3},{27,11},{20,16},... | collective-permute-start | bytes 18440 | tf_op jit(solution)/shard_map/ppermute | solution.py:54
  18.9 10.6 %collective-permute-start.3 = (f32[12,4,16,128]{3,2,1,0:T(8,128)S(1)}, f32[12,4,16,128]{3,2,1,0:T(8,128)S(1)}, u32[]{:S(2)}, u32[]{:S(2)}) collective-permute-start(f32[12,4,16,128]{3,2,1,0:T(8,128)S(1)} %pad_maximum_fusion.1.refs_1_), channel_id=1, source_target_pairs={{8,0},{1,8},{9,1},{2,9},{10,2},{3,10},{11,3},{24,16},{17,24},{25,1... | collective-permute-start | bytes 1179656 | tf_op jit(solution)/shard_map/ppermute | solution.py:54
  20.2 9.3 %collective-permute-start.2 = (f32[12,4,16,128]{3,2,1,0:T(8,128)S(1)}, f32[12,4,16,128]{3,2,1,0:T(8,128)S(1)}, u32[]{:S(2)}, u32[]{:S(2)}) collective-permute-start(f32[12,4,16,128]{3,2,1,0:T(8,128)S(1)} %pad_maximum_fusion.1.refs_1_), channel_id=1, source_target_pairs={{0,8},{8,1},{1,9},{9,2},{2,10},{10,3},{3,11},{16,24},{24,17},{17,2... | collective-permute-start | bytes 1179656 | tf_op jit(solution)/shard_map/ppermute | solution.py:54
  23.3 4.4 %collective-permute-start.6 = (f32[10,3,128]{2,1,0:T(4,128)S(1)}, f32[10,3,128]{2,1,0:T(4,128)S(1)}, u32[]{:S(2)}, u32[]{:S(2)}) collective-permute-start(f32[10,3,128]{2,1,0:T(4,128)S(1)} %get-tuple-element.47), channel_id=1, source_target_pairs={{0,8},{8,1},{1,9},{9,2},{2,10},{10,3},{3,11},{16,24},{24,17},{17,2... | collective-permute-start | bytes 46088 | tf_op jit(solution)/shard_map/ppermute | solution.py:54
  26.4 3.1 collective-permute-start.7
  35.3 0.9 copy-start.2
  36.2 6.8 %collective-permute-start.8 = (f32[1,4,4,16,128]{4,3,2,1,0:T(8,128)S(1)}, f32[1,4,4,16,128]{4,3,2,1,0:T(8,128)S(1)}, u32[]{:S(2)}, u32[]{:S(2)}) collective-permute-start(f32[1,4,4,16,128]{4,3,2,1,0:T(8,128)S(1)} %get-tuple-element.23), channel_id=1, source_target_pairs={{0,16},{8,24},{1,17},{9,25},{2,18},{10,26},{3,19},{11,27},{16,20},... | collective-permute-start | bytes 393224 | tf_op jit(solution)/shard_map/ppermute | solution.py:54
  40.1 7.0 %collective-permute-start.9 = (f32[1,4,4,16,128]{4,3,2,1,0:T(8,128)S(1)}, f32[1,4,4,16,128]{4,3,2,1,0:T(8,128)S(1)}, u32[]{:S(2)}, u32[]{:S(2)}) collective-permute-start(f32[1,4,4,16,128]{4,3,2,1,0:T(8,128)S(1)} %get-tuple-element.23), channel_id=1, source_target_pairs={{16,0},{24,8},{17,1},{25,9},{18,2},{26,10},{19,3},{27,11},{20,16},... | collective-permute-start | bytes 393224 | tf_op jit(solution)/shard_map/ppermute | solution.py:54
  47.1 5.0 %collective-permute-start.11 = (f32[1,12,4,16,128]{4,3,2,1,0:T(8,128)S(1)}, f32[1,12,4,16,128]{4,3,2,1,0:T(8,128)S(1)}, u32[]{:S(2)}, u32[]{:S(2)}) collective-permute-start(f32[1,12,4,16,128]{4,3,2,1,0:T(8,128)S(1)} %constant_dynamic-update-slice_fusion.refs_4_), channel_id=1, source_target_pairs={{8,0},{1,8},{9,1},{2,9},{10,2},{3,10},{11,3},{24,16},{17,24},{25,1... | collective-permute-start | bytes 1179656 | tf_op jit(solution)/shard_map/ppermute | solution.py:54
  48.4 5.0 %collective-permute-start.10 = (f32[1,12,4,16,128]{4,3,2,1,0:T(8,128)S(1)}, f32[1,12,4,16,128]{4,3,2,1,0:T(8,128)S(1)}, u32[]{:S(2)}, u32[]{:S(2)}) collective-permute-start(f32[1,12,4,16,128]{4,3,2,1,0:T(8,128)S(1)} %constant_dynamic-update-slice_fusion.refs_4_), channel_id=1, source_target_pairs={{0,8},{8,1},{1,9},{9,2},{2,10},{10,3},{3,11},{16,24},{24,17},{17,2... | collective-permute-start | bytes 1179656 | tf_op jit(solution)/shard_map/ppermute | solution.py:54
  65.5 20.5 %copy-start.1 = (f32[10,10,16,128]{3,2,1,0:T(8,128)}, f32[10,10,16,128]{3,2,1,0:T(8,128)S(1)}, u32[]{:S(2)}) copy-start(f32[10,10,16,128]{3,2,1,0:T(8,128)S(1)} %get-tuple-element.26.refs_11_) | copy-start | bytes 2457604
  65.5 8.3 %collective-permute-start.12 = (f32[2,4,4,16,128]{4,3,2,1,0:T(8,128)S(1)}, f32[2,4,4,16,128]{4,3,2,1,0:T(8,128)S(1)}, u32[]{:S(2)}, u32[]{:S(2)}) collective-permute-start(f32[2,4,4,16,128]{4,3,2,1,0:T(8,128)S(1)} %get-tuple-element.25), channel_id=1, source_target_pairs={{0,16},{8,24},{1,17},{9,25},{2,18},{10,26},{3,19},{11,27},{16,20},... | collective-permute-start | bytes 786440 | tf_op jit(solution)/shard_map/ppermute | solution.py:54
  67.6 8.3 %collective-permute-start.13 = (f32[2,4,4,16,128]{4,3,2,1,0:T(8,128)S(1)}, f32[2,4,4,16,128]{4,3,2,1,0:T(8,128)S(1)}, u32[]{:S(2)}, u32[]{:S(2)}) collective-permute-start(f32[2,4,4,16,128]{4,3,2,1,0:T(8,128)S(1)} %get-tuple-element.25), channel_id=1, source_target_pairs={{16,0},{24,8},{17,1},{25,9},{18,2},{26,10},{19,3},{27,11},{20,16},... | collective-permute-start | bytes 786440 | tf_op jit(solution)/shard_map/ppermute | solution.py:54
  75.9 8.3 %collective-permute-start.15 = (f32[2,12,4,16,128]{4,3,2,1,0:T(8,128)S(1)}, f32[2,12,4,16,128]{4,3,2,1,0:T(8,128)S(1)}, u32[]{:S(2)}, u32[]{:S(2)}) collective-permute-start(f32[2,12,4,16,128]{4,3,2,1,0:T(8,128)S(1)} %constant_dynamic-update-slice_fusion.3.refs_4_), channel_id=1, source_target_pairs={{8,0},{1,8},{9,1},{2,9},{10,2},{3,10},{11,3},{24,16},{17,24},{25,1... | collective-permute-start | bytes 2359304 | tf_op jit(solution)/shard_map/ppermute | solution.py:54
  77.2 8.9 %collective-permute-start.14 = (f32[2,12,4,16,128]{4,3,2,1,0:T(8,128)S(1)}, f32[2,12,4,16,128]{4,3,2,1,0:T(8,128)S(1)}, u32[]{:S(2)}, u32[]{:S(2)}) collective-permute-start(f32[2,12,4,16,128]{4,3,2,1,0:T(8,128)S(1)} %constant_dynamic-update-slice_fusion.3.refs_4_), channel_id=1, source_target_pairs={{0,8},{8,1},{1,9},{9,2},{2,10},{10,3},{3,11},{16,24},{24,17},{17,2... | collective-permute-start | bytes 2359304 | tf_op jit(solution)/shard_map/ppermute | solution.py:54
  84.2 1.8 copy-start.12
  104.3 9.7 %collective-permute-start.16 = (f32[3,4,4,16,128]{4,3,2,1,0:T(8,128)S(1)}, f32[3,4,4,16,128]{4,3,2,1,0:T(8,128)S(1)}, u32[]{:S(2)}, u32[]{:S(2)}) collective-permute-start(f32[3,4,4,16,128]{4,3,2,1,0:T(8,128)S(1)} %get-tuple-element.28), channel_id=1, source_target_pairs={{0,16},{8,24},{1,17},{9,25},{2,18},{10,26},{3,19},{11,27},{16,20},... | collective-permute-start | bytes 1179656 | tf_op jit(solution)/shard_map/ppermute | solution.py:54
  106.2 9.7 %collective-permute-start.17 = (f32[3,4,4,16,128]{4,3,2,1,0:T(8,128)S(1)}, f32[3,4,4,16,128]{4,3,2,1,0:T(8,128)S(1)}, u32[]{:S(2)}, u32[]{:S(2)}) collective-permute-start(f32[3,4,4,16,128]{4,3,2,1,0:T(8,128)S(1)} %get-tuple-element.28), channel_id=1, source_target_pairs={{16,0},{24,8},{17,1},{25,9},{18,2},{26,10},{19,3},{27,11},{20,16},... | collective-permute-start | bytes 1179656 | tf_op jit(solution)/shard_map/ppermute | solution.py:54
  115.9 17.1 %copy-start.4 = (f32[3,12,4,16,128]{4,3,2,1,0:T(8,128)}, f32[3,12,4,16,128]{4,3,2,1,0:T(8,128)S(1)}, u32[]{:S(2)}) copy-start(f32[3,12,4,16,128]{4,3,2,1,0:T(8,128)S(1)} %constant_dynamic-update-slice_fusion.6.refs_4_) | copy-start | bytes 3538948
  115.9 15.0 %collective-permute-start.19 = (f32[3,12,4,16,128]{4,3,2,1,0:T(8,128)S(1)}, f32[3,12,4,16,128]{4,3,2,1,0:T(8,128)S(1)}, u32[]{:S(2)}, u32[]{:S(2)}) collective-permute-start(f32[3,12,4,16,128]{4,3,2,1,0:T(8,128)S(1)} %constant_dynamic-update-slice_fusion.6.refs_4_), channel_id=1, source_target_pairs={{8,0},{1,8},{9,1},{2,9},{10,2},{3,10},{11,3},{24,16},{17,24},{25,1... | collective-permute-start | bytes 3538952 | tf_op jit(solution)/shard_map/ppermute | solution.py:54
  117.2 15.7 %collective-permute-start.18 = (f32[3,12,4,16,128]{4,3,2,1,0:T(8,128)S(1)}, f32[3,12,4,16,128]{4,3,2,1,0:T(8,128)S(1)}, u32[]{:S(2)}, u32[]{:S(2)}) collective-permute-start(f32[3,12,4,16,128]{4,3,2,1,0:T(8,128)S(1)} %constant_dynamic-update-slice_fusion.6.refs_4_), channel_id=1, source_target_pairs={{0,8},{8,1},{1,9},{9,2},{2,10},{10,3},{3,11},{16,24},{24,17},{17,2... | collective-permute-start | bytes 3538952 | tf_op jit(solution)/shard_map/ppermute | solution.py:54
  130.9 2.1 copy-start.8
  132.9 1.1 copy-start.9
  157.8 11.1 %collective-permute-start.20 = (f32[4,4,4,16,128]{4,3,2,1,0:T(8,128)S(1)}, f32[4,4,4,16,128]{4,3,2,1,0:T(8,128)S(1)}, u32[]{:S(2)}, u32[]{:S(2)}) collective-permute-start(f32[4,4,4,16,128]{4,3,2,1,0:T(8,128)S(1)} %get-tuple-element.32), channel_id=1, source_target_pairs={{0,16},{8,24},{1,17},{9,25},{2,18},{10,26},{3,19},{11,27},{16,20},... | collective-permute-start | bytes 1572872 | tf_op jit(solution)/shard_map/ppermute | solution.py:54
  159.8 11.1 %collective-permute-start.21 = (f32[4,4,4,16,128]{4,3,2,1,0:T(8,128)S(1)}, f32[4,4,4,16,128]{4,3,2,1,0:T(8,128)S(1)}, u32[]{:S(2)}, u32[]{:S(2)}) collective-permute-start(f32[4,4,4,16,128]{4,3,2,1,0:T(8,128)S(1)} %get-tuple-element.32), channel_id=1, source_target_pairs={{16,0},{24,8},{17,1},{25,9},{18,2},{26,10},{19,3},{27,11},{20,16},... | collective-permute-start | bytes 1572872 | tf_op jit(solution)/shard_map/ppermute | solution.py:54
  170.9 22.5 %copy-start.3 = (f32[4,12,4,16,128]{4,3,2,1,0:T(8,128)}, f32[4,12,4,16,128]{4,3,2,1,0:T(8,128)S(1)}, u32[]{:S(2)}) copy-start(f32[4,12,4,16,128]{4,3,2,1,0:T(8,128)S(1)} %constant_dynamic-update-slice_fusion.9.refs_1_) | copy-start | bytes 4718596
  170.9 20.4 %collective-permute-start.23 = (f32[4,12,4,16,128]{4,3,2,1,0:T(8,128)S(1)}, f32[4,12,4,16,128]{4,3,2,1,0:T(8,128)S(1)}, u32[]{:S(2)}, u32[]{:S(2)}) collective-permute-start(f32[4,12,4,16,128]{4,3,2,1,0:T(8,128)S(1)} %constant_dynamic-update-slice_fusion.9.refs_1_), channel_id=1, source_target_pairs={{8,0},{1,8},{9,1},{2,9},{10,2},{3,10},{11,3},{24,16},{17,24},{25,1... | collective-permute-start | bytes 4718600 | tf_op jit(solution)/shard_map/ppermute | solution.py:54
  172.2 21.2 %collective-permute-start.22 = (f32[4,12,4,16,128]{4,3,2,1,0:T(8,128)S(1)}, f32[4,12,4,16,128]{4,3,2,1,0:T(8,128)S(1)}, u32[]{:S(2)}, u32[]{:S(2)}) collective-permute-start(f32[4,12,4,16,128]{4,3,2,1,0:T(8,128)S(1)} %constant_dynamic-update-slice_fusion.9.refs_1_), channel_id=1, source_target_pairs={{0,8},{8,1},{1,9},{9,2},{2,10},{10,3},{3,11},{16,24},{24,17},{17,2... | collective-permute-start | bytes 4718600 | tf_op jit(solution)/shard_map/ppermute | solution.py:54
  191.3 2.1 copy-start.6
  193.4 1.2 copy-start.7
  215.7 9.7 %collective-permute-start.24 = (f32[3,4,4,16,128]{4,3,2,1,0:T(8,128)S(1)}, f32[3,4,4,16,128]{4,3,2,1,0:T(8,128)S(1)}, u32[]{:S(2)}, u32[]{:S(2)}) collective-permute-start(f32[3,4,4,16,128]{4,3,2,1,0:T(8,128)S(1)} %get-tuple-element.36), channel_id=1, source_target_pairs={{0,16},{8,24},{1,17},{9,25},{2,18},{10,26},{3,19},{11,27},{16,20},... | collective-permute-start | bytes 1179656 | tf_op jit(solution)/shard_map/ppermute | solution.py:54
  217.8 9.7 %collective-permute-start.25 = (f32[3,4,4,16,128]{4,3,2,1,0:T(8,128)S(1)}, f32[3,4,4,16,128]{4,3,2,1,0:T(8,128)S(1)}, u32[]{:S(2)}, u32[]{:S(2)}) collective-permute-start(f32[3,4,4,16,128]{4,3,2,1,0:T(8,128)S(1)} %get-tuple-element.36), channel_id=1, source_target_pairs={{16,0},{24,8},{17,1},{25,9},{18,2},{26,10},{19,3},{27,11},{20,16},... | collective-permute-start | bytes 1179656 | tf_op jit(solution)/shard_map/ppermute | solution.py:54
  227.5 25.9 %copy-start.5 = (f32[3,12,4,16,128]{4,3,2,1,0:T(8,128)}, f32[3,12,4,16,128]{4,3,2,1,0:T(8,128)S(1)}, u32[]{:S(2)}) copy-start(f32[3,12,4,16,128]{4,3,2,1,0:T(8,128)S(1)} %constant_dynamic-update-slice_fusion.12.refs_1_) | copy-start | bytes 3538948
  227.5 23.9 %collective-permute-start.27 = (f32[3,12,4,16,128]{4,3,2,1,0:T(8,128)S(1)}, f32[3,12,4,16,128]{4,3,2,1,0:T(8,128)S(1)}, u32[]{:S(2)}, u32[]{:S(2)}) collective-permute-start(f32[3,12,4,16,128]{4,3,2,1,0:T(8,128)S(1)} %constant_dynamic-update-slice_fusion.12.refs_1_), channel_id=1, source_target_pairs={{8,0},{1,8},{9,1},{2,9},{10,2},{3,10},{11,3},{24,16},{17,24},{25,1... | collective-permute-start | bytes 3538952 | tf_op jit(solution)/shard_map/ppermute | solution.py:54
  228.8 24.6 %collective-permute-start.26 = (f32[3,12,4,16,128]{4,3,2,1,0:T(8,128)S(1)}, f32[3,12,4,16,128]{4,3,2,1,0:T(8,128)S(1)}, u32[]{:S(2)}, u32[]{:S(2)}) collective-permute-start(f32[3,12,4,16,128]{4,3,2,1,0:T(8,128)S(1)} %constant_dynamic-update-slice_fusion.12.refs_1_), channel_id=1, source_target_pairs={{0,8},{8,1},{1,9},{9,2},{2,10},{10,3},{3,11},{16,24},{24,17},{17,2... | collective-permute-start | bytes 3538952 | tf_op jit(solution)/shard_map/ppermute | solution.py:54
  251.4 2.1 copy-start.10
  253.4 1.1 copy-start.11
  269.9 8.3 %collective-permute-start.28 = (f32[2,4,4,16,128]{4,3,2,1,0:T(8,128)S(1)}, f32[2,4,4,16,128]{4,3,2,1,0:T(8,128)S(1)}, u32[]{:S(2)}, u32[]{:S(2)}) collective-permute-start(f32[2,4,4,16,128]{4,3,2,1,0:T(8,128)S(1)} %get-tuple-element.39), channel_id=1, source_target_pairs={{0,16},{8,24},{1,17},{9,25},{2,18},{10,26},{3,19},{11,27},{16,20},... | collective-permute-start | bytes 786440 | tf_op jit(solution)/shard_map/ppermute | solution.py:54
  271.9 8.3 %collective-permute-start.29 = (f32[2,4,4,16,128]{4,3,2,1,0:T(8,128)S(1)}, f32[2,4,4,16,128]{4,3,2,1,0:T(8,128)S(1)}, u32[]{:S(2)}, u32[]{:S(2)}) collective-permute-start(f32[2,4,4,16,128]{4,3,2,1,0:T(8,128)S(1)} %get-tuple-element.39), channel_id=1, source_target_pairs={{16,0},{24,8},{17,1},{25,9},{18,2},{26,10},{19,3},{27,11},{20,16},... | collective-permute-start | bytes 786440 | tf_op jit(solution)/shard_map/ppermute | solution.py:54
  280.2 18.4 %collective-permute-start.31 = (f32[2,12,4,16,128]{4,3,2,1,0:T(8,128)S(1)}, f32[2,12,4,16,128]{4,3,2,1,0:T(8,128)S(1)}, u32[]{:S(2)}, u32[]{:S(2)}) collective-permute-start(f32[2,12,4,16,128]{4,3,2,1,0:T(8,128)S(1)} %constant_dynamic-update-slice_fusion.15.refs_1_), channel_id=1, source_target_pairs={{8,0},{1,8},{9,1},{2,9},{10,2},{3,10},{11,3},{24,16},{17,24},{25,1... | collective-permute-start | bytes 2359304 | tf_op jit(solution)/shard_map/ppermute | solution.py:54
  281.5 18.9 %collective-permute-start.30 = (f32[2,12,4,16,128]{4,3,2,1,0:T(8,128)S(1)}, f32[2,12,4,16,128]{4,3,2,1,0:T(8,128)S(1)}, u32[]{:S(2)}, u32[]{:S(2)}) collective-permute-start(f32[2,12,4,16,128]{4,3,2,1,0:T(8,128)S(1)} %constant_dynamic-update-slice_fusion.15.refs_1_), channel_id=1, source_target_pairs={{0,8},{8,1},{1,9},{9,2},{2,10},{10,3},{3,11},{16,24},{24,17},{17,2... | collective-permute-start | bytes 2359304 | tf_op jit(solution)/shard_map/ppermute | solution.py:54

commit v2 on v1

v2 whole, which is shorter than its diff:
```python
import functools

import jax
import jax.numpy as jnp
from jax import lax
from jax.experimental import pallas as pl
from jax.experimental.pallas import tpu as pltpu
from jax.sharding import PartitionSpec as P

REACT = 11
STEPS = 4
SWEEPS = 4
RIM = SWEEPS - 1
GROUP = 4
AXES = ("lvl", "gx", "gy")


class Plan:
    def __init__(self, rows, cols):
        self.levels, self.gx, self.gy = (lax.axis_size(a) for a in AXES)
        self.rows, self.cols = rows, cols
        self.closed = self.gx <= 2
        parts = self.levels
        if self.closed:
            self.parts_x, self.parts_y = 1, 1
            while parts % (2 * self.parts_y) == 0 and cols // (2 * self.parts_y) >= SWEEPS:
                self.parts_y *= 2
            self.sub_x, self.wide_x = rows * self.gx, rows * self.gx + 2
        else:
            self.parts_x = 1
            while self.parts_x * self.parts_x < parts:
                self.parts_x *= 2
            self.parts_y = parts // self.parts_x
            assert self.parts_x * self.parts_y == parts and rows % self.parts_x == 0
            self.sub_x, self.wide_x = rows // self.parts_x, rows // self.parts_x + 2 * SWEEPS
        assert cols % self.parts_y == 0
        self.sub_y = cols // self.parts_y
        assert min(self.sub_x, self.sub_y) >= SWEEPS
        self.wide_y = self.sub_y + 2 * SWEEPS
        self.core_x, self.core_y = self.wide_x - 2, self.wide_y - 2

    def spot(self, part, gx, gy):
        at_y = gy * self.parts_y + part % self.parts_y
        if self.closed:
            return gx, part // self.parts_y, at_y
        half = part // self.parts_y
        half = half if gx % 2 == 0 else self.parts_x - 1 - half
        return gx * self.parts_x + half, 0, at_y

    def devices(self):
        found = {}
        for part in range(self.levels):
            for gx in range(self.gx):
                for gy in range(self.gy):
                    found[self.spot(part, gx, gy)] = (part * self.gx + gx) * self.gy + gy
        return found

    def column(self, device):
        return device // (self.gx * self.gy) % self.parts_y

    def shifts(self, dx, dy):
        found = self.devices()
        there = lambda s: (s[0] + dx, s[1], s[2] + dy)
        return [(d, found[there(s)]) for s, d in sorted(found.items()) if there(s) in found]


def columns(own, rate, plan):
    half = lax.axis_index("lvl") % plan.parts_y
    gx = lax.axis_index("gx")
    sub, nz = plan.sub_y, own.shape[-1]
    both = jnp.concatenate([own, rate[:, :, None, :]], axis=2) if not plan.closed else None
    if plan.closed:
        cells, planes = own.shape[0] * own.shape[1], own.shape[2]

        def pack(x, r):
            return jnp.concatenate([x.reshape(-1, nz), r.reshape(-1, nz)], axis=0)

        def unpack(packed, x, r):
            return packed[: x.size // nz].reshape(x.shape), packed[x.size // nz :].reshape(r.shape)

        if plan.gx == 2:
            theirs = unpack(lax.ppermute(pack(own, rate), "gx", [(0, 1), (1, 0)]), own, rate)
            own, rate = (
                jnp.where(gx == 0, jnp.concatenate([a, b], axis=0), jnp.concatenate([b, a], axis=0))
                for a, b in zip((own, rate), theirs)
            )
        if plan.parts_y == 2:
            pairs = sorted(
                [(a, b) for a, b in plan.shifts(0, 1) if plan.column(a) == 1]
                + [(a, b) for a, b in plan.shifts(0, -1) if plan.column(a) == 0]
            )
            outer = [jnp.where(half == 1, x[:, -SWEEPS:], x[:, :SWEEPS]) for x in (own, rate)]
            come = unpack(lax.ppermute(pack(*outer), AXES, pairs), *outer)
            wide = []
            for x, o in zip((own, rate), come):
                x_before = jnp.where(half == 0, o, x[:, sub - SWEEPS : sub])
                x_after = jnp.where(half == 0, x[:, sub : sub + SWEEPS], o)
                wide.append((x_before, jnp.where(half == 0, x[:, :sub], x[:, sub:]), x_after))
            return wide
        both = jnp.concatenate([own, rate[:, :, None, :]], axis=2)
    else:
        at = lax.axis_index("lvl") // plan.parts_y
        at = jnp.where(gx % 2 == 0, at, plan.parts_x - 1 - at) * plan.sub_x
        both = lax.dynamic_slice_in_dim(both, at, plan.sub_x, axis=0)
    both = lax.dynamic_slice_in_dim(both, half * sub, sub, axis=1)
    strips = exchange(both[None], plan)
    return [[x[0, :, :, :-1] for x in strips], [x[0, :, :, -1] for x in strips]]


def exchange(states, plan):
    if not plan.closed:
        before = lax.ppermute(states[:, -SWEEPS:], AXES, plan.shifts(1, 0))
        after = lax.ppermute(states[:, :SWEEPS], AXES, plan.shifts(-1, 0))
        states = jnp.concatenate([before, states, after], axis=1)
    before = lax.ppermute(states[:, :, -SWEEPS:], AXES, plan.shifts(0, 1))
    after = lax.ppermute(states[:, :, :SWEEPS], AXES, plan.shifts(0, -1))
    return before, states, after


def halves(x):
    high = x.astype(jnp.bfloat16)
    return high, (x - high.astype(jnp.float32)).astype(jnp.bfloat16)


def product(matrix, x):
    dot = functools.partial(jnp.dot, preferred_element_type=jnp.float32)
    n = matrix.shape[0] // 2
    high, low = halves(x)
    first = dot(matrix, high)
    return first[:n] + (first[n:] + dot(matrix[:n], low))


def level_pass(strips, env, plan, node, inflow_in, inflow_out, kept_old, kept_new, out):
    u, c, chem, va, vb, wx, wy, wu, rhs, rden = env["scratch"]
    rate, mask, half_d, loss, mats = env["rate"], env["mask"], env["half_d"], env["loss"], env["mats"]
    fields, nz = u.shape[2:]
    rx, ry = plan.core_x, plan.core_y
    hd = half_d[...]
    base = 1 if plan.closed else 0
    shrink = 0 if plan.closed else 1

    def conduct(value):
        return hd + hd * (value * value)

    def widen(x, carry):
        at = 0
        for strip in strips:
            for y in range(strip.shape[1]):
                value = strip[x, y]
                u[x + base, at + y] = value
                c[x + base, at + y] = conduct(value)
            at += strip.shape[1]
        return carry

    lax.fori_loop(0, strips[0].shape[0], widen, 0)

    lane = lax.broadcasted_iota(jnp.int32, (fields, nz), 1)
    bottom, top = lane == 0, lane == nz - 1
    lr = loss[...]
    advance = node < STEPS

    def setup(x, k):
        X = x + 1
        u_here, u_next = u[X, 0], u[X, 1]
        c_here, c_next = c[X, 0], c[X, 1]
        wy_next = c_here + c_next
        for y in range(ry):
            Y = y + 1
            u_prev, u_here, u_next = u_here, u_next, u[X, Y + 1]
            c_here, c_next = c_next, c[X, Y + 1]
            wy_prev, wy_next = wy_next, c_here + c_next
            wx_prev = c_here + c[X - 1, Y]
            wx_next = c_here + c[X + 1, Y]
            below = jnp.where(bottom, 0.0, pltpu.roll(u_here, 1, 1))
            above = jnp.where(top, 0.0, pltpu.roll(u_here, nz - 1, 1))
            w_low = c_here + conduct(below)
            w_up = c_here + conduct(above)
            weights = ((wx_prev + wx_next) + (wy_prev + wy_next)) + (w_low + w_up)
            near = (
                (wx_prev * u[X - 1, Y] + wx_next * u[X + 1, Y])
                + (wy_prev * u_prev + wy_next * u_next)
                + (w_low * below + w_up * above)
            )
            factor = jnp.broadcast_to(rate[x, pl.ds(y, 1), :], (fields, nz))
            made = factor * chem[1, k, y]
            drop = factor * (lr + chem[0, k, y]) + weights
            if advance:
                source = u_here + inflow_in[x, y] if inflow_in is not None else u_here
            if inflow_out is not None or kept_new is not None:
                half_t = 0.5 * (near + made - drop * u_here)
            if inflow_out is not None:
                inflow_out[x, y] = kept_old[x, y] + (half_t - u_here)
            if kept_new is not None:
                kept_new[x, y] = half_t + source
            if advance:
                right = source + made
                inverse = (mask[0, x] * mask[1, y]) / (1.0 + drop)
                rhs[x, y] = right
                rden[x, y] = inverse
                wx[X, y] = wx_next
                wy[x, y] = wy_next
                wu[x, y] = jnp.where(top, 0.0, w_up)
                va[X, y] = (right + near) * inverse

    def rows_two(i, carry):
        value = jnp.concatenate([u[2 * i + 1 + k, 1 : 1 + ry].reshape(ry * fields, nz) for k in range(2)], axis=1)
        for j, result in enumerate((product(mats[0], value * value), product(mats[1], value))):
            for k in range(2):
                chem[j, k] = result[:, k * nz : (k + 1) * nz].reshape(ry, fields, nz)
        for k in range(2):
            setup(2 * i + k, k)
        return carry

    lax.fori_loop(0, rx // 2, rows_two, 0)
    if not advance:
        return
    if plan.closed:
        for y in range(ry):
            wx[0, y] = c[0, y + 1] + c[1, y + 1]

    old, new = va, vb
    for k in range(1, SWEEPS):
        lead = k * shrink
        count = rx - 2 * lead
        n = 4 if count % 4 == 0 else 2

        def sweep(i, carry, k=k, old=old, new=new, lead=lead, n=n):
            x = lead + n * i
            X = x + 1
            v_here = [old[X + j, k - 1] for j in range(n)]
            v_next = [old[X + j, k] for j in range(n)]
            w_next = [wy[x + j, k - 1] for j in range(n)]
            for y in range(k, ry - k):
                v_prev, v_here, v_next = v_here, v_next, [old[X + j, y + 1] for j in range(n)]
                w_prev, w_next = w_next, [wy[x + j, y] for j in range(n)]
                rows = [old[X - 1, y]] + v_here + [old[X + n, y]]
                faces = [wx[X - 1 + j, y] for j in range(n + 1)]
                for j in range(n):
                    w_up = wu[x + j, y]
                    near = (
                        (faces[j] * rows[j] + faces[j + 1] * rows[j + 2])
                        + (w_prev[j] * v_prev[j] + w_next[j] * v_next[j])
                        + (pltpu.roll(w_up * v_here[j], 1, 1) + w_up * pltpu.roll(v_here[j], nz - 1, 1))
                    )
                    value = (rhs[x + j, y] + near) * rden[x + j, y]
                    if k == SWEEPS - 1:
                        out[x + j - lead, y - k] = value
                    else:
                        new[X + j, y] = value
            return carry

        lax.fori_loop(0, count // n, sweep, 0)
        old, new = new, old


def wave(diagonal, group, plan, fields, nz, strips, inflow, common, kept):
    levels = plan.levels
    going = [p for p in group if diagonal - p < STEPS]
    keepers = [p for p in going if p < levels - 1]
    old = [p for p in group if 0 < diagonal - p and p < levels - 1]
    emits = group[-1] in old
    core = (plan.core_x, plan.core_y, fields, nz)
    sources, where = [], {}
    for p in group:
        arrays, index = strips[p]
        if not (sources and sources[-1] is arrays[-1]):
            sources += list(arrays)
        where[p] = (len(sources) - 3, index)
    n_src = len(sources)
    extra = [] if inflow is None else [inflow]

    def kernel(*refs):
        refs = list(refs)
        take = lambda n: [refs.pop(0) for _ in range(n)]
        src = take(n_src)
        rate_ref, mask_ref, half_ref, loss_ref, mats_ref = take(5)
        old_refs = dict(zip(old, take(len(old))))
        in_refs = take(len(extra))
        state_refs = take(1) if going else []
        new_refs = dict(zip(keepers, take(len(keepers))))
        out_refs = take(1) if emits else []
        held = refs.pop(-1)
        u, c, _, va, vb = refs[:5]
        env = {"scratch": refs, "rate": rate_ref, "mask": mask_ref, "half_d": half_ref, "loss": loss_ref, "mats": mats_ref}
        if plan.closed:
            for x in (0, plan.wide_x - 1):
                for y in range(plan.wide_y):
                    u[x, y] = jnp.zeros((fields, nz), jnp.float32)
                    c[x, y] = half_ref[...]
                for y in range(plan.core_y):
                    va[x, y] = jnp.zeros((fields, nz), jnp.float32)
                    vb[x, y] = jnp.zeros((fields, nz), jnp.float32)
        for p in group:
            node = diagonal - p
            at, index = where[p]
            inflow_in = None if p == 0 or node == STEPS else (in_refs[0] if p == group[0] else held)
            inflow_out = None if p not in old else (out_refs[0] if p == group[-1] else held)
            level_pass(
                [r.at[index] for r in src[at : at + 3]], env, plan, node, inflow_in, inflow_out,
                old_refs.get(p), new_refs.get(p), state_refs[0].at[going.index(p)] if p in going else None,
            )

    vmem = pl.BlockSpec(memory_space=pltpu.VMEM)
    smem = pl.BlockSpec(memory_space=pltpu.SMEM)
    f32 = jnp.float32
    operands = sources + list(common) + [kept[p] for p in old] + extra
    in_specs = [vmem] * n_src + [vmem, smem, vmem, vmem, vmem] + [vmem] * (len(old) + len(extra))
    out_shape = [jax.ShapeDtypeStruct((len(going), plan.sub_x, plan.sub_y, fields, nz), f32)] if going else []
    out_shape += [jax.ShapeDtypeStruct(core, f32)] * (len(keepers) + emits)
    cells = core[0] * core[1] * fields * nz
    wide = (plan.wide_x, plan.wide_y, fields, nz)
    tall = (plan.wide_x,) + core[1:]
    chem = (2, 2) + core[1:]
    shapes = [wide, wide, chem, tall, tall, tall, core, core, core, core, core]
    results = list(pl.pallas_call(
        kernel,
        out_shape=out_shape,
        in_specs=in_specs,
        out_specs=[vmem] * len(out_shape),
        scratch_shapes=[pltpu.VMEM(s, f32) for s in shapes],
        compiler_params=pltpu.CompilerParams(vmem_limit_bytes=56 * 2**20),
        cost_estimate=pl.CostEstimate(flops=150 * cells * len(group), bytes_accessed=8 * cells * len(group), transcendentals=0),
        name="wave%d_%d" % (diagonal, group[0]),
    )(*operands))
    states = results.pop(0) if going else None
    return going, states, dict(zip(keepers, results)), results[-1] if emits else None


def inside_mask(plan):
    part, gx, gy = (lax.axis_index(a) for a in AXES)
    offsets = jnp.arange(max(plan.core_x, plan.core_y))
    cols = (gy * plan.parts_y + part % plan.parts_y) * plan.sub_y + offsets - RIM
    if plan.closed:
        rows = offsets
    else:
        half = part // plan.parts_y
        half = jnp.where(gx % 2 == 0, half, plan.parts_x - 1 - half)
        rows = (gx * plan.parts_x + half) * plan.sub_x + offsets - RIM
    row_ok = (rows >= 0) & (rows < plan.rows * plan.gx)
    col_ok = (cols >= 0) & (cols < plan.cols * plan.gy)
    return jnp.stack([row_ok, col_ok]).astype(jnp.float32)


def matrix_halves(x):
    high = lax.reduce_precision(x, 8, 7)
    return high, x - high


def gather_finals(finals, plan):
    part, gx = lax.axis_index("lvl"), lax.axis_index("gx")
    if not plan.closed:
        parts = lax.all_to_all(jnp.stack(finals), "lvl", 0, 0, tiled=True)
        parts = parts.reshape((plan.parts_x, plan.parts_y) + parts.shape[1:])
        parts = jnp.where(gx % 2 == 0, parts, parts[::-1])
        return jnp.transpose(parts, (0, 2, 1, 3, 4, 5)).reshape((plan.rows, plan.cols) + parts.shape[4:])
    whole = jnp.stack(finals)
    whole = lax.dynamic_slice_in_dim(whole, gx * plan.rows, plan.rows, axis=1)
    n = plan.parts_y
    group = part // n
    column = part % n
    blocks = [None] * n
    got = [lax.dynamic_index_in_dim(whole, part, 0, keepdims=False)]
    for r in range(1, n):
        pairs = [(p, p // n * n + (p % n + r) % n) for p in range(plan.levels)]
        theirs = lax.dynamic_index_in_dim(whole, group * n + (column + r) % n, 0, keepdims=False)
        got.append(lax.ppermute(theirs, "lvl", pairs))
    stack = jnp.stack(got)
    order = jnp.stack([lax.dynamic_index_in_dim(stack, (column - k) % n, 0, keepdims=False) for k in range(n)], axis=1)
    return order.reshape((plan.rows, plan.cols) + order.shape[3:])


def grouped(active):
    return [active[i : i + GROUP] for i in range(0, len(active), GROUP)]


def on_device(initial, rate_factor, diffusivity, loss_rate, quench, formation):
    fields, rows, cols, nz = initial.shape
    plan = Plan(rows, cols)
    levels = plan.levels

    started, rate = columns(jnp.transpose(initial, (1, 2, 0, 3)), rate_factor, plan)
    started = [x[None] for x in started]
    rate = jnp.concatenate(rate, axis=1)
    rate = rate[:, 1:-1] if plan.closed else rate[1:-1, 1:-1]
    mask = inside_mask(plan)

    reacting = (jnp.arange(fields) < REACT).astype(jnp.float32)
    half_d = jnp.broadcast_to(0.5 * diffusivity[:, None], (fields, nz))
    loss = jnp.broadcast_to((reacting * loss_rate)[:, None], (fields, nz))
    eye = jnp.eye(plan.core_y, dtype=jnp.float32)
    mats = []
    for matrix in ((reacting * loss_rate)[:, None] * quench, reacting[:, None] * formation):
        mats.append(jnp.concatenate([jnp.kron(eye, m) for m in matrix_halves(matrix)], axis=0))
    common = [rate, mask, half_d, loss, jnp.stack(mats).astype(jnp.bfloat16)]

    strips, kept, finals = {}, {}, {}
    for diagonal in range(levels + STEPS - 1):
        if diagonal < levels:
            strips[diagonal] = (started, 0)
        active = [p for p in sorted(strips) if diagonal - p < STEPS + (p < levels - 1)]
        inflow, fresh, held = None, {}, {}
        for group in grouped(active):
            going, states, keeps, inflow = wave(diagonal, group, plan, fields, nz, strips, inflow, common, kept)
            held.update(keeps)
            for i, p in enumerate(going):
                if diagonal - p + 1 == STEPS:
                    finals[p] = states[i]
            if going and not (diagonal - going[0] + 1 == STEPS and going[0] == levels - 1):
                arrays = exchange(states, plan)
                fresh.update({p: (arrays, i) for i, p in enumerate(going)})
        strips, kept = fresh, held
    tile = gather_finals([finals[p] for p in range(levels)], plan)
    return jnp.transpose(tile, (2, 0, 1, 3))[None]


def solution(mesh):
    in_specs = (P(None, "gx", "gy", None), P("gx", "gy", None), P(), P(), P(), P())
    out_specs = P("lvl", None, "gx", "gy", None)
    return jax.shard_map(
        on_device, mesh=mesh, in_specs=in_specs, out_specs=out_specs, check_vma=False
    )
```

time: 336 us -> 298 us (0.89)
  starting transfers between devices: 145 us -> 120 us
  Pallas kernels: 105 us -> 126 us
  blocking collectives: 20.8 us -> 0 us
  waiting for transfers between devices: 46.4 us -> 25.8 us
  local copies, waits for them, and re-layouts: 9.2 us -> 16.3 us
  other arithmetic: 3.69 us -> 7.34 us
    ppermute x32 -> x15, starting transfers between devices: 145 us -> 120 us  [the longest x6 98.2 us: exchange(): before = lax.ppermute(states[:, :, -SWEEPS:], AXES, plan.shifts(0, 1))]
    pallas_call x7, Pallas kernels: 105 us -> 126 us  [wave(): pl.pallas_call(kernel, out_shape=out_shape, in_specs=in_specs, out_specs=...]
    all_to_all x1 -> x0, blocking collectives: 20.8 us -> none  [on_device(): lax.all_to_all(jnp.stack([finals[p] for p in range(levels)]), 'lvl', 0, 0...]
    ppermute x32 -> x15, waiting for transfers between devices: 46.4 us -> 25.8 us  [the longest x1 10.5 us: columns(): lax.ppermute(pack(own, rate), 'gx', [(0, 1), (1, 0)])]
    unnamed x39 -> x37, local copies, waits for them, and re-layouts: 5.57 us -> 8.11 us
  transfers between devices with their start and end apart: 32 -> 15, of which waited for: 22 -> 12; matrix products, arithmetic and copies ran while one was open for 2% -> 2% of each run, Pallas kernels for 0% -> 0%
where the time goes in v2:
time: 298 us; the launch traced here: 296 us
  Pallas kernels  126 us (42%)
  starting transfers between devices  120 us (40%)
  waiting for transfers between devices  25.8 us (9%)
  local copies, waits for them, and re-layouts  16.3 us (5%)
  other arithmetic  7.34 us (2%)
    pallas_call x7, Pallas kernels, wave(): pl.pallas_call(kernel, out_shape=out_shape, in_specs=in_specs, out_specs=...  126 us
    ppermute x6, starting transfers between devices, exchange(): before = lax.ppermute(states[:, :, -SWEEPS:], AXES, plan.shifts(0, 1))  98.2 us
    ppermute x1, starting transfers between devices, gather_finals(): got.append(lax.ppermute(theirs, 'lvl', pairs))  11.7 us
    ppermute x1, waiting for transfers between devices, columns(): lax.ppermute(pack(own, rate), 'gx', [(0, 1), (1, 0)])  10.5 us
    ppermute x6, waiting for transfers between devices, exchange(): before = lax.ppermute(states[:, :, -SWEEPS:], AXES, plan.shifts(0, 1))  9.99 us
    unnamed x37, local copies, waits for them, and re-layouts  8.11 us
    ppermute x6, starting transfers between devices, exchange(): after = lax.ppermute(states[:, :, :SWEEPS], AXES, plan.shifts(0, -1))  7.82 us
  transfers between devices with their start and end apart: 15, of which 12 were waited for; matrix products, arithmetic and copies ran while one was open for 2% of the time, Pallas kernels for 0%

profile of v2, /device:TPU:2, one launch (start us, length us, event | category | flops | bytes accessed | tf_op | source)
XLA Modules:
  0.0 295.9 jit_solution(406124064395210667)
XLA Ops:
  0.0 1.4 copy.14
  1.4 1.6 pad_maximum_fusion.1
  3.0 1.5 collective-permute-start
  7.2 10.5 %collective-permute-done = f32[1088,128]{1,0:T(8,128)} collective-permute-done((f32[1088,128]{1,0:T(8,128)}, f32[1088,128]{1,0:T(8,128)}, u32[]{:S(2)}, u32[]{:S(2)}) %collective-permute-start) | collective-permute-done | bytes 557088 | tf_op jit(solution)/shard_map/ppermute | solution.py:82
  17.7 0.8 slice_bitcast_fusion
  18.5 1.1 slice.56
  19.8 0.7 collective-permute-start.1
  21.1 0.8 pad_maximum_fusion.4.refs_7_.refs_10_
  22.0 1.3 select_bitcast_fusion
  25.3 8.1 %wave0_0.1 = (f32[1,16,4,16,128]{4,3,2,1,0:T(8,128)}, f32[16,10,16,128]{3,2,1,0:T(8,128)}) custom-call(f32[1,16,4,16,128]{4,3,2,1,0:T(8,128)} %get-tuple-element.44.refs_0_.refs_3_, f32[1,16,4,16,128]{4,3,2,1,0:T(8,128)} %get-tuple-element.45.refs_1_.refs_4_, f32[1,16,4,16,128]{4,3,2,1,0:T(8,128)} %get-tuple-element.43.refs_2_.refs_5_, ...), custom_call_target="tpu_custom_call" | custom-call | flops 49152000 | bytes 2621440 | tf_op jit(solution)/shard_map/wave0_0/pallas_call | solution.py:315
  33.4 1.3 collective-permute-start.3
  34.6 11.2 %collective-permute-start.2 = (f32[1,16,4,16,128]{4,3,2,1,0:T(8,128)}, f32[1,16,4,16,128]{4,3,2,1,0:T(8,128)S(1)}, u32[]{:S(2)}, u32[]{:S(2)}) collective-permute-start(f32[1,16,4,16,128]{4,3,2,1,0:T(8,128)} %get-tuple-element.23.refs_1_), channel_id=1, source_target_pairs={{0,8},{8,1},{1,9},{9,2},{2,10},{10,3},{3,11},{16,24},{24,17},{17,2... | collective-permute-start | bytes 1572872 | tf_op jit(solution)/shard_map/ppermute | solution.py:115
  45.9 1.7 collective-permute-done.2.refs_0_
  47.6 0.8 copy-done.12
  48.4 14.8 %wave1_0.1 = (f32[2,16,4,16,128]{4,3,2,1,0:T(8,128)}, f32[16,10,16,128]{3,2,1,0:T(8,128)}, f32[16,10,16,128]{3,2,1,0:T(8,128)}) custom-call(f32[1,16,4,16,128]{4,3,2,1,0:T(8,128)} %copy-done.12, f32[1,16,4,16,128]{4,3,2,1,0:T(8,128)} %get-tuple-element.23.refs_1_, f32[1,16,4,16,128]{4,3,2,1,0:T(8,128)} %copy-done.11, ...), custom_call_target="tpu_custom_call" | custom-call | flops 98304000 | bytes 5242880 | tf_op jit(solution)/shard_map/wave1_0/pallas_call | solution.py:315
  63.1 1.3 collective-permute-start.5
  64.4 9.0 %collective-permute-start.4 = (f32[2,16,4,16,128]{4,3,2,1,0:T(8,128)}, f32[2,16,4,16,128]{4,3,2,1,0:T(8,128)S(1)}, u32[]{:S(2)}, u32[]{:S(2)}) collective-permute-start(f32[2,16,4,16,128]{4,3,2,1,0:T(8,128)} %get-tuple-element.25.refs_1_), channel_id=1, source_target_pairs={{0,8},{8,1},{1,9},{9,2},{2,10},{10,3},{3,11},{16,24},{24,17},{17,2... | collective-permute-start | bytes 3145736 | tf_op jit(solution)/shard_map/ppermute | solution.py:115
  73.8 2.0 collective-permute-done.4.refs_0_
  75.9 1.0 copy-done.8
  76.9 21.7 %wave2_0.1 = (f32[3,16,4,16,128]{4,3,2,1,0:T(8,128)}, f32[16,10,16,128]{3,2,1,0:T(8,128)}, f32[16,10,16,128]{3,2,1,0:T(8,128)}, f32[16,10,16,128]{3,2,1,0:T(8,128)}) custom-call(f32[2,16,4,16,128]{4,3,2,1,0:T(8,128)} %copy-done.8, f32[2,16,4,16,128]{4,3,2,1,0:T(8,128)} %get-tuple-element.25.refs_1_, f32[2,16,4,16,128]{4,3,2,1,0:T(8,128)} %copy-done.7, ...), custom_call_target="tpu_custom_call" | custom-call | flops 147456000 | bytes 7864320 | tf_op jit(solution)/shard_map/wave2_0/pallas_call | solution.py:315
  98.6 1.3 collective-permute-start.7
  99.8 14.7 %collective-permute-start.6 = (f32[3,16,4,16,128]{4,3,2,1,0:T(8,128)}, f32[3,16,4,16,128]{4,3,2,1,0:T(8,128)S(1)}, u32[]{:S(2)}, u32[]{:S(2)}) collective-permute-start(f32[3,16,4,16,128]{4,3,2,1,0:T(8,128)} %get-tuple-element.28.refs_1_), channel_id=1, source_target_pairs={{0,8},{8,1},{1,9},{9,2},{2,10},{10,3},{3,11},{16,24},{24,17},{17,2... | collective-permute-start | bytes 4718600 | tf_op jit(solution)/shard_map/ppermute | solution.py:115
  114.6 0.9 collective-permute-done.7.refs_2_
  115.5 2.0 collective-permute-done.6.refs_0_
  117.5 1.2 copy-done.6
  118.7 27.9 %wave3_0.1 = (f32[4,16,4,16,128]{4,3,2,1,0:T(8,128)}, f32[16,10,16,128]{3,2,1,0:T(8,128)}, f32[16,10,16,128]{3,2,1,0:T(8,128)}, f32[16,10,16,128]{3,2,1,0:T(8,128)}) custom-call(f32[3,16,4,16,128]{4,3,2,1,0:T(8,128)} %copy-done.6, f32[3,16,4,16,128]{4,3,2,1,0:T(8,128)} %get-tuple-element.28.refs_1_, f32[3,16,4,16,128]{4,3,2,1,0:T(8,128)} %copy-done.5, ...), custom_call_target="tpu_custom_call" | custom-call | flops 196608000 | bytes 10485760 | tf_op jit(solution)/shard_map/wave3_0/pallas_call | solution.py:315
  146.6 1.3 collective-permute-start.9
  147.9 19.5 %collective-permute-start.8 = (f32[4,16,4,16,128]{4,3,2,1,0:T(8,128)}, f32[4,16,4,16,128]{4,3,2,1,0:T(8,128)S(1)}, u32[]{:S(2)}, u32[]{:S(2)}) collective-permute-start(f32[4,16,4,16,128]{4,3,2,1,0:T(8,128)} %get-tuple-element.32.refs_1_), channel_id=1, source_target_pairs={{0,8},{8,1},{1,9},{9,2},{2,10},{10,3},{3,11},{16,24},{24,17},{17,2... | collective-permute-start | bytes 6291464 | tf_op jit(solution)/shard_map/ppermute | solution.py:115
  167.4 1.8 collective-permute-done.9.refs_2_
  169.2 2.0 collective-permute-done.8.refs_0_
  171.2 1.3 copy-done.2
  172.6 24.6 %wave4_0.1 = (f32[3,16,4,16,128]{4,3,2,1,0:T(8,128)}, f32[16,10,16,128]{3,2,1,0:T(8,128)}, f32[16,10,16,128]{3,2,1,0:T(8,128)}) custom-call(f32[4,16,4,16,128]{4,3,2,1,0:T(8,128)} %copy-done.2, f32[4,16,4,16,128]{4,3,2,1,0:T(8,128)} %get-tuple-element.32.refs_1_, f32[4,16,4,16,128]{4,3,2,1,0:T(8,128)} %copy-done.1, ...), custom_call_target="tpu_custom_call" | custom-call | flops 196608000 | bytes 10485760 | tf_op jit(solution)/shard_map/wave4_0/pallas_call | solution.py:315
  197.1 1.3 collective-permute-start.11
  198.4 24.3 %collective-permute-start.10 = (f32[3,16,4,16,128]{4,3,2,1,0:T(8,128)}, f32[3,16,4,16,128]{4,3,2,1,0:T(8,128)S(1)}, u32[]{:S(2)}, u32[]{:S(2)}) collective-permute-start(f32[3,16,4,16,128]{4,3,2,1,0:T(8,128)} %get-tuple-element.36.refs_1_), channel_id=1, source_target_pairs={{0,8},{8,1},{1,9},{9,2},{2,10},{10,3},{3,11},{16,24},{24,17},{17,2... | collective-permute-start | bytes 4718600 | tf_op jit(solution)/shard_map/ppermute | solution.py:115
  222.8 1.1 collective-permute-done.11.refs_2_
  223.9 2.0 collective-permute-done.10.refs_0_
  225.9 1.1 copy-done.4
  227.1 17.9 %wave5_1.1 = (f32[2,16,4,16,128]{4,3,2,1,0:T(8,128)}, f32[16,10,16,128]{3,2,1,0:T(8,128)}) custom-call(f32[3,16,4,16,128]{4,3,2,1,0:T(8,128)} %copy-done.4, f32[3,16,4,16,128]{4,3,2,1,0:T(8,128)} %get-tuple-element.36.refs_1_, f32[3,16,4,16,128]{4,3,2,1,0:T(8,128)} %copy-done.3, f32[16,10,128]{2,1,0:T(8,128)} %pad_maximum_fusion.5.refs_3_.refs_6_, ...), custom_call_target="tpu_custom_call" | custom-call | flops 147456000 | bytes 7864320 | tf_op jit(solution)/shard_map/wave5_1/pallas_call | solution.py:315
  245.0 1.4 collective-permute-start.13
  246.4 19.4 %collective-permute-start.12 = (f32[2,16,4,16,128]{4,3,2,1,0:T(8,128)}, f32[2,16,4,16,128]{4,3,2,1,0:T(8,128)S(1)}, u32[]{:S(2)}, u32[]{:S(2)}) collective-permute-start(f32[2,16,4,16,128]{4,3,2,1,0:T(8,128)} %get-tuple-element.39.refs_1_), channel_id=1, source_target_pairs={{0,8},{8,1},{1,9},{9,2},{2,10},{10,3},{3,11},{16,24},{24,17},{17,2... | collective-permute-start | bytes 3145736 | tf_op jit(solution)/shard_map/ppermute | solution.py:115
  265.9 1.1 slice.53
  266.9 1.1 slice.54
  268.2 0.9 copy-done.9
  269.5 11.2 %wave6_2.1 = f32[1,16,4,16,128]{4,3,2,1,0:T(8,128)} custom-call(f32[2,16,4,16,128]{4,3,2,1,0:T(8,128)} %copy-done.10, f32[2,16,4,16,128]{4,3,2,1,0:T(8,128)} %get-tuple-element.39.refs_1_, f32[2,16,4,16,128]{4,3,2,1,0:T(8,128)} %copy-done.9, f32[16,10,128]{2,1,0:T(8,128)} %pad_maximum_fusion.5.refs_3_.refs_6_, f32[2,16]{1,0:T(2,128)} %add_convert_fusion.refs_4_.refs_7_, ...), custom_call_target="tpu_custom_call" | custom-call | flops 98304000 | bytes 5242880 | tf_op jit(solution)/shard_map/wave6_2/pallas_call | solution.py:315
  280.6 1.2 pad_maximum_fusion
  281.9 11.7 %collective-permute-start.14 = (f32[8,4,16,128]{3,2,1,0:T(8,128)S(1)}, f32[8,4,16,128]{3,2,1,0:T(8,128)S(1)}, u32[]{:S(2)}, u32[]{:S(2)}) collective-permute-start(f32[8,4,16,128]{3,2,1,0:T(8,128)S(1)} %get-tuple-element.41), channel_id=1, source_target_pairs={{0,8},{8,0},{16,24},{24,16},{1,9},{9,1},{17,25},{25,17},{2,10},{10... | collective-permute-start | bytes 786440 | tf_op jit(solution)/shard_map/ppermute | solution.py:366
  293.6 1.2 collective-permute-done.14
  295.0 1.0 copy.11
  (65 shorter events, 6.7 us)
Async XLA Ops:
  0.0 4.5 %copy-start.16 = (f32[16]{0:T(128)S(1)}, f32[16]{0:T(128)}, u32[]{:S(2)}) copy-start(f32[16]{0:T(128)} %param.9) | copy-start | bytes 196
  0.0 4.5 %copy-start.14 = (f32[16,16]{1,0:T(8,128)S(1)}, f32[16,16]{1,0:T(8,128)}, u32[]{:S(2)}) copy-start(f32[16,16]{1,0:T(8,128)} %param.11) | copy-start | bytes 3076
  0.0 4.5 %copy-start.15 = (f32[16,16]{1,0:T(8,128)S(1)}, f32[16,16]{1,0:T(8,128)}, u32[]{:S(2)}) copy-start(f32[16,16]{1,0:T(8,128)} %param.10) | copy-start | bytes 3076
  3.0 14.7 %collective-permute-start = (f32[1088,128]{1,0:T(8,128)}, f32[1088,128]{1,0:T(8,128)}, u32[]{:S(2)}, u32[]{:S(2)}) collective-permute-start(f32[1088,128]{1,0:T(8,128)} %pad_maximum_fusion.1), channel_id=1, source_target_pairs={{0,4},{4,0},{1,5},{5,1},{2,6},{6,2},{3,7},{7,3},{8,12},{12,8},{9,1... | collective-permute-start | bytes 1671176 | tf_op jit(solution)/shard_map/ppermute | solution.py:82
  5.8 12.6 %copy-start.13 = (f32[8,8,128]{2,1,0:T(8,128)S(1)}, f32[8,8,128]{2,1,0:T(8,128)}, u32[]{:S(2)}) copy-start(f32[8,8,128]{2,1,0:T(8,128)} %param.7) | copy-start | bytes 98308
  19.7 2.2 copy-start.17
  19.8 2.1 collective-permute-start.1
  33.4 12.5 %collective-permute-start.3 = (f32[1,16,4,16,128]{4,3,2,1,0:T(8,128)}, f32[1,16,4,16,128]{4,3,2,1,0:T(8,128)S(1)}, u32[]{:S(2)}, u32[]{:S(2)}) collective-permute-start(f32[1,16,4,16,128]{4,3,2,1,0:T(8,128)} %get-tuple-element.23.refs_1_), channel_id=1, source_target_pairs={{8,0},{1,8},{9,1},{2,9},{10,2},{3,10},{11,3},{24,16},{17,24},{25,1... | collective-permute-start | bytes 1572872 | tf_op jit(solution)/shard_map/ppermute | solution.py:116
  34.6 12.9 %collective-permute-start.2 = (f32[1,16,4,16,128]{4,3,2,1,0:T(8,128)}, f32[1,16,4,16,128]{4,3,2,1,0:T(8,128)S(1)}, u32[]{:S(2)}, u32[]{:S(2)}) collective-permute-start(f32[1,16,4,16,128]{4,3,2,1,0:T(8,128)} %get-tuple-element.23.refs_1_), channel_id=1, source_target_pairs={{0,8},{8,1},{1,9},{9,2},{2,10},{10,3},{3,11},{16,24},{24,17},{17,2... | collective-permute-start | bytes 1572872 | tf_op jit(solution)/shard_map/ppermute | solution.py:115
  45.9 1.7 copy-start.11
  47.6 0.8 copy-start.12
  63.1 10.7 %collective-permute-start.5 = (f32[2,16,4,16,128]{4,3,2,1,0:T(8,128)}, f32[2,16,4,16,128]{4,3,2,1,0:T(8,128)S(1)}, u32[]{:S(2)}, u32[]{:S(2)}) collective-permute-start(f32[2,16,4,16,128]{4,3,2,1,0:T(8,128)} %get-tuple-element.25.refs_1_), channel_id=1, source_target_pairs={{8,0},{1,8},{9,1},{2,9},{10,2},{3,10},{11,3},{24,16},{17,24},{25,1... | collective-permute-start | bytes 3145736 | tf_op jit(solution)/shard_map/ppermute | solution.py:116
  64.4 11.4 %collective-permute-start.4 = (f32[2,16,4,16,128]{4,3,2,1,0:T(8,128)}, f32[2,16,4,16,128]{4,3,2,1,0:T(8,128)S(1)}, u32[]{:S(2)}, u32[]{:S(2)}) collective-permute-start(f32[2,16,4,16,128]{4,3,2,1,0:T(8,128)} %get-tuple-element.25.refs_1_), channel_id=1, source_target_pairs={{0,8},{8,1},{1,9},{9,2},{2,10},{10,3},{3,11},{16,24},{24,17},{17,2... | collective-permute-start | bytes 3145736 | tf_op jit(solution)/shard_map/ppermute | solution.py:115
  73.8 2.1 copy-start.7
  75.9 1.0 copy-start.8
  98.6 16.9 %collective-permute-start.7 = (f32[3,16,4,16,128]{4,3,2,1,0:T(8,128)}, f32[3,16,4,16,128]{4,3,2,1,0:T(8,128)S(1)}, u32[]{:S(2)}, u32[]{:S(2)}) collective-permute-start(f32[3,16,4,16,128]{4,3,2,1,0:T(8,128)} %get-tuple-element.28.refs_1_), channel_id=1, source_target_pairs={{8,0},{1,8},{9,1},{2,9},{10,2},{3,10},{11,3},{24,16},{17,24},{25,1... | collective-permute-start | bytes 4718600 | tf_op jit(solution)/shard_map/ppermute | solution.py:116
  99.8 17.7 %collective-permute-start.6 = (f32[3,16,4,16,128]{4,3,2,1,0:T(8,128)}, f32[3,16,4,16,128]{4,3,2,1,0:T(8,128)S(1)}, u32[]{:S(2)}, u32[]{:S(2)}) collective-permute-start(f32[3,16,4,16,128]{4,3,2,1,0:T(8,128)} %get-tuple-element.28.refs_1_), channel_id=1, source_target_pairs={{0,8},{8,1},{1,9},{9,2},{2,10},{10,3},{3,11},{16,24},{24,17},{17,2... | collective-permute-start | bytes 4718600 | tf_op jit(solution)/shard_map/ppermute | solution.py:115
  115.5 2.1 copy-start.5
  117.5 1.2 copy-start.6
  146.6 22.5 %collective-permute-start.9 = (f32[4,16,4,16,128]{4,3,2,1,0:T(8,128)}, f32[4,16,4,16,128]{4,3,2,1,0:T(8,128)S(1)}, u32[]{:S(2)}, u32[]{:S(2)}) collective-permute-start(f32[4,16,4,16,128]{4,3,2,1,0:T(8,128)} %get-tuple-element.32.refs_1_), channel_id=1, source_target_pairs={{8,0},{1,8},{9,1},{2,9},{10,2},{3,10},{11,3},{24,16},{17,24},{25,1... | collective-permute-start | bytes 6291464 | tf_op jit(solution)/shard_map/ppermute | solution.py:116
  147.9 23.3 %collective-permute-start.8 = (f32[4,16,4,16,128]{4,3,2,1,0:T(8,128)}, f32[4,16,4,16,128]{4,3,2,1,0:T(8,128)S(1)}, u32[]{:S(2)}, u32[]{:S(2)}) collective-permute-start(f32[4,16,4,16,128]{4,3,2,1,0:T(8,128)} %get-tuple-element.32.refs_1_), channel_id=1, source_target_pairs={{0,8},{8,1},{1,9},{9,2},{2,10},{10,3},{3,11},{16,24},{24,17},{17,2... | collective-permute-start | bytes 6291464 | tf_op jit(solution)/shard_map/ppermute | solution.py:115
  169.2 2.1 copy-start.1
  171.2 1.3 copy-start.2
  197.1 26.7 %collective-permute-start.11 = (f32[3,16,4,16,128]{4,3,2,1,0:T(8,128)}, f32[3,16,4,16,128]{4,3,2,1,0:T(8,128)S(1)}, u32[]{:S(2)}, u32[]{:S(2)}) collective-permute-start(f32[3,16,4,16,128]{4,3,2,1,0:T(8,128)} %get-tuple-element.36.refs_1_), channel_id=1, source_target_pairs={{8,0},{1,8},{9,1},{2,9},{10,2},{3,10},{11,3},{24,16},{17,24},{25,1... | collective-permute-start | bytes 4718600 | tf_op jit(solution)/shard_map/ppermute | solution.py:116
  198.4 27.5 %collective-permute-start.10 = (f32[3,16,4,16,128]{4,3,2,1,0:T(8,128)}, f32[3,16,4,16,128]{4,3,2,1,0:T(8,128)S(1)}, u32[]{:S(2)}, u32[]{:S(2)}) collective-permute-start(f32[3,16,4,16,128]{4,3,2,1,0:T(8,128)} %get-tuple-element.36.refs_1_), channel_id=1, source_target_pairs={{0,8},{8,1},{1,9},{9,2},{2,10},{10,3},{3,11},{16,24},{24,17},{17,2... | collective-permute-start | bytes 4718600 | tf_op jit(solution)/shard_map/ppermute | solution.py:115
  223.9 2.1 copy-start.3
  225.9 1.2 copy-start.4
  245.0 23.1 %copy-start = (f32[2,16,4,16,128]{4,3,2,1,0:T(8,128)S(1)}, f32[2,16,4,16,128]{4,3,2,1,0:T(8,128)}, u32[]{:S(2)}) copy-start(f32[2,16,4,16,128]{4,3,2,1,0:T(8,128)} %get-tuple-element.39.refs_1_) | copy-start | bytes 3145732
  245.0 23.1 %collective-permute-start.13 = (f32[2,16,4,16,128]{4,3,2,1,0:T(8,128)}, f32[2,16,4,16,128]{4,3,2,1,0:T(8,128)S(1)}, u32[]{:S(2)}, u32[]{:S(2)}) collective-permute-start(f32[2,16,4,16,128]{4,3,2,1,0:T(8,128)} %get-tuple-element.39.refs_1_), channel_id=1, source_target_pairs={{8,0},{1,8},{9,1},{2,9},{10,2},{3,10},{11,3},{24,16},{17,24},{25,1... | collective-permute-start | bytes 3145736 | tf_op jit(solution)/shard_map/ppermute | solution.py:116
  246.4 21.8 %collective-permute-start.12 = (f32[2,16,4,16,128]{4,3,2,1,0:T(8,128)}, f32[2,16,4,16,128]{4,3,2,1,0:T(8,128)S(1)}, u32[]{:S(2)}, u32[]{:S(2)}) collective-permute-start(f32[2,16,4,16,128]{4,3,2,1,0:T(8,128)} %get-tuple-element.39.refs_1_), channel_id=1, source_target_pairs={{0,8},{8,1},{1,9},{9,2},{2,10},{10,3},{3,11},{16,24},{24,17},{17,2... | collective-permute-start | bytes 3145736 | tf_op jit(solution)/shard_map/ppermute | solution.py:115
  268.1 1.0 copy-start.9
  268.2 1.3 copy-start.10
  281.9 12.9 %collective-permute-start.14 = (f32[8,4,16,128]{3,2,1,0:T(8,128)S(1)}, f32[8,4,16,128]{3,2,1,0:T(8,128)S(1)}, u32[]{:S(2)}, u32[]{:S(2)}) collective-permute-start(f32[8,4,16,128]{3,2,1,0:T(8,128)S(1)} %get-tuple-element.41), channel_id=1, source_target_pairs={{0,8},{8,0},{16,24},{24,16},{1,9},{9,1},{17,25},{25,17},{2,10},{10... | collective-permute-start | bytes 786440 | tf_op jit(solution)/shard_map/ppermute | solution.py:366

commit v3 on v2

--- a/solution.py
+++ b/solution.py
@@ -11,7 +11,7 @@
 STEPS = 4
 SWEEPS = 4
 RIM = SWEEPS - 1
-GROUP = 4
+GROUP = 2
 AXES = ("lvl", "gx", "gy")
 
 
@@ -38,6 +38,7 @@
         assert min(self.sub_x, self.sub_y) >= SWEEPS
         self.wide_y = self.sub_y + 2 * SWEEPS
         self.core_x, self.core_y = self.wide_x - 2, self.wide_y - 2
+        self.paired = self.closed and self.parts_y == 2 and self.sub_y == SWEEPS
 
     def spot(self, part, gx, gy):
         at_y = gy * self.parts_y + part % self.parts_y
@@ -58,6 +59,12 @@
     def column(self, device):
         return device // (self.gx * self.gy) % self.parts_y
 
+    def swaps(self, outside):
+        return sorted(
+            [(a, b) for a, b in self.shifts(0, 1) if self.column(a) == (1 if outside else 0)]
+            + [(a, b) for a, b in self.shifts(0, -1) if self.column(a) == (0 if outside else 1)]
+        )
+
     def shifts(self, dx, dy):
         found = self.devices()
         there = lambda s: (s[0] + dx, s[1], s[2] + dy)
@@ -68,10 +75,7 @@
     half = lax.axis_index("lvl") % plan.parts_y
     gx = lax.axis_index("gx")
     sub, nz = plan.sub_y, own.shape[-1]
-    both = jnp.concatenate([own, rate[:, :, None, :]], axis=2) if not plan.closed else None
     if plan.closed:
-        cells, planes = own.shape[0] * own.shape[1], own.shape[2]
-
         def pack(x, r):
             return jnp.concatenate([x.reshape(-1, nz), r.reshape(-1, nz)], axis=0)
 
@@ -84,30 +88,27 @@
                 jnp.where(gx == 0, jnp.concatenate([a, b], axis=0), jnp.concatenate([b, a], axis=0))
                 for a, b in zip((own, rate), theirs)
             )
-        if plan.parts_y == 2:
-            pairs = sorted(
-                [(a, b) for a, b in plan.shifts(0, 1) if plan.column(a) == 1]
-                + [(a, b) for a, b in plan.shifts(0, -1) if plan.column(a) == 0]
-            )
-            outer = [jnp.where(half == 1, x[:, -SWEEPS:], x[:, :SWEEPS]) for x in (own, rate)]
-            come = unpack(lax.ppermute(pack(*outer), AXES, pairs), *outer)
-            wide = []
-            for x, o in zip((own, rate), come):
-                x_before = jnp.where(half == 0, o, x[:, sub - SWEEPS : sub])
-                x_after = jnp.where(half == 0, x[:, sub : sub + SWEEPS], o)
-                wide.append((x_before, jnp.where(half == 0, x[:, :sub], x[:, sub:]), x_after))
-            return wide
+        if plan.paired:
+            low, high = ([x[:, :sub] for x in (own, rate)], [x[:, sub:] for x in (own, rate)])
+            mine = [jnp.where(half == 0, a, b) for a, b in zip(low, high)]
+            inner = [jnp.where(half == 0, b, a) for a, b in zip(low, high)]
+            outer = unpack(lax.ppermute(pack(*mine), AXES, plan.swaps(True)), *mine)
+            rates = jnp.where(half == 0, jnp.concatenate([outer[1], rate], axis=1), jnp.concatenate([rate, outer[1]], axis=1))
+            return (inner[0], mine[0], outer[0]), rates
         both = jnp.concatenate([own, rate[:, :, None, :]], axis=2)
     else:
+        both = jnp.concatenate([own, rate[:, :, None, :]], axis=2)
         at = lax.axis_index("lvl") // plan.parts_y
         at = jnp.where(gx % 2 == 0, at, plan.parts_x - 1 - at) * plan.sub_x
         both = lax.dynamic_slice_in_dim(both, at, plan.sub_x, axis=0)
     both = lax.dynamic_slice_in_dim(both, half * sub, sub, axis=1)
     strips = exchange(both[None], plan)
-    return [[x[0, :, :, :-1] for x in strips], [x[0, :, :, -1] for x in strips]]
+    return [x[0, :, :, :-1] for x in strips], jnp.concatenate([x[0, :, :, -1] for x in strips], axis=1)
 
 
 def exchange(states, plan):
+    if plan.paired:
+        return lax.ppermute(states, AXES, plan.swaps(False)), states, lax.ppermute(states, AXES, plan.swaps(True))
     if not plan.closed:
         before = lax.ppermute(states[:, -SWEEPS:], AXES, plan.shifts(1, 0))
         after = lax.ppermute(states[:, :SWEEPS], AXES, plan.shifts(-1, 0))
@@ -130,26 +131,31 @@
     return first[:n] + (first[n:] + dot(matrix[:n], low))
 
 
-def level_pass(strips, env, plan, node, inflow_in, inflow_out, kept_old, kept_new, out):
+def level_pass(strips, env, plan, node, inflow_in, inflow_out, kept_old, kept_new, out, fresh):
     u, c, chem, va, vb, wx, wy, wu, rhs, rden = env["scratch"]
+    first = va
+    if fresh is not None:
+        first, wx, wy, wu, rhs, rden = fresh[:6]
     rate, mask, half_d, loss, mats = env["rate"], env["mask"], env["half_d"], env["loss"], env["mats"]
     fields, nz = u.shape[2:]
     rx, ry = plan.core_x, plan.core_y
     hd = half_d[...]
     base = 1 if plan.closed else 0
-    shrink = 0 if plan.closed else 1
 
     def conduct(value):
         return hd + hd * (value * value)
 
+    starts = [0, strips[0].shape[1], strips[0].shape[1] + strips[1].shape[1]]
+    if plan.paired:
+        side = env["side"][0]
+        starts[0], starts[2] = (1 - side) * starts[2], side * starts[2]
+
     def widen(x, carry):
-        at = 0
-        for strip in strips:
+        for at, strip in zip(starts, strips):
             for y in range(strip.shape[1]):
                 value = strip[x, y]
                 u[x + base, at + y] = value
                 c[x + base, at + y] = conduct(value)
-            at += strip.shape[1]
         return carry
 
     lax.fori_loop(0, strips[0].shape[0], widen, 0)
@@ -200,7 +206,7 @@
                 wx[X, y] = wx_next
                 wy[x, y] = wy_next
                 wu[x, y] = jnp.where(top, 0.0, w_up)
-                va[X, y] = (right + near) * inverse
+                first[X, y] = (right + near) * inverse
 
     def rows_two(i, carry):
         value = jnp.concatenate([u[2 * i + 1 + k, 1 : 1 + ry].reshape(ry * fields, nz) for k in range(2)], axis=1)
@@ -217,8 +223,31 @@
     if plan.closed:
         for y in range(ry):
             wx[0, y] = c[0, y + 1] + c[1, y + 1]
-
-    old, new = va, vb
+    sweeps(plan, first, va, vb, wx, wy, wu, rhs, rden, out)
+
+
+def first_pass(env, plan, inflow, kept_new, out, fresh):
+    va, vb, rhs = env["scratch"][3], env["scratch"][4], env["scratch"][8]
+    first, wx, wy, wu, right, rden, kept = fresh
+
+    def add(x, carry):
+        for y in range(plan.core_y):
+            more = inflow[x, y]
+            rhs[x, y] = right[x, y] + more
+            va[x + 1, y] = first[x + 1, y] + more * rden[x, y]
+            if kept_new is not None:
+                kept_new[x, y] = kept[x, y] + more
+        return carry
+
+    lax.fori_loop(0, plan.core_x, add, 0)
+    sweeps(plan, va, va, vb, wx, wy, wu, rhs, rden, out)
+
+
+def sweeps(plan, first, va, vb, wx, wy, wu, rhs, rden, out):
+    nz = vb.shape[3]
+    rx, ry = plan.core_x, plan.core_y
+    shrink = 0 if plan.closed else 1
+    old, new, spare = first, vb, va
     for k in range(1, SWEEPS):
         lead = k * shrink
         count = rx - 2 * lead
@@ -250,10 +279,10 @@
             return carry
 
         lax.fori_loop(0, count // n, sweep, 0)
-        old, new = new, old
-
-
-def wave(diagonal, group, plan, fields, nz, strips, inflow, common, kept):
+        old, new, spare = new, spare, new
+
+
+def wave(diagonal, group, plan, fields, nz, strips, inflow, common, kept, cache):
     levels = plan.levels
     going = [p for p in group if diagonal - p < STEPS]
     keepers = [p for p in going if p < levels - 1]
@@ -262,26 +291,32 @@
     core = (plan.core_x, plan.core_y, fields, nz)
     sources, where = [], {}
     for p in group:
+        if p == diagonal and p > 0:
+            continue
         arrays, index = strips[p]
         if not (sources and sources[-1] is arrays[-1]):
             sources += list(arrays)
         where[p] = (len(sources) - 3, index)
     n_src = len(sources)
     extra = [] if inflow is None else [inflow]
+    makes = diagonal == 0
+    shared = list(cache) if diagonal > 0 and diagonal in group else []
 
     def kernel(*refs):
         refs = list(refs)
         take = lambda n: [refs.pop(0) for _ in range(n)]
         src = take(n_src)
-        rate_ref, mask_ref, half_ref, loss_ref, mats_ref = take(5)
+        rate_ref, mask_ref, side_ref, half_ref, loss_ref, mats_ref = take(6)
         old_refs = dict(zip(old, take(len(old))))
         in_refs = take(len(extra))
+        shared_refs = take(len(shared))
         state_refs = take(1) if going else []
         new_refs = dict(zip(keepers, take(len(keepers))))
         out_refs = take(1) if emits else []
+        made_refs = take(6) if makes else []
         held = refs.pop(-1)
         u, c, _, va, vb = refs[:5]
-        env = {"scratch": refs, "rate": rate_ref, "mask": mask_ref, "half_d": half_ref, "loss": loss_ref, "mats": mats_ref}
+        env = {"scratch": refs, "rate": rate_ref, "mask": mask_ref, "side": side_ref, "half_d": half_ref, "loss": loss_ref, "mats": mats_ref}
         if plan.closed:
             for x in (0, plan.wide_x - 1):
                 for y in range(plan.wide_y):
@@ -290,27 +325,35 @@
                 for y in range(plan.core_y):
                     va[x, y] = jnp.zeros((fields, nz), jnp.float32)
                     vb[x, y] = jnp.zeros((fields, nz), jnp.float32)
+                    if makes:
+                        made_refs[0][x, y] = jnp.zeros((fields, nz), jnp.float32)
         for p in group:
             node = diagonal - p
-            at, index = where[p]
             inflow_in = None if p == 0 or node == STEPS else (in_refs[0] if p == group[0] else held)
             inflow_out = None if p not in old else (out_refs[0] if p == group[-1] else held)
+            out = state_refs[0].at[going.index(p)] if p in going else None
+            if node == 0 and p > 0:
+                first_pass(env, plan, inflow_in, new_refs.get(p), out, shared_refs)
+                continue
+            at, index = where[p]
             level_pass(
                 [r.at[index] for r in src[at : at + 3]], env, plan, node, inflow_in, inflow_out,
-                old_refs.get(p), new_refs.get(p), state_refs[0].at[going.index(p)] if p in going else None,
+                old_refs.get(p), new_refs.get(p), out, made_refs if makes else None,
             )
 
     vmem = pl.BlockSpec(memory_space=pltpu.VMEM)
     smem = pl.BlockSpec(memory_space=pltpu.SMEM)
     f32 = jnp.float32
-    operands = sources + list(common) + [kept[p] for p in old] + extra
-    in_specs = [vmem] * n_src + [vmem, smem, vmem, vmem, vmem] + [vmem] * (len(old) + len(extra))
+    operands = sources + list(common) + [kept[p] for p in old] + extra + shared
+    in_specs = [vmem] * n_src + [vmem, smem, smem, vmem, vmem, vmem] + [vmem] * (len(old) + len(extra) + len(shared))
     out_shape = [jax.ShapeDtypeStruct((len(going), plan.sub_x, plan.sub_y, fields, nz), f32)] if going else []
     out_shape += [jax.ShapeDtypeStruct(core, f32)] * (len(keepers) + emits)
     cells = core[0] * core[1] * fields * nz
     wide = (plan.wide_x, plan.wide_y, fields, nz)
     tall = (plan.wide_x,) + core[1:]
     chem = (2, 2) + core[1:]
+    if makes:
+        out_shape += [jax.ShapeDtypeStruct(shape, f32) for shape in (tall, tall, core, core, core, core)]
     shapes = [wide, wide, chem, tall, tall, tall, core, core, core, core, core]
     results = list(pl.pallas_call(
         kernel,
@@ -318,12 +361,15 @@
         in_specs=in_specs,
         out_specs=[vmem] * len(out_shape),
         scratch_shapes=[pltpu.VMEM(s, f32) for s in shapes],
-        compiler_params=pltpu.CompilerParams(vmem_limit_bytes=56 * 2**20),
+        compiler_params=pltpu.CompilerParams(vmem_limit_bytes=30 * 2**20),
         cost_estimate=pl.CostEstimate(flops=150 * cells * len(group), bytes_accessed=8 * cells * len(group), transcendentals=0),
         name="wave%d_%d" % (diagonal, group[0]),
     )(*operands))
     states = results.pop(0) if going else None
-    return going, states, dict(zip(keepers, results)), results[-1] if emits else None
+    held = dict(zip(keepers, results))
+    if makes:
+        cache.extend(results[-6:] + [held[0]])
+    return going, states, held, results[-1] if emits else None
 
 
 def inside_mask(plan):
@@ -370,7 +416,8 @@
 
 
 def grouped(active):
-    return [active[i : i + GROUP] for i in range(0, len(active), GROUP)]
+    size = 1 if len(active) == 2 and active[0] == 0 else GROUP
+    return [active[i : i + size] for i in range(0, len(active), size)]
 
 
 def on_device(initial, rate_factor, diffusivity, loss_rate, quench, formation):
@@ -380,7 +427,6 @@
 
     started, rate = columns(jnp.transpose(initial, (1, 2, 0, 3)), rate_factor, plan)
     started = [x[None] for x in started]
-    rate = jnp.concatenate(rate, axis=1)
     rate = rate[:, 1:-1] if plan.closed else rate[1:-1, 1:-1]
     mask = inside_mask(plan)
 
@@ -391,16 +437,17 @@
     mats = []
     for matrix in ((reacting * loss_rate)[:, None] * quench, reacting[:, None] * formation):
         mats.append(jnp.concatenate([jnp.kron(eye, m) for m in matrix_halves(matrix)], axis=0))
-    common = [rate, mask, half_d, loss, jnp.stack(mats).astype(jnp.bfloat16)]
-
-    strips, kept, finals = {}, {}, {}
+    side = (lax.axis_index("lvl") % plan.parts_y).astype(jnp.int32)[None]
+    common = [rate, mask, side, half_d, loss, jnp.stack(mats).astype(jnp.bfloat16)]
+
+    strips, kept, finals, cache = {}, {}, {}, []
     for diagonal in range(levels + STEPS - 1):
         if diagonal < levels:
-            strips[diagonal] = (started, 0)
+            strips[diagonal] = (started, 0) if diagonal == 0 else None
         active = [p for p in sorted(strips) if diagonal - p < STEPS + (p < levels - 1)]
         inflow, fresh, held = None, {}, {}
         for group in grouped(active):
-            going, states, keeps, inflow = wave(diagonal, group, plan, fields, nz, strips, inflow, common, kept)
+            going, states, keeps, inflow = wave(diagonal, group, plan, fields, nz, strips, inflow, common, kept, cache)
             held.update(keeps)
             for i, p in enumerate(going):
                 if diagonal - p + 1 == STEPS:

time: 298 us -> 221 us (0.74)
  Pallas kernels: 126 us -> 95.3 us
  starting transfers between devices: 120 us -> 94.4 us
  local copies, waits for them, and re-layouts: 16.3 us -> 7.57 us
  waiting for transfers between devices: 25.8 us -> 17.9 us
  other arithmetic: 7.34 us -> 3.18 us
    pallas_call x7 -> x12, Pallas kernels: 126 us -> 95.3 us  [wave(): pl.pallas_call(kernel, out_shape=out_shape, in_specs=in_specs, out_specs=...]
    ppermute x13 -> x23, starting transfers between devices: 107 us -> 85.5 us  [the longest x11 75.3 us: exchange(): lax.ppermute(states, AXES, plan.swaps(False))]
    ppermute x13 -> x23, waiting for transfers between devices: 14.1 us -> 6.23 us  [the longest x11 6.2 us: exchange(): lax.ppermute(states, AXES, plan.swaps(False))]
    unnamed x37 -> x15, local copies, waits for them, and re-layouts: 8.11 us -> 2.73 us
    ppermute x1, starting transfers between devices: 11.7 us -> 7.37 us  [gather_finals(): got.append(lax.ppermute(theirs, 'lvl', pairs))]
  transfers between devices with their start and end apart: 15 -> 25, of which waited for: 12 -> 6; matrix products, arithmetic and copies ran while one was open for 2% -> 1% of each run, Pallas kernels for 0% -> 15%
where the time goes in v3:
time: 221 us; the launch traced here: 219 us
  Pallas kernels  95.3 us (43%)
  starting transfers between devices  94.4 us (43%)
  waiting for transfers between devices  17.9 us (8%)
  local copies, waits for them, and re-layouts  7.57 us (3%)
  other arithmetic  3.18 us (1%)
    pallas_call x12, Pallas kernels, wave(): pl.pallas_call(kernel, out_shape=out_shape, in_specs=in_specs, out_specs=...  95.3 us
    ppermute x11, starting transfers between devices, exchange(): lax.ppermute(states, AXES, plan.swaps(False))  75.3 us
    ppermute x1, waiting for transfers between devices, columns(): lax.ppermute(pack(own, rate), 'gx', [(0, 1), (1, 0)])  10.5 us
    ppermute x11, starting transfers between devices, exchange(): lax.ppermute(states, AXES, plan.swaps(True))  9.49 us
    ppermute x1, starting transfers between devices, gather_finals(): got.append(lax.ppermute(theirs, 'lvl', pairs))  7.37 us
    ppermute x11, waiting for transfers between devices, exchange(): lax.ppermute(states, AXES, plan.swaps(False))  6.2 us
  transfers between devices with their start and end apart: 25, of which 6 were waited for; matrix products, arithmetic and copies ran while one was open for 1% of the time, Pallas kernels for 15%

profile of v3, /device:TPU:2, one launch (start us, length us, event | category | flops | bytes accessed | tf_op | source)
XLA Modules:
  0.0 218.8 jit_solution(10567827861421735625)
XLA Ops:
  0.0 1.4 copy.14
  1.4 1.6 pad_maximum_fusion.1
  3.0 1.5 collective-permute-start
  4.7 0.7 multiply_convert_fusion.3
  7.2 10.5 %collective-permute-done = f32[1088,128]{1,0:T(8,128)} collective-permute-done((f32[1088,128]{1,0:T(8,128)}, f32[1088,128]{1,0:T(8,128)}, u32[]{:S(2)}, u32[]{:S(2)}) %collective-permute-start) | collective-permute-done | bytes 557088 | tf_op jit(solution)/shard_map/ppermute | solution.py:86
  17.7 0.8 slice_bitcast_fusion
  18.5 1.1 slice.40
  19.8 0.7 collective-permute-start.1
  20.9 6.3 %wave0_0.1 = (f32[1,16,4,16,128]{4,3,2,1,0:T(8,128)S(1)}, f32[16,10,16,128]{3,2,1,0:T(8,128)S(1)}, f32[18,10,16,128]{3,2,1,0:T(8,128)S(1)}, f32[18,10,16,128]{3,...) custom-call(f32[1,16,4,16,128]{4,3,2,1,0:T(8,128)S(1)} %get-tuple-el, ...), custom_call_target="tpu_custom_call" | custom-call | flops 49152000 | bytes 2621440 | tf_op jit(solution)/shard_map/wave0_0/pallas_call | solution.py:358
  27.3 0.7 collective-permute-start.3
  28.0 13.0 %collective-permute-start.2 = (f32[1,16,4,16,128]{4,3,2,1,0:T(8,128)S(1)}, f32[1,16,4,16,128]{4,3,2,1,0:T(8,128)S(1)}, u32[]{:S(2)}, u32[]{:S(2)}) collective-permute-start(f32[1,16,4,16,128]{4,3,2,1,0:T(8,128)S(1)} %get-tuple-element.38.refs_1_), channel_id=1, source_target_pairs={{0,8},{1,9},{2,10},{3,11},{4,12},{5,13},{6,14},{7,15},{8,0},{9,1},... | collective-permute-start | bytes 1572872 | tf_op jit(solution)/shard_map/ppermute | solution.py:111
  40.9 1.5 collective-permute-done.2.refs_0_
  42.5 6.1 %wave1_0.1 = (f32[1,16,4,16,128]{4,3,2,1,0:T(8,128)S(1)}, f32[16,10,16,128]{3,2,1,0:T(8,128)S(1)}, f32[16,10,16,128]{3,2,1,0:T(8,128)S(1)}) custom-call(f32[1,16,4,16,128]{4,3,2,1,0:T(8,128)S(1)} %collective-permute-done.2.refs_0_, f32[1,16,4,16,128]{4,3,2,1,0:T(8,128)S(1)} %get-tuple-element.38.refs_1_, ...), custom_call_target="tpu_custom_call" | custom-call | flops 49152000 | bytes 2621440 | tf_op jit(solution)/shard_map/wave1_0/pallas_call | solution.py:358
  48.6 3.4 %wave1_1.1 = (f32[1,16,4,16,128]{4,3,2,1,0:T(8,128)S(1)}, f32[16,10,16,128]{3,2,1,0:T(8,128)S(1)}) custom-call(f32[16,10,128]{2,1,0:T(8,128)S(1)} %fusion.4.refs_3_.refs_0_.refs_6_, f32[2,16]{1,0:T(2,128)S(1)} %add_convert_fusion.refs_4_.refs_1_.refs_7_, s32[1]{0:T(128)} %bitcast.11.refs_5_.refs_2_.refs_8_, ...), custom_call_target="tpu_custom_call" | custom-call | flops 49152000 | bytes 2621440 | tf_op jit(solution)/shard_map/wave1_1/pallas_call | solution.py:358
  52.0 0.7 collective-permute-start.7
  52.7 8.3 %collective-permute-start.6 = (f32[1,16,4,16,128]{4,3,2,1,0:T(8,128)S(1)}, f32[1,16,4,16,128]{4,3,2,1,0:T(8,128)S(1)}, u32[]{:S(2)}, u32[]{:S(2)}) collective-permute-start(f32[1,16,4,16,128]{4,3,2,1,0:T(8,128)S(1)} %get-tuple-element.48.refs_4_), channel_id=1, source_target_pairs={{0,8},{1,9},{2,10},{3,11},{4,12},{5,13},{6,14},{7,15},{8,0},{9,1},... | collective-permute-start | bytes 1572872 | tf_op jit(solution)/shard_map/ppermute | solution.py:111
  61.6 3.0 %collective-permute-start.4 = (f32[1,16,4,16,128]{4,3,2,1,0:T(8,128)S(1)}, f32[1,16,4,16,128]{4,3,2,1,0:T(8,128)S(1)}, u32[]{:S(2)}, u32[]{:S(2)}) collective-permute-start(f32[1,16,4,16,128]{4,3,2,1,0:T(8,128)S(1)} %get-tuple-element.40.refs_1_), channel_id=1, source_target_pairs={{0,8},{1,9},{2,10},{3,11},{4,12},{5,13},{6,14},{7,15},{8,0},{9,1},... | collective-permute-start | bytes 1572872 | tf_op jit(solution)/shard_map/ppermute | solution.py:111
  64.6 1.5 collective-permute-done.4.refs_0_
  66.2 11.4 %wave2_0.1 = (f32[2,16,4,16,128]{4,3,2,1,0:T(8,128)S(1)}, f32[16,10,16,128]{3,2,1,0:T(8,128)S(1)}, f32[16,10,16,128]{3,2,1,0:T(8,128)S(1)}, f32[16,10,16,128]{3,2,1,0:T(8,128)S(1)}) custom-call(f32[1,16,4,16,128]{4,3,2,1,0:T(8,128)S(1)} %collective-permute-done.4.refs_0_, f32[1,16,4,16,128]{4,3,2,1,0:T(8,128)S(1)} %get-tuple-element.40.refs_1_, ...), custom_call_target="tpu_custom_call" | custom-call | flops 98304000 | bytes 5242880 | tf_op jit(solution)/shard_map/wave2_0/pallas_call | solution.py:358
  77.5 0.7 collective-permute-start.9
  78.3 10.2 %collective-permute-start.8 = (f32[2,16,4,16,128]{4,3,2,1,0:T(8,128)S(1)}, f32[2,16,4,16,128]{4,3,2,1,0:T(8,128)S(1)}, u32[]{:S(2)}, u32[]{:S(2)}) collective-permute-start(f32[2,16,4,16,128]{4,3,2,1,0:T(8,128)S(1)} %get-tuple-element.51.refs_1_), channel_id=1, source_target_pairs={{0,8},{1,9},{2,10},{3,11},{4,12},{5,13},{6,14},{7,15},{8,0},{9,1},... | collective-permute-start | bytes 3145736 | tf_op jit(solution)/shard_map/ppermute | solution.py:111
  88.5 3.4 %wave2_2.1 = (f32[1,16,4,16,128]{4,3,2,1,0:T(8,128)S(1)}, f32[16,10,16,128]{3,2,1,0:T(8,128)S(1)}) custom-call(f32[16,10,128]{2,1,0:T(8,128)S(1)} %fusion.4.refs_3_.refs_0_.refs_6_, f32[2,16]{1,0:T(2,128)S(1)} %add_convert_fusion.refs_4_.refs_1_.refs_7_, s32[1]{0:T(128)} %bitcast.11.refs_5_.refs_2_.refs_8_, ...), custom_call_target="tpu_custom_call" | custom-call | flops 49152000 | bytes 2621440 | tf_op jit(solution)/shard_map/wave2_2/pallas_call | solution.py:358
  91.8 0.7 collective-permute-start.15
  92.5 3.0 %collective-permute-start.14 = (f32[1,16,4,16,128]{4,3,2,1,0:T(8,128)S(1)}, f32[1,16,4,16,128]{4,3,2,1,0:T(8,128)S(1)}, u32[]{:S(2)}, u32[]{:S(2)}) collective-permute-start(f32[1,16,4,16,128]{4,3,2,1,0:T(8,128)S(1)} %get-tuple-element.59.refs_1_), channel_id=1, source_target_pairs={{0,8},{1,9},{2,10},{3,11},{4,12},{5,13},{6,14},{7,15},{8,0},{9,1},... | collective-permute-start | bytes 1572872 | tf_op jit(solution)/shard_map/ppermute | solution.py:111
  95.5 11.4 %wave3_0.1 = (f32[2,16,4,16,128]{4,3,2,1,0:T(8,128)S(1)}, f32[16,10,16,128]{3,2,1,0:T(8,128)S(1)}, f32[16,10,16,128]{3,2,1,0:T(8,128)S(1)}, f32[16,10,16,128]{3,2,1,0:T(8,128)S(1)}) custom-call(f32[2,16,4,16,128]{4,3,2,1,0:T(8,128)S(1)} %collective-permute-done.8.refs_0_, f32[2,16,4,16,128]{4,3,2,1,0:T(8,128)S(1)} %get-tuple-element.51.refs_1_, ...), custom_call_target="tpu_custom_call" | custom-call | flops 98304000 | bytes 5242880 | tf_op jit(solution)/shard_map/wave3_0/pallas_call | solution.py:358
  106.9 0.9 collective-permute-start.11
  107.8 8.3 %collective-permute-start.10 = (f32[2,16,4,16,128]{4,3,2,1,0:T(8,128)S(1)}, f32[2,16,4,16,128]{4,3,2,1,0:T(8,128)S(1)}, u32[]{:S(2)}, u32[]{:S(2)}) collective-permute-start(f32[2,16,4,16,128]{4,3,2,1,0:T(8,128)S(1)} %get-tuple-element.54.refs_1_), channel_id=1, source_target_pairs={{0,8},{1,9},{2,10},{3,11},{4,12},{5,13},{6,14},{7,15},{8,0},{9,1},... | collective-permute-start | bytes 3145736 | tf_op jit(solution)/shard_map/ppermute | solution.py:111
  116.2 9.1 %wave3_2.1 = (f32[2,16,4,16,128]{4,3,2,1,0:T(8,128)S(1)}, f32[16,10,16,128]{3,2,1,0:T(8,128)S(1)}) custom-call(f32[1,16,4,16,128]{4,3,2,1,0:T(8,128)S(1)} %collective-permute-done.14.refs_0_, f32[1,16,4,16,128]{4,3,2,1,0:T(8,128)S(1)} %get-tuple-element.59.refs_1_, f32[1,16,4,16,128]{4,3,2,1,0:T(8,128)S(1)} %collective-permute-done.15.refs_2_, ...), custom_call_target="tpu_custom_call" | custom-call | flops 98304000 | bytes 5242880 | tf_op jit(solution)/shard_map/wave3_2/pallas_call | solution.py:358
  125.3 0.7 collective-permute-start.17
  126.0 2.9 %collective-permute-start.16 = (f32[2,16,4,16,128]{4,3,2,1,0:T(8,128)S(1)}, f32[2,16,4,16,128]{4,3,2,1,0:T(8,128)S(1)}, u32[]{:S(2)}, u32[]{:S(2)}) collective-permute-start(f32[2,16,4,16,128]{4,3,2,1,0:T(8,128)S(1)} %get-tuple-element.62.refs_1_), channel_id=1, source_target_pairs={{0,8},{1,9},{2,10},{3,11},{4,12},{5,13},{6,14},{7,15},{8,0},{9,1},... | collective-permute-start | bytes 3145736 | tf_op jit(solution)/shard_map/ppermute | solution.py:111
  129.0 8.9 %wave4_0.1 = (f32[1,16,4,16,128]{4,3,2,1,0:T(8,128)S(1)}, f32[16,10,16,128]{3,2,1,0:T(8,128)S(1)}, f32[16,10,16,128]{3,2,1,0:T(8,128)S(1)}) custom-call(f32[2,16,4,16,128]{4,3,2,1,0:T(8,128)S(1)} %collective-permute-done.10.refs_0_, f32[2,16,4,16,128]{4,3,2,1,0:T(8,128)S(1)} %get-tuple-element.54.refs_1_, ...), custom_call_target="tpu_custom_call" | custom-call | flops 98304000 | bytes 5242880 | tf_op jit(solution)/shard_map/wave4_0/pallas_call | solution.py:358
  137.9 11.2 %wave4_2.1 = (f32[2,16,4,16,128]{4,3,2,1,0:T(8,128)S(1)}, f32[16,10,16,128]{3,2,1,0:T(8,128)S(1)}) custom-call(f32[2,16,4,16,128]{4,3,2,1,0:T(8,128)S(1)} %collective-permute-done.16.refs_0_, f32[2,16,4,16,128]{4,3,2,1,0:T(8,128)S(1)} %get-tuple-element.62.refs_1_, f32[2,16,4,16,128]{4,3,2,1,0:T(8,128)S(1)} %collective-permute-done.17.refs_2_, ...), custom_call_target="tpu_custom_call" | custom-call | flops 98304000 | bytes 5242880 | tf_op jit(solution)/shard_map/wave4_2/pallas_call | solution.py:358
  149.0 0.7 collective-permute-start.19
  149.8 6.5 %collective-permute-start.18 = (f32[2,16,4,16,128]{4,3,2,1,0:T(8,128)S(1)}, f32[2,16,4,16,128]{4,3,2,1,0:T(8,128)S(1)}, u32[]{:S(2)}, u32[]{:S(2)}) collective-permute-start(f32[2,16,4,16,128]{4,3,2,1,0:T(8,128)S(1)} %get-tuple-element.65.refs_4_.refs_1_), channel_id=1, source_target_pairs={{0,8},{1,9},{2,10},{3,11},{4,12},{5,13},{6,14},{7,15},{8,0},{9,1},... | collective-permute-start | bytes 3145736 | tf_op jit(solution)/shard_map/ppermute | solution.py:111
  156.9 3.0 %collective-permute-start.12 = (f32[1,16,4,16,128]{4,3,2,1,0:T(8,128)S(1)}, f32[1,16,4,16,128]{4,3,2,1,0:T(8,128)S(1)}, u32[]{:S(2)}, u32[]{:S(2)}) collective-permute-start(f32[1,16,4,16,128]{4,3,2,1,0:T(8,128)S(1)} %get-tuple-element.57.refs_1_), channel_id=1, source_target_pairs={{0,8},{1,9},{2,10},{3,11},{4,12},{5,13},{6,14},{7,15},{8,0},{9,1},... | collective-permute-start | bytes 1572872 | tf_op jit(solution)/shard_map/ppermute | solution.py:111
  159.9 1.5 collective-permute-done.12.refs_0_
  161.4 8.9 %wave5_1.1 = (f32[1,16,4,16,128]{4,3,2,1,0:T(8,128)S(1)}, f32[16,10,16,128]{3,2,1,0:T(8,128)S(1)}, f32[16,10,16,128]{3,2,1,0:T(8,128)S(1)}) custom-call(f32[1,16,4,16,128]{4,3,2,1,0:T(8,128)S(1)} %collective-permute-done.12.refs_0_, f32[1,16,4,16,128]{4,3,2,1,0:T(8,128)S(1)} %get-tuple-element.57.refs_1_, ...), custom_call_target="tpu_custom_call" | custom-call | flops 98304000 | bytes 5242880 | tf_op jit(solution)/shard_map/wave5_1/pallas_call | solution.py:358
  170.4 5.8 %wave5_3.1.refs_4_ = f32[1,16,4,16,128]{4,3,2,1,0:T(8,128)S(1)} custom-call(f32[2,16,4,16,128]{4,3,2,1,0:T(8,128)S(1)} %collective-permute-done.18.refs_3_.refs_0_, f32[2,16,4,16,128]{4,3,2,1,0:T(8,128)S(1)} %get-tuple-element.65.refs_4_.refs_1_, f32[2,16,4,16,128]{4,3,2,1,0:T(8,128)S(1)} %collective-permute-done.19.refs_5_.refs_2_, ...), custom_call_target="tpu_custom_call" | custom-call | flops 49152000 | bytes 2621440 | tf_op jit(solution)/shard_map/wave5_3/pallas_call | solution.py:358
  176.2 1.5 collective-permute-start.23
  177.7 15.1 %collective-permute-start.22 = (f32[1,16,4,16,128]{4,3,2,1,0:T(8,128)S(1)}, f32[1,16,4,16,128]{4,3,2,1,0:T(8,128)}, u32[]{:S(2)}, u32[]{:S(2)}) collective-permute-start(f32[1,16,4,16,128]{4,3,2,1,0:T(8,128)S(1)} %wave5_3.1.refs_4_), channel_id=1, source_target_pairs={{0,8},{1,9},{2,10},{3,11},{4,12},{5,13},{6,14},{7,15},{8,0},{9,1},... | collective-permute-start | bytes 1572872 | tf_op jit(solution)/shard_map/ppermute | solution.py:111
  192.7 1.5 collective-permute-start.21
  194.2 2.2 collective-permute-start.20
  196.5 1.6 collective-permute-done.20.refs_0_
  198.1 1.3 copy-done.1
  199.4 9.5 %wave6_2.1 = f32[1,16,4,16,128]{4,3,2,1,0:T(8,128)S(1)} custom-call(f32[1,16,4,16,128]{4,3,2,1,0:T(8,128)} %collective-permute-done.20.refs_0_, f32[1,16,4,16,128]{4,3,2,1,0:T(8,128)S(1)} %get-tuple-element.68.refs_1_, f32[1,16,4,16,128]{4,3,2,1,0:T(8,128)} %collective-permute-done.21.refs_2_, f32[1,16,4,16,128]{4,3,2,1,0:T(8,128)} %collective-permute-done.22.refs_3_, ...), custom_call_target="tpu_custom_call" | custom-call | flops 98304000 | bytes 5242880 | tf_op jit(solution)/shard_map/wave6_2/pallas_call | solution.py:358
  209.1 7.4 %collective-permute-start.24 = (f32[8,4,16,128]{3,2,1,0:T(8,128)S(1)}, f32[8,4,16,128]{3,2,1,0:T(8,128)S(1)}, u32[]{:S(2)}, u32[]{:S(2)}) collective-permute-start(f32[8,4,16,128]{3,2,1,0:T(8,128)S(1)} %get-tuple-element.71), channel_id=1, source_target_pairs={{0,8},{8,0},{16,24},{24,16},{1,9},{9,1},{17,25},{25,17},{2,10},{10... | collective-permute-start | bytes 786440 | tf_op jit(solution)/shard_map/ppermute | solution.py:412
  216.5 1.2 collective-permute-done.24
  217.9 1.0 copy.11
  (64 shorter events, 4.4 us)
Async XLA Ops:
  0.0 4.5 %copy-start.5 = (f32[16]{0:T(128)S(1)}, f32[16]{0:T(128)}, u32[]{:S(2)}) copy-start(f32[16]{0:T(128)} %param.9) | copy-start | bytes 196
  0.0 4.5 %copy-start.3 = (f32[16,16]{1,0:T(8,128)S(1)}, f32[16,16]{1,0:T(8,128)}, u32[]{:S(2)}) copy-start(f32[16,16]{1,0:T(8,128)} %param.11) | copy-start | bytes 3076
  0.0 4.6 %copy-start.4 = (f32[16,16]{1,0:T(8,128)S(1)}, f32[16,16]{1,0:T(8,128)}, u32[]{:S(2)}) copy-start(f32[16,16]{1,0:T(8,128)} %param.10) | copy-start | bytes 3076
  3.0 14.7 %collective-permute-start = (f32[1088,128]{1,0:T(8,128)}, f32[1088,128]{1,0:T(8,128)}, u32[]{:S(2)}, u32[]{:S(2)}) collective-permute-start(f32[1088,128]{1,0:T(8,128)} %pad_maximum_fusion.1), channel_id=1, source_target_pairs={{0,4},{4,0},{1,5},{5,1},{2,6},{6,2},{3,7},{7,3},{8,12},{12,8},{9,1... | collective-permute-start | bytes 1671176 | tf_op jit(solution)/shard_map/ppermute | solution.py:86
  5.8 12.6 %copy-start.2 = (f32[8,8,128]{2,1,0:T(8,128)S(1)}, f32[8,8,128]{2,1,0:T(8,128)}, u32[]{:S(2)}) copy-start(f32[8,8,128]{2,1,0:T(8,128)} %param.7) | copy-start | bytes 98308
  19.8 0.9 copy-start.6
  19.8 0.8 collective-permute-start.1
  27.3 13.7 %collective-permute-start.3 = (f32[1,16,4,16,128]{4,3,2,1,0:T(8,128)S(1)}, f32[1,16,4,16,128]{4,3,2,1,0:T(8,128)S(1)}, u32[]{:S(2)}, u32[]{:S(2)}) collective-permute-start(f32[1,16,4,16,128]{4,3,2,1,0:T(8,128)S(1)} %get-tuple-element.38.refs_1_), channel_id=1, source_target_pairs={{1,8},{2,9},{3,10},{5,12},{6,13},{7,14},{8,1},{9,2},{10,3},{12,5},... | collective-permute-start | bytes 1572872 | tf_op jit(solution)/shard_map/ppermute | solution.py:111
  28.0 14.5 %collective-permute-start.2 = (f32[1,16,4,16,128]{4,3,2,1,0:T(8,128)S(1)}, f32[1,16,4,16,128]{4,3,2,1,0:T(8,128)S(1)}, u32[]{:S(2)}, u32[]{:S(2)}) collective-permute-start(f32[1,16,4,16,128]{4,3,2,1,0:T(8,128)S(1)} %get-tuple-element.38.refs_1_), channel_id=1, source_target_pairs={{0,8},{1,9},{2,10},{3,11},{4,12},{5,13},{6,14},{7,15},{8,0},{9,1},... | collective-permute-start | bytes 1572872 | tf_op jit(solution)/shard_map/ppermute | solution.py:111
  52.0 12.6 %collective-permute-start.7 = (f32[1,16,4,16,128]{4,3,2,1,0:T(8,128)S(1)}, f32[1,16,4,16,128]{4,3,2,1,0:T(8,128)S(1)}, u32[]{:S(2)}, u32[]{:S(2)}) collective-permute-start(f32[1,16,4,16,128]{4,3,2,1,0:T(8,128)S(1)} %get-tuple-element.48.refs_4_), channel_id=1, source_target_pairs={{1,8},{2,9},{3,10},{5,12},{6,13},{7,14},{8,1},{9,2},{10,3},{12,5},... | collective-permute-start | bytes 1572872 | tf_op jit(solution)/shard_map/ppermute | solution.py:111
  52.7 11.9 %collective-permute-start.6 = (f32[1,16,4,16,128]{4,3,2,1,0:T(8,128)S(1)}, f32[1,16,4,16,128]{4,3,2,1,0:T(8,128)S(1)}, u32[]{:S(2)}, u32[]{:S(2)}) collective-permute-start(f32[1,16,4,16,128]{4,3,2,1,0:T(8,128)S(1)} %get-tuple-element.48.refs_4_), channel_id=1, source_target_pairs={{0,8},{1,9},{2,10},{3,11},{4,12},{5,13},{6,14},{7,15},{8,0},{9,1},... | collective-permute-start | bytes 1572872 | tf_op jit(solution)/shard_map/ppermute | solution.py:111
  61.0 3.7 %collective-permute-start.5 = (f32[1,16,4,16,128]{4,3,2,1,0:T(8,128)S(1)}, f32[1,16,4,16,128]{4,3,2,1,0:T(8,128)S(1)}, u32[]{:S(2)}, u32[]{:S(2)}) collective-permute-start(f32[1,16,4,16,128]{4,3,2,1,0:T(8,128)S(1)} %get-tuple-element.40.refs_1_), channel_id=1, source_target_pairs={{1,8},{2,9},{3,10},{5,12},{6,13},{7,14},{8,1},{9,2},{10,3},{12,5},... | collective-permute-start | bytes 1572872 | tf_op jit(solution)/shard_map/ppermute | solution.py:111
  61.6 4.5 %collective-permute-start.4 = (f32[1,16,4,16,128]{4,3,2,1,0:T(8,128)S(1)}, f32[1,16,4,16,128]{4,3,2,1,0:T(8,128)S(1)}, u32[]{:S(2)}, u32[]{:S(2)}) collective-permute-start(f32[1,16,4,16,128]{4,3,2,1,0:T(8,128)S(1)} %get-tuple-element.40.refs_1_), channel_id=1, source_target_pairs={{0,8},{1,9},{2,10},{3,11},{4,12},{5,13},{6,14},{7,15},{8,0},{9,1},... | collective-permute-start | bytes 1572872 | tf_op jit(solution)/shard_map/ppermute | solution.py:111
  77.5 18.0 %collective-permute-start.9 = (f32[2,16,4,16,128]{4,3,2,1,0:T(8,128)S(1)}, f32[2,16,4,16,128]{4,3,2,1,0:T(8,128)S(1)}, u32[]{:S(2)}, u32[]{:S(2)}) collective-permute-start(f32[2,16,4,16,128]{4,3,2,1,0:T(8,128)S(1)} %get-tuple-element.51.refs_1_), channel_id=1, source_target_pairs={{1,8},{2,9},{3,10},{5,12},{6,13},{7,14},{8,1},{9,2},{10,3},{12,5},... | collective-permute-start | bytes 3145736 | tf_op jit(solution)/shard_map/ppermute | solution.py:111
  78.3 17.3 %collective-permute-start.8 = (f32[2,16,4,16,128]{4,3,2,1,0:T(8,128)S(1)}, f32[2,16,4,16,128]{4,3,2,1,0:T(8,128)S(1)}, u32[]{:S(2)}, u32[]{:S(2)}) collective-permute-start(f32[2,16,4,16,128]{4,3,2,1,0:T(8,128)S(1)} %get-tuple-element.51.refs_1_), channel_id=1, source_target_pairs={{0,8},{1,9},{2,10},{3,11},{4,12},{5,13},{6,14},{7,15},{8,0},{9,1},... | collective-permute-start | bytes 3145736 | tf_op jit(solution)/shard_map/ppermute | solution.py:111
  91.8 24.3 %collective-permute-start.15 = (f32[1,16,4,16,128]{4,3,2,1,0:T(8,128)S(1)}, f32[1,16,4,16,128]{4,3,2,1,0:T(8,128)S(1)}, u32[]{:S(2)}, u32[]{:S(2)}) collective-permute-start(f32[1,16,4,16,128]{4,3,2,1,0:T(8,128)S(1)} %get-tuple-element.59.refs_1_), channel_id=1, source_target_pairs={{1,8},{2,9},{3,10},{5,12},{6,13},{7,14},{8,1},{9,2},{10,3},{12,5},... | collective-permute-start | bytes 1572872 | tf_op jit(solution)/shard_map/ppermute | solution.py:111
  92.5 23.6 %collective-permute-start.14 = (f32[1,16,4,16,128]{4,3,2,1,0:T(8,128)S(1)}, f32[1,16,4,16,128]{4,3,2,1,0:T(8,128)S(1)}, u32[]{:S(2)}, u32[]{:S(2)}) collective-permute-start(f32[1,16,4,16,128]{4,3,2,1,0:T(8,128)S(1)} %get-tuple-element.59.refs_1_), channel_id=1, source_target_pairs={{0,8},{1,9},{2,10},{3,11},{4,12},{5,13},{6,14},{7,15},{8,0},{9,1},... | collective-permute-start | bytes 1572872 | tf_op jit(solution)/shard_map/ppermute | solution.py:111
  106.9 22.0 %collective-permute-start.11 = (f32[2,16,4,16,128]{4,3,2,1,0:T(8,128)S(1)}, f32[2,16,4,16,128]{4,3,2,1,0:T(8,128)S(1)}, u32[]{:S(2)}, u32[]{:S(2)}) collective-permute-start(f32[2,16,4,16,128]{4,3,2,1,0:T(8,128)S(1)} %get-tuple-element.54.refs_1_), channel_id=1, source_target_pairs={{1,8},{2,9},{3,10},{5,12},{6,13},{7,14},{8,1},{9,2},{10,3},{12,5},... | collective-permute-start | bytes 3145736 | tf_op jit(solution)/shard_map/ppermute | solution.py:111
  107.8 21.1 %collective-permute-start.10 = (f32[2,16,4,16,128]{4,3,2,1,0:T(8,128)S(1)}, f32[2,16,4,16,128]{4,3,2,1,0:T(8,128)S(1)}, u32[]{:S(2)}, u32[]{:S(2)}) collective-permute-start(f32[2,16,4,16,128]{4,3,2,1,0:T(8,128)S(1)} %get-tuple-element.54.refs_1_), channel_id=1, source_target_pairs={{0,8},{1,9},{2,10},{3,11},{4,12},{5,13},{6,14},{7,15},{8,0},{9,1},... | collective-permute-start | bytes 3145736 | tf_op jit(solution)/shard_map/ppermute | solution.py:111
  125.3 12.6 %collective-permute-start.17 = (f32[2,16,4,16,128]{4,3,2,1,0:T(8,128)S(1)}, f32[2,16,4,16,128]{4,3,2,1,0:T(8,128)S(1)}, u32[]{:S(2)}, u32[]{:S(2)}) collective-permute-start(f32[2,16,4,16,128]{4,3,2,1,0:T(8,128)S(1)} %get-tuple-element.62.refs_1_), channel_id=1, source_target_pairs={{1,8},{2,9},{3,10},{5,12},{6,13},{7,14},{8,1},{9,2},{10,3},{12,5},... | collective-permute-start | bytes 3145736 | tf_op jit(solution)/shard_map/ppermute | solution.py:111
  126.0 11.8 %collective-permute-start.16 = (f32[2,16,4,16,128]{4,3,2,1,0:T(8,128)S(1)}, f32[2,16,4,16,128]{4,3,2,1,0:T(8,128)S(1)}, u32[]{:S(2)}, u32[]{:S(2)}) collective-permute-start(f32[2,16,4,16,128]{4,3,2,1,0:T(8,128)S(1)} %get-tuple-element.62.refs_1_), channel_id=1, source_target_pairs={{0,8},{1,9},{2,10},{3,11},{4,12},{5,13},{6,14},{7,15},{8,0},{9,1},... | collective-permute-start | bytes 3145736 | tf_op jit(solution)/shard_map/ppermute | solution.py:111
  149.0 12.4 %collective-permute-start.19 = (f32[2,16,4,16,128]{4,3,2,1,0:T(8,128)S(1)}, f32[2,16,4,16,128]{4,3,2,1,0:T(8,128)S(1)}, u32[]{:S(2)}, u32[]{:S(2)}) collective-permute-start(f32[2,16,4,16,128]{4,3,2,1,0:T(8,128)S(1)} %get-tuple-element.65.refs_4_.refs_1_), channel_id=1, source_target_pairs={{1,8},{2,9},{3,10},{5,12},{6,13},{7,14},{8,1},{9,2},{10,3},{12,5},... | collective-permute-start | bytes 3145736 | tf_op jit(solution)/shard_map/ppermute | solution.py:111
  149.8 11.7 %collective-permute-start.18 = (f32[2,16,4,16,128]{4,3,2,1,0:T(8,128)S(1)}, f32[2,16,4,16,128]{4,3,2,1,0:T(8,128)S(1)}, u32[]{:S(2)}, u32[]{:S(2)}) collective-permute-start(f32[2,16,4,16,128]{4,3,2,1,0:T(8,128)S(1)} %get-tuple-element.65.refs_4_.refs_1_), channel_id=1, source_target_pairs={{0,8},{1,9},{2,10},{3,11},{4,12},{5,13},{6,14},{7,15},{8,0},{9,1},... | collective-permute-start | bytes 3145736 | tf_op jit(solution)/shard_map/ppermute | solution.py:111
  156.2 3.7 %collective-permute-start.13 = (f32[1,16,4,16,128]{4,3,2,1,0:T(8,128)S(1)}, f32[1,16,4,16,128]{4,3,2,1,0:T(8,128)S(1)}, u32[]{:S(2)}, u32[]{:S(2)}) collective-permute-start(f32[1,16,4,16,128]{4,3,2,1,0:T(8,128)S(1)} %get-tuple-element.57.refs_1_), channel_id=1, source_target_pairs={{1,8},{2,9},{3,10},{5,12},{6,13},{7,14},{8,1},{9,2},{10,3},{12,5},... | collective-permute-start | bytes 1572872 | tf_op jit(solution)/shard_map/ppermute | solution.py:111
  156.9 4.5 %collective-permute-start.12 = (f32[1,16,4,16,128]{4,3,2,1,0:T(8,128)S(1)}, f32[1,16,4,16,128]{4,3,2,1,0:T(8,128)S(1)}, u32[]{:S(2)}, u32[]{:S(2)}) collective-permute-start(f32[1,16,4,16,128]{4,3,2,1,0:T(8,128)S(1)} %get-tuple-element.57.refs_1_), channel_id=1, source_target_pairs={{0,8},{1,9},{2,10},{3,11},{4,12},{5,13},{6,14},{7,15},{8,0},{9,1},... | collective-permute-start | bytes 1572872 | tf_op jit(solution)/shard_map/ppermute | solution.py:111
  170.4 5.8 %copy-start = (f32[16,10,16,128]{3,2,1,0:T(8,128)}, f32[16,10,16,128]{3,2,1,0:T(8,128)S(1)}, u32[]{:S(2)}) copy-start(f32[16,10,16,128]{3,2,1,0:T(8,128)S(1)} %get-tuple-element.70.refs_12_) | copy-start | bytes 3932164
  176.2 20.3 %collective-permute-start.23 = (f32[1,16,4,16,128]{4,3,2,1,0:T(8,128)S(1)}, f32[1,16,4,16,128]{4,3,2,1,0:T(8,128)}, u32[]{:S(2)}, u32[]{:S(2)}) collective-permute-start(f32[1,16,4,16,128]{4,3,2,1,0:T(8,128)S(1)} %wave5_3.1.refs_4_), channel_id=1, source_target_pairs={{1,8},{2,9},{3,10},{5,12},{6,13},{7,14},{8,1},{9,2},{10,3},{12,5},... | collective-permute-start | bytes 1572872 | tf_op jit(solution)/shard_map/ppermute | solution.py:111
  177.7 18.8 %collective-permute-start.22 = (f32[1,16,4,16,128]{4,3,2,1,0:T(8,128)S(1)}, f32[1,16,4,16,128]{4,3,2,1,0:T(8,128)}, u32[]{:S(2)}, u32[]{:S(2)}) collective-permute-start(f32[1,16,4,16,128]{4,3,2,1,0:T(8,128)S(1)} %wave5_3.1.refs_4_), channel_id=1, source_target_pairs={{0,8},{1,9},{2,10},{3,11},{4,12},{5,13},{6,14},{7,15},{8,0},{9,1},... | collective-permute-start | bytes 1572872 | tf_op jit(solution)/shard_map/ppermute | solution.py:111
  192.7 3.7 %collective-permute-start.21 = (f32[1,16,4,16,128]{4,3,2,1,0:T(8,128)S(1)}, f32[1,16,4,16,128]{4,3,2,1,0:T(8,128)}, u32[]{:S(2)}, u32[]{:S(2)}) collective-permute-start(f32[1,16,4,16,128]{4,3,2,1,0:T(8,128)S(1)} %get-tuple-element.68.refs_1_), channel_id=1, source_target_pairs={{1,8},{2,9},{3,10},{5,12},{6,13},{7,14},{8,1},{9,2},{10,3},{12,5},... | collective-permute-start | bytes 1572872 | tf_op jit(solution)/shard_map/ppermute | solution.py:111
  194.2 3.9 %collective-permute-start.20 = (f32[1,16,4,16,128]{4,3,2,1,0:T(8,128)S(1)}, f32[1,16,4,16,128]{4,3,2,1,0:T(8,128)}, u32[]{:S(2)}, u32[]{:S(2)}) collective-permute-start(f32[1,16,4,16,128]{4,3,2,1,0:T(8,128)S(1)} %get-tuple-element.68.refs_1_), channel_id=1, source_target_pairs={{0,8},{1,9},{2,10},{3,11},{4,12},{5,13},{6,14},{7,15},{8,0},{9,1},... | collective-permute-start | bytes 1572872 | tf_op jit(solution)/shard_map/ppermute | solution.py:111
  198.1 1.3 copy-start.1
  209.1 8.5 %collective-permute-start.24 = (f32[8,4,16,128]{3,2,1,0:T(8,128)S(1)}, f32[8,4,16,128]{3,2,1,0:T(8,128)S(1)}, u32[]{:S(2)}, u32[]{:S(2)}) collective-permute-start(f32[8,4,16,128]{3,2,1,0:T(8,128)S(1)} %get-tuple-element.71), channel_id=1, source_target_pairs={{0,8},{8,0},{16,24},{24,16},{1,9},{9,1},{17,25},{25,17},{2,10},{10... | collective-permute-start | bytes 786440 | tf_op jit(solution)/shard_map/ppermute | solution.py:412

commit v4 on v3

--- a/solution.py
+++ b/solution.py
@@ -11,7 +11,6 @@
 STEPS = 4
 SWEEPS = 4
 RIM = SWEEPS - 1
-GROUP = 2
 AXES = ("lvl", "gx", "gy")
 
 
@@ -415,9 +414,11 @@
     return order.reshape((plan.rows, plan.cols) + order.shape[3:])
 
 
-def grouped(active):
-    size = 1 if len(active) == 2 and active[0] == 0 else GROUP
-    return [active[i : i + size] for i in range(0, len(active), size)]
+def grouped(diagonal, active):
+    groups = [[p] for p in active]
+    if diagonal - active[0] == STEPS and len(groups) > 2:
+        groups[:2] = [groups[0] + groups[1]]
+    return groups
 
 
 def on_device(initial, rate_factor, diffusivity, loss_rate, quench, formation):
@@ -446,7 +447,7 @@
             strips[diagonal] = (started, 0) if diagonal == 0 else None
         active = [p for p in sorted(strips) if diagonal - p < STEPS + (p < levels - 1)]
         inflow, fresh, held = None, {}, {}
-        for group in grouped(active):
+        for group in grouped(diagonal, active):
             going, states, keeps, inflow = wave(diagonal, group, plan, fields, nz, strips, inflow, common, kept, cache)
             held.update(keeps)
             for i, p in enumerate(going):

time: 221 us -> 196 us (0.89)
  starting transfers between devices: 94.4 us -> 69.1 us
  waiting for transfers between devices: 17.9 us -> 13.3 us
  Pallas kernels: 95.3 us -> 99.8 us
    ppermute x11 -> x15, starting transfers between devices: 75.3 us -> 54.3 us  [exchange(): lax.ppermute(states, AXES, plan.swaps(False))]
    ppermute x1, starting transfers between devices: 7.37 us -> 1.27 us  [gather_finals(): got.append(lax.ppermute(theirs, 'lvl', pairs))]
    ppermute x11 -> x15, waiting for transfers between devices: 6.2 us -> 1.57 us  [exchange(): lax.ppermute(states, AXES, plan.swaps(False))]
    pallas_call x12 -> x17, Pallas kernels: 95.3 us -> 99.8 us  [wave(): pl.pallas_call(kernel, out_shape=out_shape, in_specs=in_specs, out_specs=...]
    ppermute x11 -> x15, starting transfers between devices: 9.49 us -> 11.4 us  [exchange(): lax.ppermute(states, AXES, plan.swaps(True))]
  transfers between devices with their start and end apart: 25 -> 33, of which waited for: 6 -> 3; matrix products, arithmetic and copies ran while one was open for 1% -> 1% of each run, Pallas kernels for 15% -> 42%
where the time goes in v4:
time: 196 us; the launch traced here: 194 us
  Pallas kernels  99.8 us (51%)
  starting transfers between devices  69.1 us (35%)
  waiting for transfers between devices  13.3 us (7%)
  local copies, waits for them, and re-layouts  7.53 us (4%)
  other arithmetic  3.19 us (2%)
    pallas_call x17, Pallas kernels, wave(): pl.pallas_call(kernel, out_shape=out_shape, in_specs=in_specs, out_specs=...  99.8 us
    ppermute x15, starting transfers between devices, exchange(): lax.ppermute(states, AXES, plan.swaps(False))  54.3 us
    ppermute x15, starting transfers between devices, exchange(): lax.ppermute(states, AXES, plan.swaps(True))  11.4 us
    ppermute x1, waiting for transfers between devices, columns(): lax.ppermute(pack(own, rate), 'gx', [(0, 1), (1, 0)])  10.5 us
  transfers between devices with their start and end apart: 33, of which 3 were waited for; matrix products, arithmetic and copies ran while one was open for 1% of the time, Pallas kernels for 42%

profile of v4, /device:TPU:2, one launch (start us, length us, event | category | flops | bytes accessed | tf_op | source)
XLA Modules:
  0.0 193.5 jit_solution(15624955407267500677)
XLA Ops:
  0.0 1.4 copy.14
  1.4 1.6 pad_maximum_fusion.1
  3.0 1.5 collective-permute-start
  7.2 10.5 %collective-permute-done = f32[1088,128]{1,0:T(8,128)} collective-permute-done((f32[1088,128]{1,0:T(8,128)}, f32[1088,128]{1,0:T(8,128)}, u32[]{:S(2)}, u32[]{:S(2)}) %collective-permute-start) | collective-permute-done | bytes 557088 | tf_op jit(solution)/shard_map/ppermute | solution.py:85
  17.7 0.8 slice_bitcast_fusion
  18.5 1.1 slice.36
  19.8 0.7 collective-permute-start.1
  21.0 6.3 %wave0_0.1 = (f32[1,16,4,16,128]{4,3,2,1,0:T(8,128)S(1)}, f32[16,10,16,128]{3,2,1,0:T(8,128)S(1)}, f32[18,10,16,128]{3,2,1,0:T(8,128)S(1)}, f32[18,10,16,128]{3,...) custom-call(f32[1,16,4,16,128]{4,3,2,1,0:T(8,128)S(1)} %get-tuple-el, ...), custom_call_target="tpu_custom_call" | custom-call | flops 49152000 | bytes 2621440 | tf_op jit(solution)/shard_map/wave0_0/pallas_call | solution.py:357
  28.0 13.0 %collective-permute-start.2 = (f32[1,16,4,16,128]{4,3,2,1,0:T(8,128)S(1)}, f32[1,16,4,16,128]{4,3,2,1,0:T(8,128)S(1)}, u32[]{:S(2)}, u32[]{:S(2)}) collective-permute-start(f32[1,16,4,16,128]{4,3,2,1,0:T(8,128)S(1)} %get-tuple-element.44.refs_1_), channel_id=1, source_target_pairs={{0,8},{1,9},{2,10},{3,11},{4,12},{5,13},{6,14},{7,15},{8,0},{9,1},... | collective-permute-start | bytes 1572872 | tf_op jit(solution)/shard_map/ppermute | solution.py:110
  40.9 1.5 collective-permute-done.2.refs_0_
  42.5 6.1 %wave1_0.1 = (f32[1,16,4,16,128]{4,3,2,1,0:T(8,128)S(1)}, f32[16,10,16,128]{3,2,1,0:T(8,128)S(1)}, f32[16,10,16,128]{3,2,1,0:T(8,128)S(1)}) custom-call(f32[1,16,4,16,128]{4,3,2,1,0:T(8,128)S(1)} %collective-permute-done.2.refs_0_, f32[1,16,4,16,128]{4,3,2,1,0:T(8,128)S(1)} %get-tuple-element.44.refs_1_, ...), custom_call_target="tpu_custom_call" | custom-call | flops 49152000 | bytes 2621440 | tf_op jit(solution)/shard_map/wave1_0/pallas_call | solution.py:357
  48.6 0.7 collective-permute-start.5
  49.3 8.3 %collective-permute-start.4 = (f32[1,16,4,16,128]{4,3,2,1,0:T(8,128)S(1)}, f32[1,16,4,16,128]{4,3,2,1,0:T(8,128)S(1)}, u32[]{:S(2)}, u32[]{:S(2)}) collective-permute-start(f32[1,16,4,16,128]{4,3,2,1,0:T(8,128)S(1)} %get-tuple-element.46.refs_1_), channel_id=1, source_target_pairs={{0,8},{1,9},{2,10},{3,11},{4,12},{5,13},{6,14},{7,15},{8,0},{9,1},... | collective-permute-start | bytes 1572872 | tf_op jit(solution)/shard_map/ppermute | solution.py:110
  57.6 3.4 %wave1_1.1 = (f32[1,16,4,16,128]{4,3,2,1,0:T(8,128)S(1)}, f32[16,10,16,128]{3,2,1,0:T(8,128)S(1)}) custom-call(f32[16,10,128]{2,1,0:T(8,128)S(1)} %fusion.4.refs_3_.refs_0_.refs_6_, f32[2,16]{1,0:T(2,128)S(1)} %add_convert_fusion.refs_4_.refs_1_.refs_7_, s32[1]{0:T(128)} %bitcast.11.refs_5_.refs_2_.refs_8_, ...), custom_call_target="tpu_custom_call" | custom-call | flops 49152000 | bytes 2621440 | tf_op jit(solution)/shard_map/wave1_1/pallas_call | solution.py:357
  61.6 3.0 %collective-permute-start.10 = (f32[1,16,4,16,128]{4,3,2,1,0:T(8,128)S(1)}, f32[1,16,4,16,128]{4,3,2,1,0:T(8,128)S(1)}, u32[]{:S(2)}, u32[]{:S(2)}) collective-permute-start(f32[1,16,4,16,128]{4,3,2,1,0:T(8,128)S(1)} %get-tuple-element.58.refs_1_), channel_id=1, source_target_pairs={{0,8},{1,9},{2,10},{3,11},{4,12},{5,13},{6,14},{7,15},{8,0},{9,1},... | collective-permute-start | bytes 1572872 | tf_op jit(solution)/shard_map/ppermute | solution.py:110
  64.6 6.1 %wave2_0.1 = (f32[1,16,4,16,128]{4,3,2,1,0:T(8,128)S(1)}, f32[16,10,16,128]{3,2,1,0:T(8,128)S(1)}, f32[16,10,16,128]{3,2,1,0:T(8,128)S(1)}) custom-call(f32[1,16,4,16,128]{4,3,2,1,0:T(8,128)S(1)} %collective-permute-done.4.refs_0_, f32[1,16,4,16,128]{4,3,2,1,0:T(8,128)S(1)} %get-tuple-element.46.refs_1_, ...), custom_call_target="tpu_custom_call" | custom-call | flops 49152000 | bytes 2621440 | tf_op jit(solution)/shard_map/wave2_0/pallas_call | solution.py:357
  71.5 3.0 %collective-permute-start.6 = (f32[1,16,4,16,128]{4,3,2,1,0:T(8,128)S(1)}, f32[1,16,4,16,128]{4,3,2,1,0:T(8,128)S(1)}, u32[]{:S(2)}, u32[]{:S(2)}) collective-permute-start(f32[1,16,4,16,128]{4,3,2,1,0:T(8,128)S(1)} %get-tuple-element.48.refs_1_), channel_id=1, source_target_pairs={{0,8},{1,9},{2,10},{3,11},{4,12},{5,13},{6,14},{7,15},{8,0},{9,1},... | collective-permute-start | bytes 1572872 | tf_op jit(solution)/shard_map/ppermute | solution.py:110
  74.4 6.3 %wave2_1.1 = (f32[1,16,4,16,128]{4,3,2,1,0:T(8,128)S(1)}, f32[16,10,16,128]{3,2,1,0:T(8,128)S(1)}, f32[16,10,16,128]{3,2,1,0:T(8,128)S(1)}) custom-call(f32[1,16,4,16,128]{4,3,2,1,0:T(8,128)S(1)} %collective-permute-done.10.refs_0_, f32[1,16,4,16,128]{4,3,2,1,0:T(8,128)S(1)} %get-tuple-element.58.refs_1_, ...), custom_call_target="tpu_custom_call" | custom-call | flops 49152000 | bytes 2621440 | tf_op jit(solution)/shard_map/wave2_1/pallas_call | solution.py:357
  80.7 0.7 collective-permute-start.13
  81.4 2.7 %collective-permute-start.12 = (f32[1,16,4,16,128]{4,3,2,1,0:T(8,128)S(1)}, f32[1,16,4,16,128]{4,3,2,1,0:T(8,128)S(1)}, u32[]{:S(2)}, u32[]{:S(2)}) collective-permute-start(f32[1,16,4,16,128]{4,3,2,1,0:T(8,128)S(1)} %get-tuple-element.61.refs_1_), channel_id=1, source_target_pairs={{0,8},{1,9},{2,10},{3,11},{4,12},{5,13},{6,14},{7,15},{8,0},{9,1},... | collective-permute-start | bytes 1572872 | tf_op jit(solution)/shard_map/ppermute | solution.py:110
  84.1 3.4 %wave2_2.1 = (f32[1,16,4,16,128]{4,3,2,1,0:T(8,128)S(1)}, f32[16,10,16,128]{3,2,1,0:T(8,128)S(1)}) custom-call(f32[16,10,128]{2,1,0:T(8,128)S(1)} %fusion.4.refs_3_.refs_0_.refs_6_, f32[2,16]{1,0:T(2,128)S(1)} %add_convert_fusion.refs_4_.refs_1_.refs_7_, s32[1]{0:T(128)} %bitcast.11.refs_5_.refs_2_.refs_8_, ...), custom_call_target="tpu_custom_call" | custom-call | flops 49152000 | bytes 2621440 | tf_op jit(solution)/shard_map/wave2_2/pallas_call | solution.py:357
  88.2 3.0 %collective-permute-start.18 = (f32[1,16,4,16,128]{4,3,2,1,0:T(8,128)S(1)}, f32[1,16,4,16,128]{4,3,2,1,0:T(8,128)S(1)}, u32[]{:S(2)}, u32[]{:S(2)}) collective-permute-start(f32[1,16,4,16,128]{4,3,2,1,0:T(8,128)S(1)} %get-tuple-element.69.refs_1_), channel_id=1, source_target_pairs={{0,8},{1,9},{2,10},{3,11},{4,12},{5,13},{6,14},{7,15},{8,0},{9,1},... | collective-permute-start | bytes 1572872 | tf_op jit(solution)/shard_map/ppermute | solution.py:110
  91.2 6.1 %wave3_0.1 = (f32[1,16,4,16,128]{4,3,2,1,0:T(8,128)S(1)}, f32[16,10,16,128]{3,2,1,0:T(8,128)S(1)}, f32[16,10,16,128]{3,2,1,0:T(8,128)S(1)}) custom-call(f32[1,16,4,16,128]{4,3,2,1,0:T(8,128)S(1)} %collective-permute-done.6.refs_0_, f32[1,16,4,16,128]{4,3,2,1,0:T(8,128)S(1)} %get-tuple-element.48.refs_1_, ...), custom_call_target="tpu_custom_call" | custom-call | flops 49152000 | bytes 2621440 | tf_op jit(solution)/shard_map/wave3_0/pallas_call | solution.py:357
  98.1 1.5 collective-permute-start.8
  99.5 6.3 %wave3_1.1 = (f32[1,16,4,16,128]{4,3,2,1,0:T(8,128)S(1)}, f32[16,10,16,128]{3,2,1,0:T(8,128)S(1)}, f32[16,10,16,128]{3,2,1,0:T(8,128)S(1)}) custom-call(f32[1,16,4,16,128]{4,3,2,1,0:T(8,128)S(1)} %collective-permute-done.12.refs_0_, f32[1,16,4,16,128]{4,3,2,1,0:T(8,128)S(1)} %get-tuple-element.61.refs_1_, ...), custom_call_target="tpu_custom_call" | custom-call | flops 49152000 | bytes 2621440 | tf_op jit(solution)/shard_map/wave3_1/pallas_call | solution.py:357
  105.8 0.9 collective-permute-start.15
  106.7 2.9 %collective-permute-start.14 = (f32[1,16,4,16,128]{4,3,2,1,0:T(8,128)S(1)}, f32[1,16,4,16,128]{4,3,2,1,0:T(8,128)S(1)}, u32[]{:S(2)}, u32[]{:S(2)}) collective-permute-start(f32[1,16,4,16,128]{4,3,2,1,0:T(8,128)S(1)} %get-tuple-element.64.refs_4_), channel_id=1, source_target_pairs={{0,8},{1,9},{2,10},{3,11},{4,12},{5,13},{6,14},{7,15},{8,0},{9,1},... | collective-permute-start | bytes 1572872 | tf_op jit(solution)/shard_map/ppermute | solution.py:110
  109.6 6.3 %wave3_2.1 = (f32[1,16,4,16,128]{4,3,2,1,0:T(8,128)S(1)}, f32[16,10,16,128]{3,2,1,0:T(8,128)S(1)}, f32[16,10,16,128]{3,2,1,0:T(8,128)S(1)}) custom-call(f32[1,16,4,16,128]{4,3,2,1,0:T(8,128)S(1)} %collective-permute-done.18.refs_0_, f32[1,16,4,16,128]{4,3,2,1,0:T(8,128)S(1)} %get-tuple-element.69.refs_1_, ...), custom_call_target="tpu_custom_call" | custom-call | flops 49152000 | bytes 2621440 | tf_op jit(solution)/shard_map/wave3_2/pallas_call | solution.py:357
  116.6 1.8 collective-permute-start.20
  118.4 3.3 %wave3_3.1.refs_1_ = f32[1,16,4,16,128]{4,3,2,1,0:T(8,128)S(1)} custom-call(f32[16,10,128]{2,1,0:T(8,128)S(1)} %fusion.4.refs_3_.refs_0_.refs_6_, f32[2,16]{1,0:T(2,128)S(1)} %add_convert_fusion.refs_4_.refs_1_.refs_7_, s32[1]{0:T(128)} %bitcast.11.refs_5_.refs_2_.refs_8_, f32[16,128]{1,0:T(8,128)S(1)} %broadcast_in_dim.39.refs_6_.refs_3_.refs_9_, ...), custom_call_target="tpu_custom_call" | custom-call | flops 49152000 | bytes 2621440 | tf_op jit(solution)/shard_map/wave3_3/pallas_call | solution.py:357
  122.4 3.0 %collective-permute-start.24 = (f32[1,16,4,16,128]{4,3,2,1,0:T(8,128)S(1)}, f32[1,16,4,16,128]{4,3,2,1,0:T(8,128)S(1)}, u32[]{:S(2)}, u32[]{:S(2)}) collective-permute-start(f32[1,16,4,16,128]{4,3,2,1,0:T(8,128)S(1)} %wave3_3.1.refs_1_), channel_id=1, source_target_pairs={{0,8},{1,9},{2,10},{3,11},{4,12},{5,13},{6,14},{7,15},{8,0},{9,1},... | collective-permute-start | bytes 1572872 | tf_op jit(solution)/shard_map/ppermute | solution.py:110
  125.4 8.9 %wave4_0.1 = (f32[1,16,4,16,128]{4,3,2,1,0:T(8,128)S(1)}, f32[16,10,16,128]{3,2,1,0:T(8,128)S(1)}, f32[16,10,16,128]{3,2,1,0:T(8,128)S(1)}) custom-call(f32[1,16,4,16,128]{4,3,2,1,0:T(8,128)S(1)} %collective-permute-done.8.refs_0_, f32[1,16,4,16,128]{4,3,2,1,0:T(8,128)S(1)} %get-tuple-element.50.refs_1_, ...), custom_call_target="tpu_custom_call" | custom-call | flops 98304000 | bytes 5242880 | tf_op jit(solution)/shard_map/wave4_0/pallas_call | solution.py:357
  134.4 6.3 %wave4_2.1 = (f32[1,16,4,16,128]{4,3,2,1,0:T(8,128)S(1)}, f32[16,10,16,128]{3,2,1,0:T(8,128)S(1)}, f32[16,10,16,128]{3,2,1,0:T(8,128)S(1)}) custom-call(f32[1,16,4,16,128]{4,3,2,1,0:T(8,128)S(1)} %collective-permute-done.20.refs_0_, f32[1,16,4,16,128]{4,3,2,1,0:T(8,128)S(1)} %get-tuple-element.72.refs_1_, ...), custom_call_target="tpu_custom_call" | custom-call | flops 49152000 | bytes 2621440 | tf_op jit(solution)/shard_map/wave4_2/pallas_call | solution.py:357
  141.3 1.8 collective-permute-start.22
  143.9 3.0 %collective-permute-start.16 = (f32[1,16,4,16,128]{4,3,2,1,0:T(8,128)S(1)}, f32[1,16,4,16,128]{4,3,2,1,0:T(8,128)S(1)}, u32[]{:S(2)}, u32[]{:S(2)}) collective-permute-start(f32[1,16,4,16,128]{4,3,2,1,0:T(8,128)S(1)} %get-tuple-element.67.refs_1_), channel_id=1, source_target_pairs={{0,8},{1,9},{2,10},{3,11},{4,12},{5,13},{6,14},{7,15},{8,0},{9,1},... | collective-permute-start | bytes 1572872 | tf_op jit(solution)/shard_map/ppermute | solution.py:110
  146.9 5.8 %wave4_3.1.refs_1_ = f32[1,16,4,16,128]{4,3,2,1,0:T(8,128)S(1)} custom-call(f32[1,16,4,16,128]{4,3,2,1,0:T(8,128)S(1)} %collective-permute-done.24.refs_0_, f32[1,16,4,16,128]{4,3,2,1,0:T(8,128)S(1)} %wave3_3.1.refs_1_, f32[1,16,4,16,128]{4,3,2,1,0:T(8,128)S(1)} %collective-permute-done.25.refs_2_, f32[16,10,128]{2,1,0:T(8,128)S(1)} %fusion.4.refs_3_.refs_0_.refs_6_, ...), custom_call_target="tpu_custom_call" | custom-call | flops 49152000 | bytes 2621440 | tf_op jit(solution)/shard_map/wave4_3/pallas_call | solution.py:357
  153.4 1.5 collective-permute-start.26
  154.8 8.9 %wave5_1.1 = (f32[1,16,4,16,128]{4,3,2,1,0:T(8,128)S(1)}, f32[16,10,16,128]{3,2,1,0:T(8,128)S(1)}, f32[16,10,16,128]{3,2,1,0:T(8,128)S(1)}) custom-call(f32[1,16,4,16,128]{4,3,2,1,0:T(8,128)S(1)} %collective-permute-done.16.refs_0_, f32[1,16,4,16,128]{4,3,2,1,0:T(8,128)S(1)} %get-tuple-element.67.refs_1_, ...), custom_call_target="tpu_custom_call" | custom-call | flops 98304000 | bytes 5242880 | tf_op jit(solution)/shard_map/wave5_1/pallas_call | solution.py:357
  163.8 1.5 collective-permute-start.31
  165.2 3.0 %collective-permute-start.30 = (f32[1,16,4,16,128]{4,3,2,1,0:T(8,128)S(1)}, f32[1,16,4,16,128]{4,3,2,1,0:T(8,128)}, u32[]{:S(2)}, u32[]{:S(2)}) collective-permute-start(f32[1,16,4,16,128]{4,3,2,1,0:T(8,128)S(1)} %get-tuple-element.78.refs_1_), channel_id=1, source_target_pairs={{0,8},{1,9},{2,10},{3,11},{4,12},{5,13},{6,14},{7,15},{8,0},{9,1},... | collective-permute-start | bytes 1572872 | tf_op jit(solution)/shard_map/ppermute | solution.py:110
  168.2 5.8 %wave5_3.1.refs_1_ = f32[1,16,4,16,128]{4,3,2,1,0:T(8,128)S(1)} custom-call(f32[1,16,4,16,128]{4,3,2,1,0:T(8,128)S(1)} %collective-permute-done.26.refs_0_, f32[1,16,4,16,128]{4,3,2,1,0:T(8,128)S(1)} %wave4_3.1.refs_1_, f32[1,16,4,16,128]{4,3,2,1,0:T(8,128)S(1)} %collective-permute-done.27.refs_2_, f32[16,10,128]{2,1,0:T(8,128)S(1)} %fusion.4.refs_3_.refs_0_.refs_6_, ...), custom_call_target="tpu_custom_call" | custom-call | flops 49152000 | bytes 2621440 | tf_op jit(solution)/shard_map/wave5_3/pallas_call | solution.py:357
  174.7 3.0 %collective-permute-start.28 = (f32[1,16,4,16,128]{4,3,2,1,0:T(8,128)S(1)}, f32[1,16,4,16,128]{4,3,2,1,0:T(8,128)}, u32[]{:S(2)}, u32[]{:S(2)}) collective-permute-start(f32[1,16,4,16,128]{4,3,2,1,0:T(8,128)S(1)} %wave5_3.1.refs_1_), channel_id=1, source_target_pairs={{0,8},{1,9},{2,10},{3,11},{4,12},{5,13},{6,14},{7,15},{8,0},{9,1},... | collective-permute-start | bytes 1572872 | tf_op jit(solution)/shard_map/ppermute | solution.py:110
  177.7 1.3 copy-done.1
  179.0 4.3 %wave6_2.1.refs_9_ = f32[16,10,16,128]{3,2,1,0:T(8,128)S(1)} custom-call(f32[1,16,4,16,128]{4,3,2,1,0:T(8,128)} %collective-permute-done.30.refs_0_, f32[1,16,4,16,128]{4,3,2,1,0:T(8,128)S(1)} %get-tuple-element.78.refs_1_, f32[1,16,4,16,128]{4,3,2,1,0:T(8,128)} %collective-permute-done.31.refs_2_, f32[16,10,128]{2,1,0:T(8,128)S(1)} %fusion.4.refs_3_.refs_0_.refs_6_, ...), custom_call_target="tpu_custom_call" | custom-call | flops 49152000 | bytes 2621440 | tf_op jit(solution)/shard_map/wave6_2/pallas_call | solution.py:357
  183.3 6.3 %wave6_3.1 = f32[1,16,4,16,128]{4,3,2,1,0:T(8,128)S(1)} custom-call(f32[1,16,4,16,128]{4,3,2,1,0:T(8,128)} %collective-permute-done.28.refs_0_, f32[1,16,4,16,128]{4,3,2,1,0:T(8,128)S(1)} %wave5_3.1.refs_1_, f32[1,16,4,16,128]{4,3,2,1,0:T(8,128)S(1)} %collective-permute-done.29.refs_2_, f32[16,10,128]{2,1,0:T(8,128)S(1)} %fusion.4.refs_3_.refs_0_.refs_6_, ...), custom_call_target="tpu_custom_call" | custom-call | flops 49152000 | bytes 2621440 | tf_op jit(solution)/shard_map/wave6_3/pallas_call | solution.py:357
  189.9 1.3 collective-permute-start.32
  191.2 1.2 collective-permute-done.32
  192.5 1.0 copy.11
  (84 shorter events, 11.3 us)
Async XLA Ops:
  0.0 4.5 %copy-start.5 = (f32[16]{0:T(128)S(1)}, f32[16]{0:T(128)}, u32[]{:S(2)}) copy-start(f32[16]{0:T(128)} %param.9) | copy-start | bytes 196
  0.0 4.5 %copy-start.3 = (f32[16,16]{1,0:T(8,128)S(1)}, f32[16,16]{1,0:T(8,128)}, u32[]{:S(2)}) copy-start(f32[16,16]{1,0:T(8,128)} %param.11) | copy-start | bytes 3076
  0.0 4.6 %copy-start.4 = (f32[16,16]{1,0:T(8,128)S(1)}, f32[16,16]{1,0:T(8,128)}, u32[]{:S(2)}) copy-start(f32[16,16]{1,0:T(8,128)} %param.10) | copy-start | bytes 3076
  3.0 14.7 %collective-permute-start = (f32[1088,128]{1,0:T(8,128)}, f32[1088,128]{1,0:T(8,128)}, u32[]{:S(2)}, u32[]{:S(2)}) collective-permute-start(f32[1088,128]{1,0:T(8,128)} %pad_maximum_fusion.1), channel_id=1, source_target_pairs={{0,4},{4,0},{1,5},{5,1},{2,6},{6,2},{3,7},{7,3},{8,12},{12,8},{9,1... | collective-permute-start | bytes 1671176 | tf_op jit(solution)/shard_map/ppermute | solution.py:85
  5.8 12.6 %copy-start.2 = (f32[8,8,128]{2,1,0:T(8,128)S(1)}, f32[8,8,128]{2,1,0:T(8,128)}, u32[]{:S(2)}) copy-start(f32[8,8,128]{2,1,0:T(8,128)} %param.7) | copy-start | bytes 98308
  19.8 0.9 copy-start.6
  19.8 0.8 collective-permute-start.1
  27.3 13.7 %collective-permute-start.3 = (f32[1,16,4,16,128]{4,3,2,1,0:T(8,128)S(1)}, f32[1,16,4,16,128]{4,3,2,1,0:T(8,128)S(1)}, u32[]{:S(2)}, u32[]{:S(2)}) collective-permute-start(f32[1,16,4,16,128]{4,3,2,1,0:T(8,128)S(1)} %get-tuple-element.44.refs_1_), channel_id=1, source_target_pairs={{1,8},{2,9},{3,10},{5,12},{6,13},{7,14},{8,1},{9,2},{10,3},{12,5},... | collective-permute-start | bytes 1572872 | tf_op jit(solution)/shard_map/ppermute | solution.py:110
  28.0 14.5 %collective-permute-start.2 = (f32[1,16,4,16,128]{4,3,2,1,0:T(8,128)S(1)}, f32[1,16,4,16,128]{4,3,2,1,0:T(8,128)S(1)}, u32[]{:S(2)}, u32[]{:S(2)}) collective-permute-start(f32[1,16,4,16,128]{4,3,2,1,0:T(8,128)S(1)} %get-tuple-element.44.refs_1_), channel_id=1, source_target_pairs={{0,8},{1,9},{2,10},{3,11},{4,12},{5,13},{6,14},{7,15},{8,0},{9,1},... | collective-permute-start | bytes 1572872 | tf_op jit(solution)/shard_map/ppermute | solution.py:110
  48.6 16.0 %collective-permute-start.5 = (f32[1,16,4,16,128]{4,3,2,1,0:T(8,128)S(1)}, f32[1,16,4,16,128]{4,3,2,1,0:T(8,128)S(1)}, u32[]{:S(2)}, u32[]{:S(2)}) collective-permute-start(f32[1,16,4,16,128]{4,3,2,1,0:T(8,128)S(1)} %get-tuple-element.46.refs_1_), channel_id=1, source_target_pairs={{1,8},{2,9},{3,10},{5,12},{6,13},{7,14},{8,1},{9,2},{10,3},{12,5},... | collective-permute-start | bytes 1572872 | tf_op jit(solution)/shard_map/ppermute | solution.py:110
  49.3 15.3 %collective-permute-start.4 = (f32[1,16,4,16,128]{4,3,2,1,0:T(8,128)S(1)}, f32[1,16,4,16,128]{4,3,2,1,0:T(8,128)S(1)}, u32[]{:S(2)}, u32[]{:S(2)}) collective-permute-start(f32[1,16,4,16,128]{4,3,2,1,0:T(8,128)S(1)} %get-tuple-element.46.refs_1_), channel_id=1, source_target_pairs={{0,8},{1,9},{2,10},{3,11},{4,12},{5,13},{6,14},{7,15},{8,0},{9,1},... | collective-permute-start | bytes 1572872 | tf_op jit(solution)/shard_map/ppermute | solution.py:110
  60.9 13.5 %collective-permute-start.11 = (f32[1,16,4,16,128]{4,3,2,1,0:T(8,128)S(1)}, f32[1,16,4,16,128]{4,3,2,1,0:T(8,128)S(1)}, u32[]{:S(2)}, u32[]{:S(2)}) collective-permute-start(f32[1,16,4,16,128]{4,3,2,1,0:T(8,128)S(1)} %get-tuple-element.58.refs_1_), channel_id=1, source_target_pairs={{1,8},{2,9},{3,10},{5,12},{6,13},{7,14},{8,1},{9,2},{10,3},{12,5},... | collective-permute-start | bytes 1572872 | tf_op jit(solution)/shard_map/ppermute | solution.py:110
  61.6 12.8 %collective-permute-start.10 = (f32[1,16,4,16,128]{4,3,2,1,0:T(8,128)S(1)}, f32[1,16,4,16,128]{4,3,2,1,0:T(8,128)S(1)}, u32[]{:S(2)}, u32[]{:S(2)}) collective-permute-start(f32[1,16,4,16,128]{4,3,2,1,0:T(8,128)S(1)} %get-tuple-element.58.refs_1_), channel_id=1, source_target_pairs={{0,8},{1,9},{2,10},{3,11},{4,12},{5,13},{6,14},{7,15},{8,0},{9,1},... | collective-permute-start | bytes 1572872 | tf_op jit(solution)/shard_map/ppermute | solution.py:110
  70.8 17.5 %collective-permute-start.7 = (f32[1,16,4,16,128]{4,3,2,1,0:T(8,128)S(1)}, f32[1,16,4,16,128]{4,3,2,1,0:T(8,128)S(1)}, u32[]{:S(2)}, u32[]{:S(2)}) collective-permute-start(f32[1,16,4,16,128]{4,3,2,1,0:T(8,128)S(1)} %get-tuple-element.48.refs_1_), channel_id=1, source_target_pairs={{1,8},{2,9},{3,10},{5,12},{6,13},{7,14},{8,1},{9,2},{10,3},{12,5},... | collective-permute-start | bytes 1572872 | tf_op jit(solution)/shard_map/ppermute | solution.py:110
  71.5 19.8 %collective-permute-start.6 = (f32[1,16,4,16,128]{4,3,2,1,0:T(8,128)S(1)}, f32[1,16,4,16,128]{4,3,2,1,0:T(8,128)S(1)}, u32[]{:S(2)}, u32[]{:S(2)}) collective-permute-start(f32[1,16,4,16,128]{4,3,2,1,0:T(8,128)S(1)} %get-tuple-element.48.refs_1_), channel_id=1, source_target_pairs={{0,8},{1,9},{2,10},{3,11},{4,12},{5,13},{6,14},{7,15},{8,0},{9,1},... | collective-permute-start | bytes 1572872 | tf_op jit(solution)/shard_map/ppermute | solution.py:110
  80.7 17.4 %collective-permute-start.13 = (f32[1,16,4,16,128]{4,3,2,1,0:T(8,128)S(1)}, f32[1,16,4,16,128]{4,3,2,1,0:T(8,128)S(1)}, u32[]{:S(2)}, u32[]{:S(2)}) collective-permute-start(f32[1,16,4,16,128]{4,3,2,1,0:T(8,128)S(1)} %get-tuple-element.61.refs_1_), channel_id=1, source_target_pairs={{1,8},{2,9},{3,10},{5,12},{6,13},{7,14},{8,1},{9,2},{10,3},{12,5},... | collective-permute-start | bytes 1572872 | tf_op jit(solution)/shard_map/ppermute | solution.py:110
  81.4 18.1 %collective-permute-start.12 = (f32[1,16,4,16,128]{4,3,2,1,0:T(8,128)S(1)}, f32[1,16,4,16,128]{4,3,2,1,0:T(8,128)S(1)}, u32[]{:S(2)}, u32[]{:S(2)}) collective-permute-start(f32[1,16,4,16,128]{4,3,2,1,0:T(8,128)S(1)} %get-tuple-element.61.refs_1_), channel_id=1, source_target_pairs={{0,8},{1,9},{2,10},{3,11},{4,12},{5,13},{6,14},{7,15},{8,0},{9,1},... | collective-permute-start | bytes 1572872 | tf_op jit(solution)/shard_map/ppermute | solution.py:110
  87.5 19.2 %collective-permute-start.19 = (f32[1,16,4,16,128]{4,3,2,1,0:T(8,128)S(1)}, f32[1,16,4,16,128]{4,3,2,1,0:T(8,128)S(1)}, u32[]{:S(2)}, u32[]{:S(2)}) collective-permute-start(f32[1,16,4,16,128]{4,3,2,1,0:T(8,128)S(1)} %get-tuple-element.69.refs_1_), channel_id=1, source_target_pairs={{1,8},{2,9},{3,10},{5,12},{6,13},{7,14},{8,1},{9,2},{10,3},{12,5},... | collective-permute-start | bytes 1572872 | tf_op jit(solution)/shard_map/ppermute | solution.py:110
  88.2 21.4 %collective-permute-start.18 = (f32[1,16,4,16,128]{4,3,2,1,0:T(8,128)S(1)}, f32[1,16,4,16,128]{4,3,2,1,0:T(8,128)S(1)}, u32[]{:S(2)}, u32[]{:S(2)}) collective-permute-start(f32[1,16,4,16,128]{4,3,2,1,0:T(8,128)S(1)} %get-tuple-element.69.refs_1_), channel_id=1, source_target_pairs={{0,8},{1,9},{2,10},{3,11},{4,12},{5,13},{6,14},{7,15},{8,0},{9,1},... | collective-permute-start | bytes 1572872 | tf_op jit(solution)/shard_map/ppermute | solution.py:110
  97.4 19.2 %collective-permute-start.9 = (f32[1,16,4,16,128]{4,3,2,1,0:T(8,128)S(1)}, f32[1,16,4,16,128]{4,3,2,1,0:T(8,128)S(1)}, u32[]{:S(2)}, u32[]{:S(2)}) collective-permute-start(f32[1,16,4,16,128]{4,3,2,1,0:T(8,128)S(1)} %get-tuple-element.50.refs_1_), channel_id=1, source_target_pairs={{1,8},{2,9},{3,10},{5,12},{6,13},{7,14},{8,1},{9,2},{10,3},{12,5},... | collective-permute-start | bytes 1572872 | tf_op jit(solution)/shard_map/ppermute | solution.py:110
  98.1 23.7 %collective-permute-start.8 = (f32[1,16,4,16,128]{4,3,2,1,0:T(8,128)S(1)}, f32[1,16,4,16,128]{4,3,2,1,0:T(8,128)S(1)}, u32[]{:S(2)}, u32[]{:S(2)}) collective-permute-start(f32[1,16,4,16,128]{4,3,2,1,0:T(8,128)S(1)} %get-tuple-element.50.refs_1_), channel_id=1, source_target_pairs={{0,8},{1,9},{2,10},{3,11},{4,12},{5,13},{6,14},{7,15},{8,0},{9,1},... | collective-permute-start | bytes 1572872 | tf_op jit(solution)/shard_map/ppermute | solution.py:110
  105.8 16.6 %collective-permute-start.15 = (f32[1,16,4,16,128]{4,3,2,1,0:T(8,128)S(1)}, f32[1,16,4,16,128]{4,3,2,1,0:T(8,128)S(1)}, u32[]{:S(2)}, u32[]{:S(2)}) collective-permute-start(f32[1,16,4,16,128]{4,3,2,1,0:T(8,128)S(1)} %get-tuple-element.64.refs_4_), channel_id=1, source_target_pairs={{1,8},{2,9},{3,10},{5,12},{6,13},{7,14},{8,1},{9,2},{10,3},{12,5},... | collective-permute-start | bytes 1572872 | tf_op jit(solution)/shard_map/ppermute | solution.py:110
  106.7 18.7 %collective-permute-start.14 = (f32[1,16,4,16,128]{4,3,2,1,0:T(8,128)S(1)}, f32[1,16,4,16,128]{4,3,2,1,0:T(8,128)S(1)}, u32[]{:S(2)}, u32[]{:S(2)}) collective-permute-start(f32[1,16,4,16,128]{4,3,2,1,0:T(8,128)S(1)} %get-tuple-element.64.refs_4_), channel_id=1, source_target_pairs={{0,8},{1,9},{2,10},{3,11},{4,12},{5,13},{6,14},{7,15},{8,0},{9,1},... | collective-permute-start | bytes 1572872 | tf_op jit(solution)/shard_map/ppermute | solution.py:110
  115.9 18.5 %collective-permute-start.21 = (f32[1,16,4,16,128]{4,3,2,1,0:T(8,128)S(1)}, f32[1,16,4,16,128]{4,3,2,1,0:T(8,128)S(1)}, u32[]{:S(2)}, u32[]{:S(2)}) collective-permute-start(f32[1,16,4,16,128]{4,3,2,1,0:T(8,128)S(1)} %get-tuple-element.72.refs_1_), channel_id=1, source_target_pairs={{1,8},{2,9},{3,10},{5,12},{6,13},{7,14},{8,1},{9,2},{10,3},{12,5},... | collective-permute-start | bytes 1572872 | tf_op jit(solution)/shard_map/ppermute | solution.py:110
  116.6 17.8 %collective-permute-start.20 = (f32[1,16,4,16,128]{4,3,2,1,0:T(8,128)S(1)}, f32[1,16,4,16,128]{4,3,2,1,0:T(8,128)S(1)}, u32[]{:S(2)}, u32[]{:S(2)}) collective-permute-start(f32[1,16,4,16,128]{4,3,2,1,0:T(8,128)S(1)} %get-tuple-element.72.refs_1_), channel_id=1, source_target_pairs={{0,8},{1,9},{2,10},{3,11},{4,12},{5,13},{6,14},{7,15},{8,0},{9,1},... | collective-permute-start | bytes 1572872 | tf_op jit(solution)/shard_map/ppermute | solution.py:110
  121.7 22.1 %collective-permute-start.25 = (f32[1,16,4,16,128]{4,3,2,1,0:T(8,128)S(1)}, f32[1,16,4,16,128]{4,3,2,1,0:T(8,128)S(1)}, u32[]{:S(2)}, u32[]{:S(2)}) collective-permute-start(f32[1,16,4,16,128]{4,3,2,1,0:T(8,128)S(1)} %wave3_3.1.refs_1_), channel_id=1, source_target_pairs={{1,8},{2,9},{3,10},{5,12},{6,13},{7,14},{8,1},{9,2},{10,3},{12,5},... | collective-permute-start | bytes 1572872 | tf_op jit(solution)/shard_map/ppermute | solution.py:110
  122.4 24.4 %collective-permute-start.24 = (f32[1,16,4,16,128]{4,3,2,1,0:T(8,128)S(1)}, f32[1,16,4,16,128]{4,3,2,1,0:T(8,128)S(1)}, u32[]{:S(2)}, u32[]{:S(2)}) collective-permute-start(f32[1,16,4,16,128]{4,3,2,1,0:T(8,128)S(1)} %wave3_3.1.refs_1_), channel_id=1, source_target_pairs={{0,8},{1,9},{2,10},{3,11},{4,12},{5,13},{6,14},{7,15},{8,0},{9,1},... | collective-permute-start | bytes 1572872 | tf_op jit(solution)/shard_map/ppermute | solution.py:110
  140.6 12.7 %collective-permute-start.23 = (f32[1,16,4,16,128]{4,3,2,1,0:T(8,128)S(1)}, f32[1,16,4,16,128]{4,3,2,1,0:T(8,128)S(1)}, u32[]{:S(2)}, u32[]{:S(2)}) collective-permute-start(f32[1,16,4,16,128]{4,3,2,1,0:T(8,128)S(1)} %get-tuple-element.75.refs_4_), channel_id=1, source_target_pairs={{1,8},{2,9},{3,10},{5,12},{6,13},{7,14},{8,1},{9,2},{10,3},{12,5},... | collective-permute-start | bytes 1572872 | tf_op jit(solution)/shard_map/ppermute | solution.py:110
  141.3 13.5 %collective-permute-start.22 = (f32[1,16,4,16,128]{4,3,2,1,0:T(8,128)S(1)}, f32[1,16,4,16,128]{4,3,2,1,0:T(8,128)S(1)}, u32[]{:S(2)}, u32[]{:S(2)}) collective-permute-start(f32[1,16,4,16,128]{4,3,2,1,0:T(8,128)S(1)} %get-tuple-element.75.refs_4_), channel_id=1, source_target_pairs={{0,8},{1,9},{2,10},{3,11},{4,12},{5,13},{6,14},{7,15},{8,0},{9,1},... | collective-permute-start | bytes 1572872 | tf_op jit(solution)/shard_map/ppermute | solution.py:110
  143.2 11.7 %collective-permute-start.17 = (f32[1,16,4,16,128]{4,3,2,1,0:T(8,128)S(1)}, f32[1,16,4,16,128]{4,3,2,1,0:T(8,128)S(1)}, u32[]{:S(2)}, u32[]{:S(2)}) collective-permute-start(f32[1,16,4,16,128]{4,3,2,1,0:T(8,128)S(1)} %get-tuple-element.67.refs_1_), channel_id=1, source_target_pairs={{1,8},{2,9},{3,10},{5,12},{6,13},{7,14},{8,1},{9,2},{10,3},{12,5},... | collective-permute-start | bytes 1572872 | tf_op jit(solution)/shard_map/ppermute | solution.py:110
  143.9 11.0 %collective-permute-start.16 = (f32[1,16,4,16,128]{4,3,2,1,0:T(8,128)S(1)}, f32[1,16,4,16,128]{4,3,2,1,0:T(8,128)S(1)}, u32[]{:S(2)}, u32[]{:S(2)}) collective-permute-start(f32[1,16,4,16,128]{4,3,2,1,0:T(8,128)S(1)} %get-tuple-element.67.refs_1_), channel_id=1, source_target_pairs={{0,8},{1,9},{2,10},{3,11},{4,12},{5,13},{6,14},{7,15},{8,0},{9,1},... | collective-permute-start | bytes 1572872 | tf_op jit(solution)/shard_map/ppermute | solution.py:110
  152.6 15.6 %collective-permute-start.27 = (f32[1,16,4,16,128]{4,3,2,1,0:T(8,128)S(1)}, f32[1,16,4,16,128]{4,3,2,1,0:T(8,128)S(1)}, u32[]{:S(2)}, u32[]{:S(2)}) collective-permute-start(f32[1,16,4,16,128]{4,3,2,1,0:T(8,128)S(1)} %wave4_3.1.refs_1_), channel_id=1, source_target_pairs={{1,8},{2,9},{3,10},{5,12},{6,13},{7,14},{8,1},{9,2},{10,3},{12,5},... | collective-permute-start | bytes 1572872 | tf_op jit(solution)/shard_map/ppermute | solution.py:110
  153.4 14.8 %collective-permute-start.26 = (f32[1,16,4,16,128]{4,3,2,1,0:T(8,128)S(1)}, f32[1,16,4,16,128]{4,3,2,1,0:T(8,128)S(1)}, u32[]{:S(2)}, u32[]{:S(2)}) collective-permute-start(f32[1,16,4,16,128]{4,3,2,1,0:T(8,128)S(1)} %wave4_3.1.refs_1_), channel_id=1, source_target_pairs={{0,8},{1,9},{2,10},{3,11},{4,12},{5,13},{6,14},{7,15},{8,0},{9,1},... | collective-permute-start | bytes 1572872 | tf_op jit(solution)/shard_map/ppermute | solution.py:110
  163.8 10.2 %copy-start = (f32[16,10,16,128]{3,2,1,0:T(8,128)}, f32[16,10,16,128]{3,2,1,0:T(8,128)S(1)}, u32[]{:S(2)}) copy-start(f32[16,10,16,128]{3,2,1,0:T(8,128)S(1)} %get-tuple-element.82.refs_9_) | copy-start | bytes 3932164
  163.8 13.9 %collective-permute-start.31 = (f32[1,16,4,16,128]{4,3,2,1,0:T(8,128)S(1)}, f32[1,16,4,16,128]{4,3,2,1,0:T(8,128)}, u32[]{:S(2)}, u32[]{:S(2)}) collective-permute-start(f32[1,16,4,16,128]{4,3,2,1,0:T(8,128)S(1)} %get-tuple-element.78.refs_1_), channel_id=1, source_target_pairs={{1,8},{2,9},{3,10},{5,12},{6,13},{7,14},{8,1},{9,2},{10,3},{12,5},... | collective-permute-start | bytes 1572872 | tf_op jit(solution)/shard_map/ppermute | solution.py:110
  165.2 12.5 %collective-permute-start.30 = (f32[1,16,4,16,128]{4,3,2,1,0:T(8,128)S(1)}, f32[1,16,4,16,128]{4,3,2,1,0:T(8,128)}, u32[]{:S(2)}, u32[]{:S(2)}) collective-permute-start(f32[1,16,4,16,128]{4,3,2,1,0:T(8,128)S(1)} %get-tuple-element.78.refs_1_), channel_id=1, source_target_pairs={{0,8},{1,9},{2,10},{3,11},{4,12},{5,13},{6,14},{7,15},{8,0},{9,1},... | collective-permute-start | bytes 1572872 | tf_op jit(solution)/shard_map/ppermute | solution.py:110
  174.0 9.3 %collective-permute-start.29 = (f32[1,16,4,16,128]{4,3,2,1,0:T(8,128)S(1)}, f32[1,16,4,16,128]{4,3,2,1,0:T(8,128)S(1)}, u32[]{:S(2)}, u32[]{:S(2)}) collective-permute-start(f32[1,16,4,16,128]{4,3,2,1,0:T(8,128)S(1)} %wave5_3.1.refs_1_), channel_id=1, source_target_pairs={{1,8},{2,9},{3,10},{5,12},{6,13},{7,14},{8,1},{9,2},{10,3},{12,5},... | collective-permute-start | bytes 1572872 | tf_op jit(solution)/shard_map/ppermute | solution.py:110
  174.7 8.6 %collective-permute-start.28 = (f32[1,16,4,16,128]{4,3,2,1,0:T(8,128)S(1)}, f32[1,16,4,16,128]{4,3,2,1,0:T(8,128)}, u32[]{:S(2)}, u32[]{:S(2)}) collective-permute-start(f32[1,16,4,16,128]{4,3,2,1,0:T(8,128)S(1)} %wave5_3.1.refs_1_), channel_id=1, source_target_pairs={{0,8},{1,9},{2,10},{3,11},{4,12},{5,13},{6,14},{7,15},{8,0},{9,1},... | collective-permute-start | bytes 1572872 | tf_op jit(solution)/shard_map/ppermute | solution.py:110
  177.7 1.3 copy-start.1
  189.9 2.4 %collective-permute-start.32 = (f32[8,4,16,128]{3,2,1,0:T(8,128)S(1)}, f32[8,4,16,128]{3,2,1,0:T(8,128)S(1)}, u32[]{:S(2)}, u32[]{:S(2)}) collective-permute-start(f32[8,4,16,128]{3,2,1,0:T(8,128)S(1)} %get-tuple-element.83), channel_id=1, source_target_pairs={{0,8},{8,0},{16,24},{24,16},{1,9},{9,1},{17,25},{25,17},{2,10},{10... | collective-permute-start | bytes 786440 | tf_op jit(solution)/shard_map/ppermute | solution.py:411
